TPU v7x, 32 devices: a whole 2x2x4 slice. The times are simulated.
32 devices in a mesh: grp: 2 (over x), seq: 8 (over z, y), tp: 2 (over core).
Axes of the slice: x: 2, y: 2, z: 4, core: 2. Of those that a mesh axis runs over, the one named last changes fastest.
Arguments:
- x_in: bfloat16 [4096, 8192], P(('grp', 'seq'), 'tp'), parts along dimension 0, may hold values from -6 to 6
- z_in: bfloat16 [4096, 8192], P(('grp', 'seq'), 'tp'), parts along dimension 0, may hold values from -6 to 6
- bc_in: bfloat16 [2, 4096, 1024], P(None, ('grp', 'seq'), 'tp'), parts along dimension 1, may hold values from -6 to 6
- dt_raw: float32 [4096, 128], P(('grp', 'seq'), 'tp'), parts along dimension 0, may hold values from -4 to 24
- conv_x: bfloat16 [4, 8192], P(None, 'tp'), may hold values from -3 to 3
- conv_bc: bfloat16 [2, 4, 1024], P(None, None, 'tp'), may hold values from -3 to 3
- a_log: float32 [128], P('tp'), may hold values from -6 to 4
- dt_bias: float32 [128], P('tp'), may hold values from -7.4 to -6.4
- d_skip: float32 [128], P('tp'), may hold values from 0.5 to 2
- gain: float32 [8192], P('tp'), may hold values from 0.1 to 1.9
- sign_bits: int32 [8192], P('tp'), may hold values from 0 to 1
- out_weight: bfloat16 [8192, 2048], P('tp', 'seq'), may hold values from -0.0625 to 0.0625
Outputs:
- out: bfloat16 [4096, 2048], P(('grp', 'seq'), 'tp'), parts along dimension 0
There are 2 independent parts, one for each index of `grp`. A program takes and returns all parts, laid end to end along the dimension named above; an argument that names none is the same for every part. Nothing has to cross between parts.
All inputs are finite; a program needn't handle non-finite values.
Results may differ from a plain program's by a relative error of at most 0.013.
Values may be sent and summed in bfloat16 or wider, within the bound.
No kernel may reach another device: no remote copies, remote signals or barrier semaphores. Data moves between devices by JAX's collectives and lax.ppermute only.
A program may use at most 320 MiB of HBM per device.

v0:
```python
import math

import jax
import jax.numpy as jnp
from jax import lax
from jax.sharding import PartitionSpec as P

HEADDIM = 64
STATE = 128
BLOCK = 256
INNER = 8192


def from_behind(block, axis, distance):
    devices = range(lax.axis_size(axis))
    route = [(i - distance, i) for i in devices if i - distance in devices]
    return lax.ppermute(block, axis, route)


def carried_in(array, axis, combine, identity):
    size, here = (lax.axis_size(axis), lax.axis_index(axis))
    everything = jax.tree.map(
        lambda part, kind: lax.all_gather(part.astype(kind), axis),
        array,
        jax.tree.map(lambda a: jnp.bfloat16 if a.dtype == jnp.float32 else a.dtype, array),
    )
    start = jax.tree.map(
        lambda part, zero: jnp.broadcast_to(jnp.asarray(zero, part.dtype), part.shape),
        array,
        identity,
    )

    def hop(k, before):
        reached = k < here
        new = combine(
            before, jax.tree.map(lambda part, own: part[k].astype(own.dtype), everything, array)
        )
        return jax.tree.map(lambda a, b: jnp.where(reached, a, b), new, before)

    return lax.fori_loop(0, size, hop, start)


def sylvester(extent):
    index = jnp.arange(extent, dtype=jnp.int32)
    shared = jnp.bitwise_and(index[:, None], index[None, :])
    parity = jnp.zeros((extent, extent), jnp.int32)
    for position in range(extent.bit_length() - 1):
        parity = parity + jnp.bitwise_and(jnp.right_shift(shared, position), 1)
    return (1 - 2 * jnp.bitwise_and(parity, 1)).astype(jnp.float32)


def local_wht(values):
    row_count, breadth = values.shape
    minor_size = min(breadth, 128)
    major_size = breadth // minor_size
    shaped = values.reshape(row_count, major_size, minor_size)
    shaped = jnp.einsum(
        "rab,bd->rad", shaped, sylvester(minor_size), precision=lax.Precision.HIGHEST
    )
    shaped = jnp.einsum(
        "rab,ac->rcb", shaped, sylvester(major_size), precision=lax.Precision.HIGHEST
    )
    return shaped.reshape(row_count, breadth)


def conv_silu(padded, kernel_rows, length_out):
    summed = jnp.zeros(padded.shape[:-2] + (length_out, padded.shape[-1]), jnp.float32)
    for offset in range(len(kernel_rows)):
        summed = summed + padded[..., offset : offset + length_out, :].astype(
            jnp.float32
        ) * kernel_rows[offset].astype(jnp.float32)
    return jax.nn.silu(summed).astype(jnp.bfloat16)


def group_terms(x_grp, b_grp, c_grp, cum_grp, dt_grp):
    scores = jnp.einsum("ktn,ksn->kts", c_grp, b_grp, preferred_element_type=jnp.float32)
    extent = cum_grp.shape[1]
    cum_heads = jnp.swapaxes(cum_grp, 1, 2)
    dt_heads = jnp.swapaxes(dt_grp, 1, 2)
    causal = (jnp.arange(extent)[:, None] >= jnp.arange(extent)[None, :])[None, None, :, :]
    exponent = jnp.where(causal, cum_heads[:, :, :, None] - cum_heads[:, :, None, :], 0.0)
    weights = jnp.where(
        causal, scores[:, None, :, :] * jnp.exp(exponent) * dt_heads[:, :, None, :], 0.0
    ).astype(jnp.bfloat16)
    within = jnp.einsum("kjts,ksjp->ktjp", weights, x_grp, preferred_element_type=jnp.float32)
    to_end = jnp.exp(cum_grp[:, -1:, :] - cum_grp) * dt_grp
    loaded = (b_grp[:, :, None, :].astype(jnp.float32) * to_end[..., None]).astype(jnp.bfloat16)
    states = jnp.einsum("ksjn,ksjp->kjpn", loaded, x_grp, preferred_element_type=jnp.float32)
    return (within, states)


def combine(earlier, latter):
    return (earlier[0] * latter[0], earlier[1] * latter[0][:, None, None] + latter[1])


def per_device(
    x_in, z_in, bc_in, dt_raw, conv_x, conv_bc, a_log, dt_bias, d_skip, gain, sign_bits, out_weight
):
    row_count, channels = x_in.shape
    kernel = conv_x.shape[0]
    heads_here = a_log.shape[0]
    groups_here = bc_in.shape[2] // STATE
    per_group = heads_here // groups_here
    blocks = row_count // BLOCK
    x_rim, bc_rim = from_behind(
        (x_in[row_count - kernel + 1 :], bc_in[:, row_count - kernel + 1 :]), "seq", 1
    )
    x_conv = conv_silu(
        jnp.concatenate([x_rim, x_in], axis=0),
        [conv_x[offset] for offset in range(kernel)],
        row_count,
    )
    bc_conv = conv_silu(
        jnp.concatenate([bc_rim, bc_in], axis=1),
        [conv_bc[:, offset][:, None, :] for offset in range(kernel)],
        row_count,
    )
    dt_step = jax.nn.softplus(dt_raw + dt_bias)
    log_decay = dt_step * -jnp.exp(a_log)
    cumulative = jnp.cumsum(log_decay.reshape(blocks, BLOCK, heads_here), axis=1)
    x_blocks = x_conv.reshape(blocks, BLOCK, groups_here, per_group, HEADDIM)
    b_blocks = bc_conv[0].reshape(blocks, BLOCK, groups_here, STATE)
    c_blocks = bc_conv[1].reshape(blocks, BLOCK, groups_here, STATE)
    cum_g = cumulative.reshape(blocks, BLOCK, groups_here, per_group)
    dt_g = dt_step.reshape(blocks, BLOCK, groups_here, per_group)
    within, states = lax.map(
        lambda packed: group_terms(*packed),
        (
            jnp.moveaxis(x_blocks, 2, 0),
            jnp.moveaxis(b_blocks, 2, 0),
            jnp.moveaxis(c_blocks, 2, 0),
            jnp.moveaxis(cum_g, 2, 0),
            jnp.moveaxis(dt_g, 2, 0),
        ),
    )
    within = jnp.moveaxis(within, 0, 2).reshape(blocks, BLOCK, heads_here, HEADDIM)
    states = jnp.moveaxis(states, 0, 1).reshape(blocks, heads_here, HEADDIM, STATE)
    end_decay = jnp.exp(cumulative[:, -1, :])

    def advance(running, element):
        decay_here, state_here = element
        return (
            (running[0] * decay_here, running[1] * decay_here[:, None, None] + state_here),
            running,
        )

    identity = (
        jnp.ones((heads_here,), jnp.float32),
        jnp.zeros((heads_here, HEADDIM, STATE), jnp.float32),
    )
    device_total, prefixes = lax.scan(advance, identity, (end_decay, states))
    arrived_decay, arrived_state = carried_in(device_total, "seq", combine, identity)
    incoming = prefixes[0][:, :, None, None] * arrived_state[None] + prefixes[1]
    carried = jnp.einsum(
        "kcgn,kgjpn->kcgjp",
        c_blocks.astype(jnp.float32),
        incoming.reshape(blocks, groups_here, per_group, HEADDIM, STATE),
        precision=lax.Precision.HIGHEST,
    )
    carried = carried.reshape(blocks, BLOCK, heads_here, HEADDIM) * jnp.exp(cumulative)[..., None]
    skipped = d_skip[:, None] * x_conv.reshape(blocks, BLOCK, heads_here, HEADDIM).astype(
        jnp.float32
    )
    y_full = (within + carried + skipped).reshape(row_count, channels)
    gated = y_full * jax.nn.silu(z_in.astype(jnp.float32))
    grouped = gated.reshape(row_count, groups_here, channels // groups_here)
    mean_sq = jnp.mean(grouped * grouped, axis=-1, keepdims=True)
    normed = ((grouped * lax.rsqrt(mean_sq + 1e-05)).reshape(row_count, channels) * gain).astype(
        jnp.bfloat16
    )
    signed = normed * (1 - 2 * sign_bits).astype(jnp.bfloat16)
    norm_scale = 1.0 / math.sqrt(INNER)
    gathered = lax.all_to_all(signed, "tp", split_axis=0, concat_axis=1, tiled=True)
    half_rows = gathered.shape[0]
    first_half = gathered[:, :channels].astype(jnp.float32)
    second_half = gathered[:, channels:].astype(jnp.float32)
    stacked = jnp.concatenate([first_half + second_half, first_half - second_half], axis=0)
    transformed = local_wht(stacked) * norm_scale
    whole_rot = jnp.concatenate([transformed[:half_rows], transformed[half_rows:]], axis=1).astype(
        jnp.bfloat16
    )
    rotated = lax.all_to_all(whole_rot, "tp", split_axis=1, concat_axis=0, tiled=True)
    partial_out = jnp.dot(
        rotated,
        lax.all_gather(out_weight, "seq", axis=1, tiled=True),
        preferred_element_type=jnp.float32,
    )
    return lax.psum_scatter(partial_out.astype(jnp.bfloat16), "tp", scatter_dimension=1, tiled=True)


def solution(mesh):
    in_specs = (
        P(("grp", "seq"), "tp"),
        P(("grp", "seq"), "tp"),
        P(None, ("grp", "seq"), "tp"),
        P(("grp", "seq"), "tp"),
        P(None, "tp"),
        P(None, None, "tp"),
        P("tp"),
        P("tp"),
        P("tp"),
        P("tp"),
        P("tp"),
        P("tp", "seq"),
    )
    out_specs = P(("grp", "seq"), "tp")
    return jax.shard_map(
        per_device, mesh=mesh, in_specs=in_specs, out_specs=out_specs, check_vma=False
    )
```

profile of v0, /device:TPU:28, one launch (start us, length us, event | category | flops | bytes accessed | tf_op | source)
XLA Modules:
  0.0 449.4 jit_solution(14694288354521563225)
XLA Ops:
  21.4 3.3 copy.76
  24.7 2.1 multiply_convert_fusion.4
  28.9 7.7 %multiply_convert_fusion.3 = bf16[256,4096]{0,1:T(8,128)(2,1)} fusion(bf16[256,4096]{0,1:T(8,128)(2,1)S(1)} %copy.76, bf16[3,4096]{0,1:T(8,128)(2,1)S(1)} %copy.75, f32[4096]{0:T(1024)} %bitcast.214, f32[4096]{0:T(1024)} %bitcast.215, f32[4096]{0:T(1024)} %bitcast.213, f32[4096]{0:T(1024)S(1)} %bitcast.212), kind=kLoop, calls=%fused_computation.55 | loop fusion | flops 26214400 | bytes 4284416 | tf_op jit(solution)/shard_map/convert_element_type | solution.py:72
  36.6 30.7 %while.8 = (s32[]{:T(128)}, f32[4,1,256,16,64]{2,4,3,1,0:T(8,128)}, f32[4,1,16,64,128]{4,3,2,1,0:T(8,128)}, bf16[4,1,256,16,64]{2,4,3,1,0:T(8,128)(2,1)}, bf16[4...) while((s32[]{:T(128)}, ...), condition=%wide.region_3.4_spmd, body=%wide.region_2.3_spmd.sunk | while | flops 225550336 | bytes 4197677 | solution.py:126
  37.7 3.5 fusion.140
  41.7 2.6 fusion.141
  45.4 3.5 fusion.140
  49.3 2.6 fusion.141
  53.1 3.5 fusion.140
  57.0 2.7 fusion.141
  60.8 3.5 fusion.140
  64.7 2.7 fusion.141
  67.3 2.9 add_convert_fusion
  71.3 18.9 %all-gather = bf16[8,1,64]{2,1,0:T(2,128)(2,1)S(1)} all-gather(bf16[1,1,64]{2,1,0:T(2,128)(2,1)S(1)} %copy.88), channel_id=2, replica_groups=mesh['grp'=2,'seq'=8,'tp'=2] {'seq'}, dimensions={0}, use_global_device_ids=true | all-gather | bytes 1152 | tf_op jit(solution)/shard_map/all_gather | solution.py:23
  90.2 4.1 copy.90
  94.4 101.8 %all-gather.4.cloned.1.call-done = bf16[8,64,64,128]{3,2,1,0:T(8,128)(2,1)} async-done(((bf16[1,64,64,128]{3,2,1,0:T(8,128)(2,1)}), bf16[8,64,64,128]{3,2,1,0:T(8,128)(2,1)}) %all-gather.4.cloned.1.call-update) | async-done | bytes 8388624 | tf_op jit(solution)/shard_map/all_gather | solution.py:23
  196.2 14.8 %while.34 = (s32[]{:T(128)}, f32[64,64,128]{2,1,0:T(8,128)S(1)}, s32[]{:T(128)}, bf16[8,64]{1,0:T(8,128)(2,1)S(1)}, bf16[8,64,64,128]{3,2,1,0:T(8,128)(2,1)}, /*index=5*/s32[]{:T(128)}, s32[]{:T(128)}) while((s32[]{:T(128)}, f32[64,64,128]{2,1,0:T(8,128)S(1)}, s32[]{:T(128)}, bf16[8,64]{1,0:T(8,128)(2,1)S(1)}, ...), condition=%wide.region_5.6_spmd.clone, body=%wide.region_4.5_spmd.clone.sunk | while | flops 2621508 | bytes 5243625 | solution.py:40
  196.2 1.8 fusion.142
  198.0 1.8 fusion.142
  207.1 2.0 fusion.142
  209.1 1.9 fusion.142
  211.0 1.8 fusion.119
  213.4 3.8 bitcast_reduce_fusion
  218.7 5.4 %all_to_all.35 = bf16[2,128,4096]{1,2,0:T(8,128)(2,1)S(1)} all-to-all(bf16[2,128,4096]{1,2,0:T(8,128)(2,1)S(1)} %copy_bitcast_fusion), channel_id=1, replica_groups=mesh['grp'=2,'seq'=8,'tp'=2] {'tp'}, dimensions={0} | all-to-all | bytes 4194304 | tf_op jit(solution)/shard_map/all_to_all | solution.py:173
  224.4 2.2 pad_maximum_fusion
  226.6 5.5 %copy.96 = f32[256,32,128]{2,1,0:T(8,128)} copy(f32[256,32,128]{0,2,1:T(8,128)} %bitcast.197) | data formatting | bytes 8388608 | tf_op jit(solution)/shard_map/reshape | solution.py:56
  232.0 6.6 %fusion.40 = f32[256,32,128]{2,1,0:T(8,128)S(1)} fusion(f32[256,32,128]{2,1,0:T(8,128)} %copy.96), kind=kOutput, calls=%fused_computation.83 | convolution fusion | flops 1611022336 | bytes 8388608 | tf_op jit(solution)/shard_map/rab,bd->rad/dot_general | solution.py:57
  238.7 3.9 fusion.37
  244.2 5.4 %all_to_all.36 = bf16[128,2,4096]{2,0,1:T(8,128)(2,1)S(1)} all-to-all(bf16[128,2,4096]{2,0,1:T(8,128)(2,1)S(1)} %pad_maximum_fusion.2), channel_id=1, replica_groups=mesh['grp'=2,'seq'=8,'tp'=2] {'tp'}, dimensions={1} | all-to-all | bytes 4194304 | tf_op jit(solution)/shard_map/all_to_all | solution.py:182
  249.6 174.2 %all-gather.6.cloned.1.call-done = bf16[4096,2048]{1,0:T(8,128)(2,1)} async-done(((bf16[4096,256]{1,0:T(8,128)(2,1)}), bf16[4096,2048]{1,0:T(8,128)(2,1)}) %all-gather.6.cloned.1.call-update) | async-done | bytes 16777232 | tf_op jit(solution)/shard_map/all_gather | solution.py:185
  423.8 9.2 %convolution_convert_fusion = bf16[256,2048]{1,0:T(8,128)(2,1)} fusion(bf16[256,4096]{1,0:T(8,128)(2,1)S(1)} %bitcast.205, bf16[4096,2048]{1,0:T(8,128)(2,1)} %all-gather.6.cloned.1.call-done), kind=kOutput, calls=%fused_computation.62 | convolution fusion | flops 4295491584 | bytes 19922944 | tf_op jit(solution)/shard_map/dot_general | solution.py:183
  433.0 9.8 %reduce-scatter.2.cloned.1.call-done = bf16[256,1024]{1,0:T(8,128)(2,1)} async-done(((bf16[256,2048]{1,0:T(8,128)(2,1)}), bf16[256,1024]{1,0:T(8,128)(2,1)}) %reduce-scatter.2.cloned.1.call-update) | async-done | bytes 524304 | tf_op jit(solution)/shard_map/reduce_scatter | solution.py:188
  (119 shorter events, 34.9 us)
Async XLA Ops:
  6.5 189.7 %all-gather.4.cloned.1.call-start = ((), (), s32[]{:S(2)}) async-start(), calls=%async_computation.3 | async-start | bytes 9437184 | tf_op jit(solution)/shard_map/all_gather | solution.py:23
  7.5 17.2 %collective-permute-start.1 = (bf16[2,3,512]{1,2,0:T(8,128)(2,1)S(1)}, bf16[2,3,512]{1,2,0:T(8,128)(2,1)S(1)}, u32[]{:S(2)}, u32[]{:S(2)}) collective-permute-start(bf16[2,3,512]{1,2,0:T(8,128)(2,1)S(1)} %copy.79), channel_id=1, source_target_pairs={{0,2},{2,4},{4,6},{6,8},{8,10},{10,12},{12,14},{1,3},{3,5},{5,7},{... | collective-permute-start | bytes 18440 | tf_op jit(solution)/shard_map/ppermute | solution.py:17
  10.2 17.4 %collective-permute-start = (bf16[3,4096]{1,0:T(4,128)(2,1)}, bf16[3,4096]{1,0:T(4,128)(2,1)}, u32[]{:S(2)}, u32[]{:S(2)}) collective-permute-start(bf16[3,4096]{1,0:T(4,128)(2,1)} %slice.82), channel_id=1, source_target_pairs={{0,2},{2,4},{4,6},{6,8},{8,10},{10,12},{12,14},{1,3},{3,5},{5,7},{... | collective-permute-start | bytes 73736 | tf_op jit(solution)/shard_map/ppermute | solution.py:17
  18.6 6.1 %copy-start.3 = (f32[1,256,64]{1,0,2:T(1,128)}, f32[1,256,64]{1,0,2:T(1,128)S(1)}, u32[]{:S(2)}) copy-start(f32[1,256,64]{1,0,2:T(1,128)S(1)} %get-tuple-element.250) | copy-start | bytes 196612
  36.6 30.8 %copy-start.8 = (f32[64]{0:T(128)S(1)}, f32[64]{0:T(128)}, u32[]{:S(2)}) copy-start(f32[64]{0:T(128)} %multiply_reduce_fusion) | copy-start | bytes 772
  67.3 3.7 copy-start.4
  67.3 22.8 %copy-start.5 = (f32[1,256,64]{1,0,2:T(1,128)S(1)}, f32[1,256,64]{1,0,2:T(1,128)}, u32[]{:S(2)}) copy-start(f32[1,256,64]{1,0,2:T(1,128)} %get-tuple-element.249) | copy-start | bytes 196612
  70.2 24.1 %copy-start.9 = (f32[64]{0:T(128)S(1)}, f32[64]{0:T(128)}, u32[]{:S(2)}) copy-start(f32[64]{0:T(128)} %param.24) | copy-start | bytes 772
  70.2 24.2 %copy-start.7 = (s32[4096]{0:T(1024)S(1)}, s32[4096]{0:T(1024)}, u32[]{:S(2)}) copy-start(s32[4096]{0:T(1024)} %param.26) | copy-start | bytes 49156
  70.2 353.6 %all-gather.6.cloned.1.call-start = ((), (), s32[]{:S(2)}) async-start(), calls=%async_computation.4 | async-start | bytes 18874368 | tf_op jit(solution)/shard_map/all_gather | solution.py:185
  71.0 371.9 %reduce-scatter.2.cloned.1.call-start = ((), (), s32[]{:S(2)}) async-start(), calls=%async_computation.5 | async-start | bytes 1572864 | tf_op jit(solution)/shard_map/reduce_scatter | solution.py:188
  196.2 14.8 %copy-start.2 = (bf16[4,1,256,128]{2,3,0,1:T(8,128)(2,1)S(1)}, bf16[4,1,256,128]{2,3,0,1:T(8,128)(2,1)}, u32[]{:S(2)}) copy-start(bf16[4,1,256,128]{2,3,0,1:T(8,128)(2,1)} %get-tuple-element.412) | copy-start | bytes 786436
  211.0 1.8 copy-start
  211.0 2.4 copy-start.1
  213.4 3.8 copy-start.6
Sparse Core Ops, SparseCore 0:
  70.3 125.7 all-gather.3
  198.2 225.5 all-gather.5
  433.2 9.6 reduce-scatter.1
where the time goes:
time: 453 us; the launch traced here: 449 us
  waiting for transfers between devices  286 us (63%)
  matrix products  50.3 us (11%)
  other arithmetic  42.6 us (9%)
  blocking collectives  29.7 us (7%)
  local copies, waits for them, and re-layouts  23.8 us (5%)
  between operations  13.4 us (3%)
    all_gather x1, waiting for transfers between devices, per_device(): lax.all_gather(out_weight, 'seq', axis=1, tiled=True)  174 us
    all_gather x1, waiting for transfers between devices, carried_in(): lax.all_gather(part.astype(kind), axis)  102 us
    all_gather x1, blocking collectives, carried_in(): lax.all_gather(part.astype(kind), axis)  18.9 us
    select_n x8, other arithmetic, hop(): return jax.tree.map(lambda a, b: jnp.where(reached, a, b), new, before)  14.5 us
    dot_general x4, matrix products, group_terms(): jnp.einsum('kjts,ksjp->ktjp', weights, x_grp, preferred_element_type=jnp....  14 us
    dot_general x4, matrix products, group_terms(): jnp.einsum('ksjn,ksjp->kjpn', loaded, x_grp, preferred_element_type=jnp.f...  10.6 us
    unnamed x28, local copies, waits for them, and re-layouts  10.4 us
    convert_element_type x2, other arithmetic, conv_silu(): return jax.nn.silu(summed).astype(jnp.bfloat16)  9.82 us
  transfers between devices with their start and end apart: 5, of which 3 were waited for; matrix products, arithmetic and copies ran while one was open for 14% of the time, Pallas kernels for 0%

commit v1 on v0

v1 whole, which is shorter than its diff:
```python
import math

import jax
import jax.numpy as jnp
from jax import lax
from jax.experimental import pallas as pl
from jax.experimental.pallas import tpu as pltpu
from jax.sharding import Mesh
from jax.sharding import PartitionSpec as P

HEADDIM = 64
STATE = 128
BLOCK = 256
INNER = 8192
GROUP = 1024
PER = 16
AXES = ("grp", "sz", "sy", "tp")
LOG2E = 1.4426950408889634
F32 = jnp.float32
BF16 = jnp.bfloat16
HIGH = lax.Precision.HIGHEST
VM = pl.BlockSpec(memory_space=pltpu.VMEM)


def send(array, route):
    sizes = [lax.axis_size(a) for a in AXES]
    pairs = []
    for x in range(sizes[0]):
        for z in range(sizes[1]):
            for y in range(sizes[2]):
                for t in range(sizes[3]):
                    to = route(x, z, y, t)
                    if to is None or not 0 <= to[1] < sizes[1]:
                        continue
                    source = ((x * sizes[1] + z) * sizes[2] + y) * sizes[3] + t
                    target = ((to[0] * sizes[1] + to[1]) * sizes[2] + to[2]) * sizes[3] + to[3]
                    pairs.append((source, target))
    return lax.ppermute(array, AXES, pairs)


def swap(array, k):
    return send(array, lambda x, z, y, t: (x ^ (k >> 1), z, y ^ (k & 1), t))


def onward(array, distance):
    return send(array, lambda x, z, y, t: (x, z + distance, y, t))


def expander():
    row = lax.broadcasted_iota(jnp.int32, (PER, GROUP), 0)
    lane = lax.broadcasted_iota(jnp.int32, (PER, GROUP), 1)
    return jnp.where(lane // HEADDIM == row, 1.0, 0.0).astype(F32)


def silu(v):
    return v * lax.logistic(v)


def pack_kernel(order, x0, x1, x2, x3, b0, b1, b2, b3, dt, o0, o1, o2, o3, d0, d1, d2, d3, turned):
    turned[...] = dt[...].T
    for k, (x, b, o, d) in enumerate(
        ((x0, b0, o0, d0), (x1, b1, o1, d1), (x2, b2, o2, d2), (x3, b3, o3, d3))
    ):
        o[:, :GROUP] = x[...]
        o[:, GROUP : GROUP + STATE] = b[0]
        o[:, GROUP + STATE :] = b[1]
        first = pl.multiple_of(order[k] * PER, PER)
        d[...] = turned[pl.ds(first, PER), :]


def pack(order, x_in, bc_in, dt_raw):
    rows = x_in.shape[0]
    wide = GROUP + 2 * STATE
    whole = lambda *shape: pl.BlockSpec(shape, lambda i, order: (0,) * len(shape))
    return pl.pallas_call(
        pack_kernel,
        grid_spec=pltpu.PrefetchScalarGridSpec(
            num_scalar_prefetch=1,
            grid=(1,),
            in_specs=[
                pl.BlockSpec((rows, GROUP), lambda i, order, k=k: (0, order[k])) for k in range(4)
            ]
            + [
                pl.BlockSpec((2, rows, STATE), lambda i, order, k=k: (0, 0, order[k]))
                for k in range(4)
            ]
            + [whole(rows, dt_raw.shape[1])],
            out_specs=[whole(rows, wide)] * 4 + [whole(PER, rows)] * 4,
            scratch_shapes=[pltpu.VMEM((dt_raw.shape[1], rows), F32)],
        ),
        out_shape=[jax.ShapeDtypeStruct((rows, wide), BF16)] * 4
        + [jax.ShapeDtypeStruct((PER, rows), F32)] * 4,
        name="pack",
    )(order, x_in, x_in, x_in, x_in, bc_in, bc_in, bc_in, bc_in, dt_raw)


def cut_kernel(order, z1, z2, z3, o1, o2, o3):
    o1[...] = z1[...]
    o2[...] = z2[...]
    o3[...] = z3[...]


def cut(order, z_in):
    rows = z_in.shape[0]
    return pl.pallas_call(
        cut_kernel,
        grid_spec=pltpu.PrefetchScalarGridSpec(
            num_scalar_prefetch=1,
            grid=(1,),
            in_specs=[
                pl.BlockSpec((rows, GROUP), lambda i, order, k=k: (0, order[k]))
                for k in range(1, 4)
            ],
            out_specs=[pl.BlockSpec((rows, GROUP), lambda i, order: (0, 0))] * 3,
        ),
        out_shape=[jax.ShapeDtypeStruct((rows, GROUP), BF16)] * 3,
        name="cut",
    )(order, z_in, z_in, z_in)


def turn_kernel(sign, w, out, mid):
    size = 256
    chunks = w.shape[0] // size
    half = chunks // 2
    row = lax.broadcasted_iota(jnp.int32, (size, size), 0)
    col = lax.broadcasted_iota(jnp.int32, (size, size), 1)
    shared = row & col
    parity = jnp.zeros((size, size), jnp.int32)
    for position in range(8):
        parity = parity ^ ((shared >> position) & 1)
    small = (1 - 2 * parity).astype(F32).astype(BF16)
    for j in range(chunks):
        mid[j] = jnp.dot(small, w[j * size : (j + 1) * size, :], preferred_element_type=F32)
    scale = 1.0 / math.sqrt(INNER)
    upper = jnp.where(sign[0] == 0, scale, -scale)

    def step(i, carry):
        at = pl.ds(pl.multiple_of(i * 16, 16), 16)
        values = [mid[j, at, :] * scale + mid[j + half, at, :] * upper for j in range(half)]
        width = 1
        while width < half:
            fresh = list(values)
            for j in range(half):
                if j & width == 0:
                    fresh[j] = values[j] + values[j + width]
                    fresh[j + width] = values[j] - values[j + width]
            values = fresh
            width *= 2
        for j in range(half):
            out[j, at, :] = values[j].astype(BF16)
        return carry

    lax.fori_loop(0, size // 16, step, 0)


def turn(sign, weight):
    rows, cols = weight.shape
    return pl.pallas_call(
        turn_kernel,
        in_specs=[pl.BlockSpec(memory_space=pltpu.SMEM), VM],
        out_specs=VM,
        out_shape=jax.ShapeDtypeStruct((rows // 512, 256, cols), BF16),
        scratch_shapes=[pltpu.VMEM((rows // 256, 256, cols), F32)],
        name="turn",
    )(sign, weight)


def conv_kernel(
    place, p0, p1, p2, p3, halo, cx, cbc, d0, d1, d2, d3, al, db,
    xc, bc, low, cum, pair, first, fade, states, decays,
):
    here = place[1]
    pieces = (p0, p1, p2, p3)
    steps = (d0, d1, d2, d3)
    rows = p0.shape[0]
    spread = expander()
    row = lax.broadcasted_iota(jnp.int32, (rows, rows), 0)
    col = lax.broadcasted_iota(jnp.int32, (rows, rows), 1)
    upto = jnp.where(row <= col, 1.0, 0.0).astype(F32)
    for k in range(4):
        piece, other = pieces[k], pieces[k ^ 1]
        opening = here == (k & 1)

        def conv(at, taps):
            outer = halo[k >> 1, :, at].astype(F32)
            inner = other[rows - 16 :, at].astype(F32)
            before = jnp.where(opening, outer, inner)[8:]
            padded = jnp.concatenate([before, piece[:, at].astype(F32)], axis=0)
            summed = padded[5 : 5 + rows] * taps[0:1]
            for tap in range(1, 4):
                summed = summed + padded[5 + tap : 5 + tap + rows] * taps[tap : tap + 1]
            return silu(summed).astype(BF16)

        def chunk(c, carry, conv=conv, k=k):
            at = pl.ds(pl.multiple_of(c * 128, 128), 128)
            xc[k, :, at] = conv(at, cx[:, at].astype(F32))
            return carry

        lax.fori_loop(0, GROUP // 128, chunk, 0)
        b = conv(slice(GROUP, GROUP + STATE), cbc[0].astype(F32))
        c = conv(slice(GROUP + STATE, GROUP + 2 * STATE), cbc[1].astype(F32))
        bc[k, :, :STATE] = b
        bc[k, :, STATE:] = c
        raw = steps[k][...] + db[...]
        dt = jnp.maximum(raw, 0.0) + jnp.log1p(jnp.exp(-jnp.abs(raw)))
        rate = -jnp.exp(al[...])
        total = jnp.dot(dt * rate, upto, precision=HIGH, preferred_element_type=F32)
        low[k] = (total - jnp.log(dt)) * LOG2E
        upright = total.T
        cum[k] = upright
        load = (jnp.exp(total[:, rows - 1 :] - total) * dt).T
        wide = jnp.dot(load, spread, precision=HIGH, preferred_element_type=F32)
        loaded = (xc[k].astype(F32) * wide).astype(BF16)
        states[k] = lax.dot_general(
            b, loaded, (((0,), (0,)), ((), ())), preferred_element_type=F32
        )
        end = jnp.broadcast_to(jnp.exp(upright[rows - 1 :, :]), (8, PER))
        decays[k] = jnp.dot(end, spread, precision=HIGH, preferred_element_type=F32)
    for r in range(2):
        early, late = 2 * r + here, 2 * r + 1 - here
        decay_early, decay_late = decays[early], decays[late]
        pair[r, :STATE, :] = (states[late] + decay_late[0:1] * states[early]).astype(BF16)
        pair[r, STATE:, :] = split(decay_early * decay_late)
        first[r] = states[early]
        fade[r] = decay_early


def split(decay):
    high = decay.astype(BF16).astype(F32)
    middle = (decay - high).astype(BF16).astype(F32)
    last = decay - high - middle
    both = jnp.concatenate([decay, decay], axis=0)
    row = lax.broadcasted_iota(jnp.int32, both.shape, 0)
    twice = lambda v: jnp.concatenate([v, v], axis=0)
    out = jnp.where(row == 0, twice(high), jnp.where(row == 1, twice(middle), twice(last)))
    return jnp.where(row < 3, out, 0.0).astype(BF16)


def joined(tail):
    tail = tail.astype(F32)
    return tail[0:1] + tail[1:2] + tail[2:3]


def conv_states(place, pieces, halo, conv_x, conv_bc, steps, a_log, dt_bias):
    rows = pieces[0].shape[0]
    whole = lambda *shape: pl.BlockSpec(shape, lambda i, place: (0,) * len(shape))
    shapes = [
        ((4, rows, GROUP), BF16),
        ((4, rows, 2 * STATE), BF16),
        ((4, PER, rows), F32),
        ((4, rows, PER), F32),
        ((2, STATE + 16, GROUP), BF16),
        ((2, STATE, GROUP), F32),
        ((2, 8, GROUP), F32),
    ]
    return pl.pallas_call(
        conv_kernel,
        grid_spec=pltpu.PrefetchScalarGridSpec(
            num_scalar_prefetch=1,
            grid=(1,),
            in_specs=[whole(rows, GROUP + 2 * STATE)] * 4
            + [
                whole(2, 16, GROUP + 2 * STATE),
                pl.BlockSpec((4, GROUP), lambda i, place: (0, place[0])),
                pl.BlockSpec((2, 4, STATE), lambda i, place: (0, 0, place[0])),
            ]
            + [whole(PER, rows)] * 4
            + [pl.BlockSpec((PER, 1), lambda i, place: (place[0], 0))] * 2,
            out_specs=[whole(*shape) for shape, _ in shapes],
            scratch_shapes=[
                pltpu.VMEM((4, STATE, GROUP), F32),
                pltpu.VMEM((4, 8, GROUP), F32),
            ],
        ),
        out_shape=[jax.ShapeDtypeStruct(shape, kind) for shape, kind in shapes],
        name="conv_states",
    )(place, *pieces, halo, conv_x, conv_bc, *steps, a_log, dt_bias)


def join_kernel(late, early, out):
    for r in range(2):
        decay = joined(late[r, STATE:, :])
        out[r, :STATE, :] = (
            late[r, :STATE, :].astype(F32) + decay * early[r, :STATE, :].astype(F32)
        ).astype(BF16)
        both = decay * joined(early[r, STATE:, :])
        out[r, STATE:, :] = split(jnp.broadcast_to(both, (8, GROUP)))


def join(late, early):
    return pl.pallas_call(
        join_kernel,
        in_specs=[VM, VM],
        out_specs=VM,
        out_shape=jax.ShapeDtypeStruct(late.shape, BF16),
        name="join",
    )(late, early)


def within_kernel(place, xc, bc, low, cum, skip, out):
    rows = xc.shape[1]
    half = rows // 2
    b = bc[0, :, :STATE]
    c = bc[0, :, STATE:]
    scores = lax.dot_general(c, b, (((1,), (1,)), ((), ())), preferred_element_type=F32)
    row = lax.broadcasted_iota(jnp.int32, (half, half), 0)
    col = lax.broadcasted_iota(jnp.int32, (half, half), 1)
    causal = row >= col
    corner = jnp.where(causal, scores[:half, :half], 0.0)
    square = scores[half:, :half]
    end = jnp.where(causal, scores[half:, half:], 0.0)
    lane = lax.broadcasted_iota(jnp.int32, (rows, 2 * HEADDIM), 1)
    upright = cum[0] * LOG2E
    for j in range(PER // 2):
        at = slice(j * 2 * HEADDIM, (j + 1) * 2 * HEADDIM)
        x = xc[0, :, at]
        top = bottom = None
        for side in range(2):
            h = 2 * j + side
            mine = jnp.where((lane < HEADDIM) == (side == 0), x, jnp.zeros_like(x))
            level = upright[:, h : h + 1]
            floor = low[0, h : h + 1, :]
            one = jnp.exp2(jnp.minimum(level[:half] - floor[:, :half], 64.0)) * corner
            two = jnp.exp2(level[half:] - floor[:, :half]) * square
            three = jnp.exp2(jnp.minimum(level[half:] - floor[:, half:], 64.0)) * end
            low_rows = jnp.concatenate([two.astype(BF16), three.astype(BF16)], axis=1)
            first = jnp.dot(one.astype(BF16), mine[:half], preferred_element_type=F32)
            last = jnp.dot(low_rows, mine, preferred_element_type=F32)
            top = first if top is None else top + first
            bottom = last if bottom is None else bottom + last
        skipped = x.astype(F32) * skip[:, at]
        out[0, :half, at] = top + skipped[:half]
        out[0, half:, at] = bottom + skipped[half:]


def within(place, xc, bc, low, cum, skip):
    rows = xc.shape[1]
    block = lambda *shape: pl.BlockSpec((1,) + shape, lambda k, place: (k, 0, 0))
    return pl.pallas_call(
        within_kernel,
        grid_spec=pltpu.PrefetchScalarGridSpec(
            num_scalar_prefetch=1,
            grid=(4,),
            in_specs=[
                block(rows, GROUP),
                block(rows, 2 * STATE),
                block(PER, rows),
                block(rows, PER),
                pl.BlockSpec((1, GROUP), lambda k, place: (0, place[0])),
            ],
            out_specs=block(rows, GROUP),
        ),
        out_shape=jax.ShapeDtypeStruct((4, rows, GROUP), F32),
        name="within",
    )(place, xc, bc, low, cum, skip)


def gate_kernel(
    place, y, bc, cum, near, far, first, fade, z0, z1, z2, z3, gain, bits, out, gate
):
    k = pl.program_id(0)
    for index, z in enumerate((z0, z1, z2, z3)):

        @pl.when(k == index)
        def _(z=z):
            gate[...] = silu(z[...].astype(F32))

    opening = place[1] == (k % 2)
    incoming = near[0, :STATE, :].astype(F32) + joined(near[0, STATE:, :]) * far[
        0, :STATE, :
    ].astype(F32)
    incoming = jnp.where(opening, incoming, fade[0, 0:1] * incoming + first[0])
    carried = jnp.dot(bc[0, :, STATE:], incoming.astype(BF16), preferred_element_type=F32)
    kept = jnp.dot(jnp.exp(cum[0]), expander(), precision=HIGH, preferred_element_type=F32)
    gated = (y[0] + kept * carried) * gate[...]
    scale = lax.rsqrt(jnp.mean(gated * gated, axis=1, keepdims=True) + 1e-05)
    signed = gain[...] * (1 - 2 * bits[...]).astype(F32)
    out[0] = (gated * scale * signed).astype(BF16)


def gate_norm(place, y, bc, cum, near, far, first, fade, z_in, zs, gain, bits):
    rows = y.shape[1]
    block = lambda *shape: pl.BlockSpec((1,) + shape, lambda k, place: (k, 0, 0))
    part = lambda *shape: pl.BlockSpec((1,) + shape, lambda k, place: (k // 2, 0, 0))
    mine = lambda rows: pl.BlockSpec((rows, GROUP), lambda k, place: (0, place[0]))
    return pl.pallas_call(
        gate_kernel,
        grid_spec=pltpu.PrefetchScalarGridSpec(
            num_scalar_prefetch=1,
            grid=(4,),
            in_specs=[
                block(rows, GROUP),
                block(rows, 2 * STATE),
                block(rows, PER),
                part(STATE + 16, GROUP),
                part(STATE + 16, GROUP),
                part(STATE, GROUP),
                part(8, GROUP),
                mine(rows),
            ]
            + [pl.BlockSpec((rows, GROUP), lambda k, place: (0, 0))] * 3
            + [mine(1), mine(1)],
            out_specs=block(rows, GROUP),
            scratch_shapes=[pltpu.VMEM((rows, GROUP), F32)],
        ),
        out_shape=jax.ShapeDtypeStruct((4, rows, GROUP), BF16),
        name="gate_norm",
    )(place, y, bc, cum, near, far, first, fade, z_in, *zs, gain, bits)


def per_device(
    x_in, z_in, bc_in, dt_raw, conv_x, conv_bc, a_log, dt_bias, d_skip, gain, sign_bits, out_weight
):
    rows = x_in.shape[0]
    x_here, y_here, t_here = (lax.axis_index(a) for a in ("grp", "sy", "tp"))
    length = lax.axis_size("sz")
    mine = 2 * x_here + y_here
    order = jnp.stack([mine ^ k for k in range(4)]).astype(jnp.int32)
    place = jnp.stack([mine, y_here]).astype(jnp.int32)

    packed = pack(order, x_in, bc_in, dt_raw)
    pieces = [packed[0]] + [swap(packed[k], k) for k in range(1, 4)]
    steps = [packed[4]] + [swap(packed[4 + k], k) for k in range(1, 4)]
    tails = [p[rows - 16 :] for p in pieces]
    closing = jnp.where(
        y_here == 1, jnp.stack([tails[0], tails[2]]), jnp.stack([tails[1], tails[3]])
    )
    halo = onward(closing, 1)

    turned = turn(x_here.reshape(1).astype(jnp.int32), out_weight)
    turned = turned.reshape(2, GROUP, out_weight.shape[1])
    across = send(turned, lambda x, z, y, t: (x, z, y, 1 - t))
    own = turned.astype(F32)
    rotated = (across.astype(F32) + jnp.where(t_here == 0, own, -own)).astype(BF16)
    kept = lax.dynamic_index_in_dim(rotated, y_here, 0, keepdims=False)
    given = swap(lax.dynamic_index_in_dim(rotated, 1 - y_here, 0, keepdims=False), 1)
    columns = jnp.where(
        y_here == 0,
        jnp.concatenate([kept, given], axis=1),
        jnp.concatenate([given, kept], axis=1),
    )
    weight = lax.all_gather(columns, "sz", axis=1, tiled=True)

    zs = [swap(z, k + 1) for k, z in enumerate(cut(order, z_in))]

    xc, bc, low, cum, pair, first, fade = conv_states(
        place, pieces, halo, conv_x, conv_bc, steps, a_log[:, None], dt_bias[:, None]
    )
    near = onward(pair, 1)
    y = within(place, xc, bc, low, cum, jnp.repeat(d_skip, HEADDIM)[None])
    span = join(pair, near)
    distance = 2
    far = onward(span, distance)
    while 2 * distance < length:
        near, span = join(near, far), join(span, far)
        distance *= 2
        far = onward(span, distance)
    act = gate_norm(
        place, y, bc, cum, near, far, first, fade, z_in, zs, gain[None], sign_bits[None]
    )

    act = act.reshape(4 * rows, GROUP)
    half = weight.shape[1] // 2
    theirs = lax.dynamic_slice_in_dim(weight, (1 - t_here) * half, half, 1)
    ours = lax.dynamic_slice_in_dim(weight, t_here * half, half, 1)
    away = jnp.dot(act, theirs, preferred_element_type=F32).astype(BF16)
    back = send(away, lambda x, z, y, t: (x, z, y, 1 - t))
    stay = jnp.dot(act, ours, preferred_element_type=F32) + back.astype(F32)
    stay = stay.reshape(4, rows, half)
    total = stay[0]
    for k in range(1, 4):
        total = total + swap(stay[k].astype(BF16), k).astype(F32)
    return total.astype(BF16)


def solution(mesh):
    shape = mesh.devices.shape
    fine = Mesh(mesh.devices.reshape(shape[0], shape[1] // 2, 2, shape[2]), AXES)
    seq = ("sz", "sy")
    rows = ("grp",) + seq
    in_specs = (
        P(rows, "tp"),
        P(rows, "tp"),
        P(None, rows, "tp"),
        P(rows, "tp"),
        P(None, "tp"),
        P(None, None, "tp"),
        P("tp"),
        P("tp"),
        P("tp"),
        P("tp"),
        P("tp"),
        P("tp", seq),
    )
    return jax.shard_map(
        per_device, mesh=fine, in_specs=in_specs, out_specs=P(rows, "tp"), check_vma=False
    )
```

time: 453 us -> 225 us (0.50)
  the two profiles are of different devices: /device:TPU:28 before, /device:TPU:0 now
where the time goes in v1:
time: 225 us; the launch traced here: 224 us
  waiting for transfers between devices  107 us (48%)
  Pallas kernels  47.2 us (21%)
  starting transfers between devices  33.9 us (15%)
  between operations  13.6 us (6%)
  matrix products  10.7 us (5%)
  local copies, waits for them, and re-layouts  6.42 us (3%)
  other arithmetic  5.25 us (2%)
    ppermute x18, waiting for transfers between devices, send(): return lax.ppermute(array, AXES, pairs)  107 us
    ppermute x18, starting transfers between devices, send(): return lax.ppermute(array, AXES, pairs)  33.9 us
    pallas_call x1, Pallas kernels, conv_states(): pl.pallas_call(conv_kernel, grid_spec=pltpu.PrefetchScalarGridSpec(num_sc...  15.9 us
    pallas_call x1, Pallas kernels, gate_norm(): pl.pallas_call(gate_kernel, grid_spec=pltpu.PrefetchScalarGridSpec(num_sc...  10.1 us
    pallas_call x1, Pallas kernels, within(): pl.pallas_call(within_kernel, grid_spec=pltpu.PrefetchScalarGridSpec(num_...  7.58 us
    dot_general x1, matrix products, per_device(): away = jnp.dot(act, theirs, preferred_element_type=F32).astype(BF16)  6.11 us
    dot_general x1, matrix products, per_device(): stay = jnp.dot(act, ours, preferred_element_type=F32) + back.astype(F32)  4.55 us
  transfers between devices with their start and end apart: 19, of which 14 were waited for; matrix products, arithmetic and copies ran while one was open for 2% of the time, Pallas kernels for 19%

profile of v1, /device:TPU:0, one launch (start us, length us, event | category | flops | bytes accessed | tf_op | source)
XLA Modules:
  0.0 224.2 jit_solution(6863485381313470782)
XLA Ops:
  6.5 4.0 %turn.1 = bf16[8,256,256]{2,1,0:T(8,128)(2,1)} custom-call(s32[1]{0:T(128)} %bitcast.14.sign, bf16[4096,256]{1,0:T(8,128)(2,1)} %w.1), custom_call_target="tpu_custom_call" | custom-call | tf_op jit(solution)/shard_map/turn/pallas_call | solution.py:158
  11.0 2.5 %collective-permute-done.12 = bf16[2,1024,256]{2,1,0:T(8,128)(2,1)S(1)} collective-permute-done((bf16[2,1024,256]{2,1,0:T(8,128)(2,1)}, bf16[2,1024,256]{2,1,0:T(8,128)(2,1)S(1)}, u32[]{:S(2)}, u32[]{:S(2)}) %collective-permute-start.12) | collective-permute-done | bytes 1048608 | tf_op jit(solution)/shard_map/ppermute | solution.py:38
  13.5 1.6 fusion.1
  15.2 2.9 %collective-permute-start.13 = (bf16[1024,256]{1,0:T(8,128)(2,1)S(1)}, bf16[1024,256]{1,0:T(8,128)(2,1)S(1)}, u32[]{:S(2)}, u32[]{:S(2)}) collective-permute-start(bf16[1024,256]{1,0:T(8,128)(2,1)S(1)} %get-tuple-element.45), channel_id=1, source_target_pairs={{0,2},{1,3},{2,0},{3,1},{4,6},{5,7},{6,4},{7,5},{8,10},{9,11},{10,... | collective-permute-start | bytes 1572872 | tf_op jit(solution)/shard_map/ppermute | solution.py:38
  18.2 12.2 %collective-permute-done.13 = bf16[1024,256]{1,0:T(8,128)(2,1)S(1)} collective-permute-done((bf16[1024,256]{1,0:T(8,128)(2,1)S(1)}, bf16[1024,256]{1,0:T(8,128)(2,1)S(1)}, u32[]{:S(2)}, u32[]{:S(2)}) %collective-permute-start.13) | collective-permute-done | bytes 524320 | tf_op jit(solution)/shard_map/ppermute | solution.py:38
  33.0 4.1 %pack.1 = (bf16[256,1280]{1,0:T(8,128)(2,1)}, bf16[256,1280]{1,0:T(8,128)(2,1)}, bf16[256,1280]{1,0:T(8,128)(2,1)}, bf16[256,1280]{1,0:T(8,128)(2,1)}, f32[16,25...) custom-call(s32[4]{0:T(128)} %pad_add_fusion.1.order, bf16[256,4096]{1,0:T(8,128)(2,1)} %x3.1, ...), custom_call_target="tpu_custom_call" | custom-call | tf_op jit(solution)/shard_map/pack/pallas_call | solution.py:75
  37.1 2.7 %collective-permute-start.2 = (bf16[256,1280]{1,0:T(8,128)(2,1)}, bf16[256,1280]{1,0:T(8,128)(2,1)S(1)}, u32[]{:S(2)}, u32[]{:S(2)}) collective-permute-start(bf16[256,1280]{1,0:T(8,128)(2,1)} %get-tuple-element.26), channel_id=1, source_target_pairs={{0,18},{1,19},{2,16},{3,17},{4,22},{5,23},{6,20},{7,21},{8,26},{9,... | collective-permute-start | bytes 1966088 | tf_op jit(solution)/shard_map/ppermute | solution.py:38
  40.6 1.7 collective-permute-start.4
  42.4 1.5 collective-permute-start.5
  44.7 11.3 %collective-permute-done.2.p3 = bf16[256,1280]{1,0:T(8,128)(2,1)S(1)} collective-permute-done((bf16[256,1280]{1,0:T(8,128)(2,1)}, bf16[256,1280]{1,0:T(8,128)(2,1)S(1)}, u32[]{:S(2)}, u32[]{:S(2)}) %collective-permute-start.2) | collective-permute-done | bytes 655392 | tf_op jit(solution)/shard_map/ppermute | solution.py:38
  55.9 2.6 %collective-permute-start.6 = (f32[16,256]{1,0:T(8,128)}, f32[16,256]{1,0:T(8,128)S(1)}, u32[]{:S(2)}, u32[]{:S(2)}) collective-permute-start(f32[16,256]{1,0:T(8,128)} %get-tuple-element.30), channel_id=1, source_target_pairs={{0,18},{1,19},{2,16},{3,17},{4,22},{5,23},{6,20},{7,21},{8,26},{9,... | collective-permute-start | bytes 49160 | tf_op jit(solution)/shard_map/ppermute | solution.py:38
  58.5 10.2 %collective-permute-done.p1 = bf16[256,1280]{1,0:T(8,128)(2,1)S(1)} collective-permute-done((bf16[256,1280]{1,0:T(8,128)(2,1)}, bf16[256,1280]{1,0:T(8,128)(2,1)S(1)}, u32[]{:S(2)}, u32[]{:S(2)}) %collective-permute-start) | collective-permute-done | bytes 655392 | tf_op jit(solution)/shard_map/ppermute | solution.py:38
  68.9 3.5 %collective-permute-start.3 = (bf16[2,16,1280]{2,1,0:T(8,128)(2,1)S(1)}, bf16[2,16,1280]{2,1,0:T(8,128)(2,1)S(1)}, u32[]{:S(2)}, u32[]{:S(2)}) collective-permute-start(bf16[2,16,1280]{2,1,0:T(8,128)(2,1)S(1)} %maximum_select_fusion.1), channel_id=1, source_target_pairs={{0,4},{1,5},{2,6},{3,7},{4,8},{5,9},{6,10},{7,11},{8,12},{9,13},{1... | collective-permute-start | bytes 245768 | tf_op jit(solution)/shard_map/ppermute | solution.py:38
  74.6 2.1 collective-permute-done.3.halo
  77.3 15.9 %conv_states.1 = (bf16[4,256,1024]{2,1,0:T(8,128)(2,1)}, bf16[4,256,256]{2,1,0:T(8,128)(2,1)}, f32[4,16,256]{2,1,0:T(8,128)}, f32[4,256,16]{2,1,0:T(8,128)}, bf1...) custom-call(s32[2]{0:T(128)} %pad_add_fusion.place, ...), custom_call_target="tpu_custom_call" | custom-call | tf_op jit(solution)/shard_map/conv_states/pallas_call | solution.py:256
  93.2 4.4 %collective-permute-start.7 = (bf16[2,144,1024]{2,1,0:T(8,128)(2,1)}, bf16[2,144,1024]{2,1,0:T(8,128)(2,1)S(1)}, u32[]{:S(2)}, u32[]{:S(2)}) collective-permute-start(bf16[2,144,1024]{2,1,0:T(8,128)(2,1)} %get-tuple-element.35.late), channel_id=1, source_target_pairs={{0,4},{1,5},{2,6},{3,7},{4,8},{5,9},{6,10},{7,11},{8,12},{9,13},{1... | collective-permute-start | bytes 1769480 | tf_op jit(solution)/shard_map/ppermute | solution.py:38
  97.6 26.1 %collective-permute-done.7.early.near = bf16[2,144,1024]{2,1,0:T(8,128)(2,1)S(1)} collective-permute-done((bf16[2,144,1024]{2,1,0:T(8,128)(2,1)}, bf16[2,144,1024]{2,1,0:T(8,128)(2,1)S(1)}, u32[]{:S(2)}, u32[]{:S(2)}) %collective-permute-start.7) | collective-permute-done | bytes 589856 | tf_op jit(solution)/shard_map/ppermute | solution.py:38
  124.6 2.3 %join.1 = bf16[2,144,1024]{2,1,0:T(8,128)(2,1)} custom-call(bf16[2,144,1024]{2,1,0:T(8,128)(2,1)} %get-tuple-element.35.late, bf16[2,144,1024]{2,1,0:T(8,128)(2,1)} %copy-done), custom_call_target="tpu_custom_call" | custom-call | tf_op jit(solution)/shard_map/join/pallas_call | solution.py:291
  126.9 6.1 %collective-permute-start.8 = (bf16[2,144,1024]{2,1,0:T(8,128)(2,1)}, bf16[2,144,1024]{2,1,0:T(8,128)(2,1)S(1)}, u32[]{:S(2)}, u32[]{:S(2)}) collective-permute-start(bf16[2,144,1024]{2,1,0:T(8,128)(2,1)} %join.1), channel_id=1, source_target_pairs={{0,8},{1,9},{2,10},{3,11},{4,12},{5,13},{6,14},{7,15},{16,24},{17,... | collective-permute-start | bytes 1769480 | tf_op jit(solution)/shard_map/ppermute | solution.py:38
  133.0 3.2 %cut.1 = (bf16[256,1024]{1,0:T(8,128)(2,1)}, bf16[256,1024]{1,0:T(8,128)(2,1)}, bf16[256,1024]{1,0:T(8,128)(2,1)}) custom-call(s32[4]{0:T(128)} %pad_add_fusion.1.order, bf16[256,4096]{1,0:T(8,128)(2,1)} %z0.1, bf16[256,4096]{1,0:T(8,128)(2,1)} %z0.1, bf16[256,4096]{1,0:T(8,128)(2,1)} %z0.1), custom_call_target="tpu_custom_call" | custom-call | tf_op jit(solution)/shard_map/cut/pallas_call | solution.py:105
  136.2 1.7 collective-permute-start.10
  137.9 1.5 collective-permute-start.11
  140.4 7.6 %within.1.y = f32[4,256,1024]{2,1,0:T(8,128)} custom-call(s32[2]{0:T(128)} %pad_add_fusion.place, bf16[4,256,1024]{2,1,0:T(8,128)(2,1)} %get-tuple-element.31.xc, bf16[4,256,256]{2,1,0:T(8,128)(2,1)} %get-tuple-element.32.bc, f32[4,16,256]{2,1,0:T(8,128)} %get-tuple-element.33.low, f32[4,256,16]{2,1,0:T(8,128)} %get-tuple-element.34.cum, ...), custom_call_target="tpu_custom_call" | custom-call | tf_op jit(solution)/shard_map/within/pallas_call | solution.py:339
  148.0 3.2 %collective-permute-done.10.z2 = bf16[256,1024]{1,0:T(8,128)(2,1)S(1)} collective-permute-done((bf16[256,1024]{1,0:T(8,128)(2,1)}, bf16[256,1024]{1,0:T(8,128)(2,1)S(1)}, u32[]{:S(2)}, u32[]{:S(2)}) %collective-permute-start.10) | collective-permute-done | bytes 524320 | tf_op jit(solution)/shard_map/ppermute | solution.py:38
  151.2 10.7 %collective-permute-done.11.z3 = bf16[256,1024]{1,0:T(8,128)(2,1)S(1)} collective-permute-done((bf16[256,1024]{1,0:T(8,128)(2,1)}, bf16[256,1024]{1,0:T(8,128)(2,1)S(1)}, u32[]{:S(2)}, u32[]{:S(2)}) %collective-permute-start.11) | collective-permute-done | bytes 524320 | tf_op jit(solution)/shard_map/ppermute | solution.py:38
  164.3 10.1 %gate_norm.1 = bf16[4,256,1024]{2,1,0:T(8,128)(2,1)} custom-call(s32[2]{0:T(128)} %pad_add_fusion.place, f32[4,256,1024]{2,1,0:T(8,128)} %within.1.y, bf16[4,256,256]{2,1,0:T(8,128)(2,1)} %get-tuple-element.32.bc, f32[4,256,16]{2,1,0:T(8,128)} %get-tuple-element.34.cum, bf16[2,144,1024]{2,1,0:T(8,128)(2,1)} %copy-done, bf16[2,144,1024]{2,1,0:T(8,128)(2,1)} %copy-done.5, ...), custom_call_target="tpu_custom_call" | custom-call | tf_op jit(solution)/shard_map/gate_norm/pallas_call | solution.py:386
  174.4 6.1 %fusion.8 = bf16[1024,1024]{1,0:T(8,128)(2,1)} fusion(bf16[1024,1024]{1,0:T(8,128)(2,1)} %bitcast.30, bf16[1024,2048]{1,0:T(8,128)(2,1)} %all-gather.2.cloned.1.call-done, s32[]{:T(128)S(6)} %select_n.46), kind=kOutput, calls=%fused_computation.8 | convolution fusion | flops 2148532224 | bytes 6291460 | tf_op jit(solution)/shard_map/dot_general | solution.py:466
  180.6 4.5 %collective-permute-done.14 = bf16[1024,1024]{1,0:T(8,128)(2,1)} collective-permute-done((bf16[1024,1024]{1,0:T(8,128)(2,1)}, bf16[1024,1024]{1,0:T(8,128)(2,1)}, u32[]{:S(2)}, u32[]{:S(2)}) %collective-permute-start.14) | collective-permute-done | bytes 2097184 | tf_op jit(solution)/shard_map/ppermute | solution.py:38
  185.1 4.6 %fusion.17 = (bf16[1024,1024]{1,0:T(8,128)(2,1)S(1)}, f32[1024,1024]{1,0:T(8,128)S(1)}) fusion(bf16[1024,1024]{1,0:T(8,128)(2,1)} %collective-permute-done.14, bf16[1024,1024]{1,0:T(8,128)(2,1)S(1)} %bitcast.31, bf16[1024,2048]{1,0:T(8,128)(2,1)} %all-gather.2.cloned.1.call-done, s32[]{:T(128)S(6)} %select_n.45), kind=kOutput, calls=%fused_computation.26 | convolution fusion | flops 2150629376 | bytes 12582916 | tf_op jit(solution)/shard_map/dot_general | solution.py:468
  190.4 1.5 collective-permute-start.16
  193.3 10.5 %collective-permute-done.15 = bf16[256,1024]{1,0:T(8,128)(2,1)S(1)} collective-permute-done((bf16[256,1024]{1,0:T(8,128)(2,1)S(1)}, bf16[256,1024]{1,0:T(8,128)(2,1)S(1)}, u32[]{:S(2)}, u32[]{:S(2)}) %collective-permute-start.15) | collective-permute-done | bytes 524320 | tf_op jit(solution)/shard_map/ppermute | solution.py:38
  205.2 11.0 %collective-permute-done.17 = bf16[256,1024]{1,0:T(8,128)(2,1)S(1)} collective-permute-done((bf16[256,1024]{1,0:T(8,128)(2,1)S(1)}, bf16[256,1024]{1,0:T(8,128)(2,1)S(1)}, u32[]{:S(2)}, u32[]{:S(2)}) %collective-permute-start.17) | collective-permute-done | bytes 524320 | tf_op jit(solution)/shard_map/ppermute | solution.py:38
  (67 shorter events, 16.7 us)
Async XLA Ops:
  6.5 167.9 %all-gather.2.cloned.1.call-start = ((), (), s32[]{:S(2)}) async-start(), calls=%async_computation | async-start | bytes 5242880 | tf_op jit(solution)/shard_map/all_gather | solution.py:442
  10.5 3.0 %collective-permute-start.12 = (bf16[2,1024,256]{2,1,0:T(8,128)(2,1)}, bf16[2,1024,256]{2,1,0:T(8,128)(2,1)S(1)}, u32[]{:S(2)}, u32[]{:S(2)}) collective-permute-start(bf16[2,1024,256]{2,1,0:T(8,128)(2,1)} %bitcast.28), channel_id=1, source_target_pairs={{0,1},{1,0},{2,3},{3,2},{4,5},{5,4},{6,7},{7,6},{8,9},{9,8},{10,11... | collective-permute-start | bytes 3145736 | tf_op jit(solution)/shard_map/ppermute | solution.py:38
  15.2 16.4 %copy-start.10 = (f32[256,64]{0,1:T(8,128)S(1)}, f32[256,64]{0,1:T(8,128)}, u32[]{:S(2)}) copy-start(f32[256,64]{0,1:T(8,128)} %param.15) | copy-start | bytes 196612
  15.2 15.2 %collective-permute-start.13 = (bf16[1024,256]{1,0:T(8,128)(2,1)S(1)}, bf16[1024,256]{1,0:T(8,128)(2,1)S(1)}, u32[]{:S(2)}, u32[]{:S(2)}) collective-permute-start(bf16[1024,256]{1,0:T(8,128)(2,1)S(1)} %get-tuple-element.45), channel_id=1, source_target_pairs={{0,2},{1,3},{2,0},{3,1},{4,6},{5,7},{6,4},{7,5},{8,10},{9,11},{10,... | collective-permute-start | bytes 1572872 | tf_op jit(solution)/shard_map/ppermute | solution.py:38
  33.0 40.1 %copy-start.14 = (f32[64]{0:T(128)S(1)}, f32[64]{0:T(128)}, u32[]{:S(2)}) copy-start(f32[64]{0:T(128)} %param.18) | copy-start | bytes 772
  33.0 40.8 %copy-start.15 = (f32[64]{0:T(128)S(1)}, f32[64]{0:T(128)}, u32[]{:S(2)}) copy-start(f32[64]{0:T(128)} %param.19) | copy-start | bytes 772
  37.1 18.8 %collective-permute-start.2 = (bf16[256,1280]{1,0:T(8,128)(2,1)}, bf16[256,1280]{1,0:T(8,128)(2,1)S(1)}, u32[]{:S(2)}, u32[]{:S(2)}) collective-permute-start(bf16[256,1280]{1,0:T(8,128)(2,1)} %get-tuple-element.26), channel_id=1, source_target_pairs={{0,18},{1,19},{2,16},{3,17},{4,22},{5,23},{6,20},{7,21},{8,26},{9,... | collective-permute-start | bytes 1966088 | tf_op jit(solution)/shard_map/ppermute | solution.py:38
  39.8 29.0 %collective-permute-start = (bf16[256,1280]{1,0:T(8,128)(2,1)}, bf16[256,1280]{1,0:T(8,128)(2,1)S(1)}, u32[]{:S(2)}, u32[]{:S(2)}) collective-permute-start(bf16[256,1280]{1,0:T(8,128)(2,1)} %get-tuple-element.24), channel_id=1, source_target_pairs={{0,2},{1,3},{2,0},{3,1},{4,6},{5,7},{6,4},{7,5},{8,10},{9,11},{10,... | collective-permute-start | bytes 1966088 | tf_op jit(solution)/shard_map/ppermute | solution.py:38
  40.3 28.6 %collective-permute-start.1 = (bf16[256,1280]{1,0:T(8,128)(2,1)}, bf16[256,1280]{1,0:T(8,128)(2,1)S(1)}, u32[]{:S(2)}, u32[]{:S(2)}) collective-permute-start(bf16[256,1280]{1,0:T(8,128)(2,1)} %get-tuple-element.25), channel_id=1, source_target_pairs={{0,16},{1,17},{2,18},{3,19},{4,20},{5,21},{6,22},{7,23},{8,24},{9,... | collective-permute-start | bytes 1966088 | tf_op jit(solution)/shard_map/ppermute | solution.py:38
  40.6 33.9 %collective-permute-start.4 = (f32[16,256]{1,0:T(8,128)}, f32[16,256]{1,0:T(8,128)S(1)}, u32[]{:S(2)}, u32[]{:S(2)}) collective-permute-start(f32[16,256]{1,0:T(8,128)} %get-tuple-element.28), channel_id=1, source_target_pairs={{0,2},{1,3},{2,0},{3,1},{4,6},{5,7},{6,4},{7,5},{8,10},{9,11},{10,... | collective-permute-start | bytes 49160 | tf_op jit(solution)/shard_map/ppermute | solution.py:38
  42.4 32.1 %collective-permute-start.5 = (f32[16,256]{1,0:T(8,128)}, f32[16,256]{1,0:T(8,128)S(1)}, u32[]{:S(2)}, u32[]{:S(2)}) collective-permute-start(f32[16,256]{1,0:T(8,128)} %get-tuple-element.29), channel_id=1, source_target_pairs={{0,16},{1,17},{2,18},{3,19},{4,20},{5,21},{6,22},{7,23},{8,24},{9,... | collective-permute-start | bytes 49160 | tf_op jit(solution)/shard_map/ppermute | solution.py:38
  55.9 20.8 %copy-start.2 = (bf16[256,1280]{1,0:T(8,128)(2,1)}, bf16[256,1280]{1,0:T(8,128)(2,1)S(1)}, u32[]{:S(2)}) copy-start(bf16[256,1280]{1,0:T(8,128)(2,1)S(1)} %collective-permute-done.2.p3) | copy-start | bytes 1966084
  55.9 18.6 %collective-permute-start.6 = (f32[16,256]{1,0:T(8,128)}, f32[16,256]{1,0:T(8,128)S(1)}, u32[]{:S(2)}, u32[]{:S(2)}) collective-permute-start(f32[16,256]{1,0:T(8,128)} %get-tuple-element.30), channel_id=1, source_target_pairs={{0,18},{1,19},{2,16},{3,17},{4,22},{5,23},{6,20},{7,21},{8,26},{9,... | collective-permute-start | bytes 49160 | tf_op jit(solution)/shard_map/ppermute | solution.py:38
  68.8 7.9 %copy-start.3 = (bf16[256,1280]{1,0:T(8,128)(2,1)}, bf16[256,1280]{1,0:T(8,128)(2,1)S(1)}, u32[]{:S(2)}) copy-start(bf16[256,1280]{1,0:T(8,128)(2,1)S(1)} %collective-permute-done.p1) | copy-start | bytes 1966084
  68.9 7.8 %copy-start.4 = (bf16[256,1280]{1,0:T(8,128)(2,1)}, bf16[256,1280]{1,0:T(8,128)(2,1)S(1)}, u32[]{:S(2)}) copy-start(bf16[256,1280]{1,0:T(8,128)(2,1)S(1)} %collective-permute-done.1.p2) | copy-start | bytes 1966084
  68.9 7.7 %collective-permute-start.3 = (bf16[2,16,1280]{2,1,0:T(8,128)(2,1)S(1)}, bf16[2,16,1280]{2,1,0:T(8,128)(2,1)S(1)}, u32[]{:S(2)}, u32[]{:S(2)}) collective-permute-start(bf16[2,16,1280]{2,1,0:T(8,128)(2,1)S(1)} %maximum_select_fusion.1), channel_id=1, source_target_pairs={{0,4},{1,5},{2,6},{3,7},{4,8},{5,9},{6,10},{7,11},{8,12},{9,13},{1... | collective-permute-start | bytes 245768 | tf_op jit(solution)/shard_map/ppermute | solution.py:38
  74.5 2.2 copy-start.11
  74.5 2.2 copy-start.12
  74.5 2.2 copy-start.13
  93.2 30.5 %collective-permute-start.7 = (bf16[2,144,1024]{2,1,0:T(8,128)(2,1)}, bf16[2,144,1024]{2,1,0:T(8,128)(2,1)S(1)}, u32[]{:S(2)}, u32[]{:S(2)}) collective-permute-start(bf16[2,144,1024]{2,1,0:T(8,128)(2,1)} %get-tuple-element.35.late), channel_id=1, source_target_pairs={{0,4},{1,5},{2,6},{3,7},{4,8},{5,9},{6,10},{7,11},{8,12},{9,13},{1... | collective-permute-start | bytes 1769480 | tf_op jit(solution)/shard_map/ppermute | solution.py:38
  126.9 12.8 %copy-start.16 = (f32[64]{0:T(128)S(1)}, f32[64]{0:T(128)}, u32[]{:S(2)}) copy-start(f32[64]{0:T(128)} %param.20) | copy-start | bytes 772
  126.9 36.4 %collective-permute-start.8 = (bf16[2,144,1024]{2,1,0:T(8,128)(2,1)}, bf16[2,144,1024]{2,1,0:T(8,128)(2,1)S(1)}, u32[]{:S(2)}, u32[]{:S(2)}) collective-permute-start(bf16[2,144,1024]{2,1,0:T(8,128)(2,1)} %join.1), channel_id=1, source_target_pairs={{0,8},{1,9},{2,10},{3,11},{4,12},{5,13},{6,14},{7,15},{16,24},{17,... | collective-permute-start | bytes 1769480 | tf_op jit(solution)/shard_map/ppermute | solution.py:38
  136.2 15.0 %collective-permute-start.10 = (bf16[256,1024]{1,0:T(8,128)(2,1)}, bf16[256,1024]{1,0:T(8,128)(2,1)S(1)}, u32[]{:S(2)}, u32[]{:S(2)}) collective-permute-start(bf16[256,1024]{1,0:T(8,128)(2,1)} %get-tuple-element.39), channel_id=1, source_target_pairs={{0,16},{1,17},{2,18},{3,19},{4,20},{5,21},{6,22},{7,23},{8,24},{9,... | collective-permute-start | bytes 1572872 | tf_op jit(solution)/shard_map/ppermute | solution.py:38
  137.9 24.0 %collective-permute-start.11 = (bf16[256,1024]{1,0:T(8,128)(2,1)}, bf16[256,1024]{1,0:T(8,128)(2,1)S(1)}, u32[]{:S(2)}, u32[]{:S(2)}) collective-permute-start(bf16[256,1024]{1,0:T(8,128)(2,1)} %get-tuple-element.40), channel_id=1, source_target_pairs={{0,18},{1,19},{2,16},{3,17},{4,22},{5,23},{6,20},{7,21},{8,26},{9,... | collective-permute-start | bytes 1572872 | tf_op jit(solution)/shard_map/ppermute | solution.py:38
  139.3 23.9 %collective-permute-start.9 = (bf16[256,1024]{1,0:T(8,128)(2,1)}, bf16[256,1024]{1,0:T(8,128)(2,1)S(1)}, u32[]{:S(2)}, u32[]{:S(2)}) collective-permute-start(bf16[256,1024]{1,0:T(8,128)(2,1)} %get-tuple-element.38), channel_id=1, source_target_pairs={{0,2},{1,3},{2,0},{3,1},{4,6},{5,7},{6,4},{7,5},{8,10},{9,11},{10,... | collective-permute-start | bytes 1572872 | tf_op jit(solution)/shard_map/ppermute | solution.py:38
  151.2 12.1 %copy-start.6 = (bf16[256,1024]{1,0:T(8,128)(2,1)}, bf16[256,1024]{1,0:T(8,128)(2,1)S(1)}, u32[]{:S(2)}) copy-start(bf16[256,1024]{1,0:T(8,128)(2,1)S(1)} %collective-permute-done.10.z2) | copy-start | bytes 1572868
  161.9 1.4 copy-start.7
  174.4 10.6 %copy-start.1 = (bf16[4,256,1024]{2,1,0:T(8,128)(2,1)S(1)}, bf16[4,256,1024]{2,1,0:T(8,128)(2,1)}, u32[]{:S(2)}) copy-start(bf16[4,256,1024]{2,1,0:T(8,128)(2,1)} %gate_norm.1) | copy-start | bytes 6291460
  180.6 4.5 %collective-permute-start.14 = (bf16[1024,1024]{1,0:T(8,128)(2,1)}, bf16[1024,1024]{1,0:T(8,128)(2,1)}, u32[]{:S(2)}, u32[]{:S(2)}) collective-permute-start(bf16[1024,1024]{1,0:T(8,128)(2,1)} %fusion.8), channel_id=1, source_target_pairs={{0,1},{1,0},{2,3},{3,2},{4,5},{5,4},{6,7},{7,6},{8,9},{9,8},{10,11... | collective-permute-start | bytes 6291464 | tf_op jit(solution)/shard_map/ppermute | solution.py:38
  189.7 14.0 %collective-permute-start.15 = (bf16[256,1024]{1,0:T(8,128)(2,1)S(1)}, bf16[256,1024]{1,0:T(8,128)(2,1)S(1)}, u32[]{:S(2)}, u32[]{:S(2)}) collective-permute-start(bf16[256,1024]{1,0:T(8,128)(2,1)S(1)} %get-tuple-element.41), channel_id=1, source_target_pairs={{0,2},{1,3},{2,0},{3,1},{4,6},{5,7},{6,4},{7,5},{8,10},{9,11},{10,... | collective-permute-start | bytes 1572872 | tf_op jit(solution)/shard_map/ppermute | solution.py:38
  190.4 14.8 %collective-permute-start.16 = (bf16[256,1024]{1,0:T(8,128)(2,1)S(1)}, bf16[256,1024]{1,0:T(8,128)(2,1)S(1)}, u32[]{:S(2)}, u32[]{:S(2)}) collective-permute-start(bf16[256,1024]{1,0:T(8,128)(2,1)S(1)} %get-tuple-element.43), channel_id=1, source_target_pairs={{0,16},{1,17},{2,18},{3,19},{4,20},{5,21},{6,22},{7,23},{8,24},{9,... | collective-permute-start | bytes 1572872 | tf_op jit(solution)/shard_map/ppermute | solution.py:38
  191.8 24.4 %collective-permute-start.17 = (bf16[256,1024]{1,0:T(8,128)(2,1)S(1)}, bf16[256,1024]{1,0:T(8,128)(2,1)S(1)}, u32[]{:S(2)}, u32[]{:S(2)}) collective-permute-start(bf16[256,1024]{1,0:T(8,128)(2,1)S(1)} %get-tuple-element.42), channel_id=1, source_target_pairs={{0,18},{1,19},{2,16},{3,17},{4,22},{5,23},{6,20},{7,21},{8,26},{9,... | collective-permute-start | bytes 1572872 | tf_op jit(solution)/shard_map/ppermute | solution.py:38
  (4 other events, 3.3 us)
Sparse Core Ops, SparseCore 0:
  31.7 92.6 all-gather.1

commit v2 on v1

--- a/solution.py
+++ b/solution.py
@@ -46,14 +46,31 @@
     return send(array, lambda x, z, y, t: (x, z + distance, y, t))
 
 
+def after(these, those):
+    return lax.optimization_barrier((these, those))
+
+
 def expander():
-    row = lax.broadcasted_iota(jnp.int32, (PER, GROUP), 0)
-    lane = lax.broadcasted_iota(jnp.int32, (PER, GROUP), 1)
-    return jnp.where(lane // HEADDIM == row, 1.0, 0.0).astype(F32)
+    row = lax.broadcasted_iota(jnp.int32, (3 * PER, GROUP), 0)
+    lane = lax.broadcasted_iota(jnp.int32, (3 * PER, GROUP), 1)
+    return jnp.where(lane // HEADDIM == row % PER, 1.0, 0.0).astype(BF16)
+
+
+def thirds(v):
+    high = v.astype(BF16)
+    rest = v - high.astype(F32)
+    middle = rest.astype(BF16)
+    last = (rest - middle.astype(F32)).astype(BF16)
+    return jnp.concatenate([high, middle, last], axis=0)
+
+
+def widen(terms, spread):
+    return lax.dot_general(terms, spread, (((0,), (0,)), ((), ())), preferred_element_type=F32)
 
 
 def silu(v):
-    return v * lax.logistic(v)
+    half = 0.5 * v
+    return half + half * jnp.tanh(half)
 
 
 def pack_kernel(order, x0, x1, x2, x3, b0, b1, b2, b3, dt, o0, o1, o2, o3, d0, d1, d2, d3, turned):
@@ -167,7 +184,7 @@
 
 def conv_kernel(
     place, p0, p1, p2, p3, halo, cx, cbc, d0, d1, d2, d3, al, db,
-    xc, bc, low, cum, pair, first, fade, states, decays,
+    xc, bc, low, cum, kept, pair, first, fade, states, decays,
 ):
     here = place[1]
     pieces = (p0, p1, p2, p3)
@@ -176,7 +193,7 @@
     spread = expander()
     row = lax.broadcasted_iota(jnp.int32, (rows, rows), 0)
     col = lax.broadcasted_iota(jnp.int32, (rows, rows), 1)
-    upto = jnp.where(row <= col, 1.0, 0.0).astype(F32)
+    upto = jnp.where(row <= col, 1.0, 0.0).astype(BF16)
     for k in range(4):
         piece, other = pieces[k], pieces[k ^ 1]
         opening = here == (k & 1)
@@ -204,23 +221,23 @@
         raw = steps[k][...] + db[...]
         dt = jnp.maximum(raw, 0.0) + jnp.log1p(jnp.exp(-jnp.abs(raw)))
         rate = -jnp.exp(al[...])
-        total = jnp.dot(dt * rate, upto, precision=HIGH, preferred_element_type=F32)
+        sums = jnp.dot(thirds(dt * rate), upto, preferred_element_type=F32)
+        total = sums[:PER] + sums[PER : 2 * PER] + sums[2 * PER :]
         low[k] = (total - jnp.log(dt)) * LOG2E
-        upright = total.T
-        cum[k] = upright
-        load = (jnp.exp(total[:, rows - 1 :] - total) * dt).T
-        wide = jnp.dot(load, spread, precision=HIGH, preferred_element_type=F32)
+        cum[k] = (total * LOG2E).T
+        fall = jnp.exp(total)
+        kept[k] = thirds(fall)
+        wide = widen(thirds(jnp.exp(total[:, rows - 1 :] - total) * dt), spread)
         loaded = (xc[k].astype(F32) * wide).astype(BF16)
         states[k] = lax.dot_general(
             b, loaded, (((0,), (0,)), ((), ())), preferred_element_type=F32
         )
-        end = jnp.broadcast_to(jnp.exp(upright[rows - 1 :, :]), (8, PER))
-        decays[k] = jnp.dot(end, spread, precision=HIGH, preferred_element_type=F32)
+        decays[k] = widen(kept[k, :, rows - 128 :], spread)[120:]
     for r in range(2):
         early, late = 2 * r + here, 2 * r + 1 - here
         decay_early, decay_late = decays[early], decays[late]
-        pair[r, :STATE, :] = (states[late] + decay_late[0:1] * states[early]).astype(BF16)
-        pair[r, STATE:, :] = split(decay_early * decay_late)
+        pair[r, :STATE, :] = (states[late] + decay_late[7:8] * states[early]).astype(BF16)
+        pair[r, STATE:, :] = split(jnp.broadcast_to((decay_early * decay_late)[7:8], (8, GROUP)))
         first[r] = states[early]
         fade[r] = decay_early
 
@@ -249,6 +266,7 @@
         ((4, rows, 2 * STATE), BF16),
         ((4, PER, rows), F32),
         ((4, rows, PER), F32),
+        ((4, 3 * PER, rows), BF16),
         ((2, STATE + 16, GROUP), BF16),
         ((2, STATE, GROUP), F32),
         ((2, 8, GROUP), F32),
@@ -310,7 +328,7 @@
     square = scores[half:, :half]
     end = jnp.where(causal, scores[half:, half:], 0.0)
     lane = lax.broadcasted_iota(jnp.int32, (rows, 2 * HEADDIM), 1)
-    upright = cum[0] * LOG2E
+    upright = cum[0]
     for j in range(PER // 2):
         at = slice(j * 2 * HEADDIM, (j + 1) * 2 * HEADDIM)
         x = xc[0, :, at]
@@ -356,7 +374,7 @@
 
 
 def gate_kernel(
-    place, y, bc, cum, near, far, first, fade, z0, z1, z2, z3, gain, bits, out, gate
+    place, y, bc, kept, near, far, first, fade, z0, z1, z2, z3, gain, bits, out, gate
 ):
     k = pl.program_id(0)
     for index, z in enumerate((z0, z1, z2, z3)):
@@ -369,16 +387,15 @@
     incoming = near[0, :STATE, :].astype(F32) + joined(near[0, STATE:, :]) * far[
         0, :STATE, :
     ].astype(F32)
-    incoming = jnp.where(opening, incoming, fade[0, 0:1] * incoming + first[0])
+    incoming = jnp.where(opening, incoming, fade[0, 7:8] * incoming + first[0])
     carried = jnp.dot(bc[0, :, STATE:], incoming.astype(BF16), preferred_element_type=F32)
-    kept = jnp.dot(jnp.exp(cum[0]), expander(), precision=HIGH, preferred_element_type=F32)
-    gated = (y[0] + kept * carried) * gate[...]
+    gated = (y[0] + widen(kept[0], expander()) * carried) * gate[...]
     scale = lax.rsqrt(jnp.mean(gated * gated, axis=1, keepdims=True) + 1e-05)
     signed = gain[...] * (1 - 2 * bits[...]).astype(F32)
     out[0] = (gated * scale * signed).astype(BF16)
 
 
-def gate_norm(place, y, bc, cum, near, far, first, fade, z_in, zs, gain, bits):
+def gate_norm(place, y, bc, kept, near, far, first, fade, z_in, zs, gain, bits):
     rows = y.shape[1]
     block = lambda *shape: pl.BlockSpec((1,) + shape, lambda k, place: (k, 0, 0))
     part = lambda *shape: pl.BlockSpec((1,) + shape, lambda k, place: (k // 2, 0, 0))
@@ -391,7 +408,7 @@
             in_specs=[
                 block(rows, GROUP),
                 block(rows, 2 * STATE),
-                block(rows, PER),
+                block(3 * PER, rows),
                 part(STATE + 16, GROUP),
                 part(STATE + 16, GROUP),
                 part(STATE, GROUP),
@@ -405,7 +422,7 @@
         ),
         out_shape=jax.ShapeDtypeStruct((4, rows, GROUP), BF16),
         name="gate_norm",
-    )(place, y, bc, cum, near, far, first, fade, z_in, *zs, gain, bits)
+    )(place, y, bc, kept, near, far, first, fade, z_in, *zs, gain, bits)
 
 
 def per_device(
@@ -418,36 +435,44 @@
     order = jnp.stack([mine ^ k for k in range(4)]).astype(jnp.int32)
     place = jnp.stack([mine, y_here]).astype(jnp.int32)
 
+    turned = turn(x_here.reshape(1).astype(jnp.int32), out_weight)
+    turned = turned.reshape(2, GROUP, out_weight.shape[1])
+    across = send(turned, lambda x, z, y, t: (x, z, y, 1 - t))
+
+    x_in, turned = after(x_in, turned)
     packed = pack(order, x_in, bc_in, dt_raw)
+    packed, across = after(packed, across)
+    own = turned.astype(F32)
+    rotated = (across.astype(F32) + jnp.where(t_here == 0, own, -own)).astype(BF16)
+    packed, rotated = after(packed, rotated)
+    keep = lax.dynamic_index_in_dim(rotated, y_here, 0, keepdims=False)
+    given = swap(lax.dynamic_index_in_dim(rotated, 1 - y_here, 0, keepdims=False), 1)
     pieces = [packed[0]] + [swap(packed[k], k) for k in range(1, 4)]
     steps = [packed[4]] + [swap(packed[4 + k], k) for k in range(1, 4)]
+    z_in, packed = after(z_in, packed)
+    slices = cut(order, z_in)
+    given, slices = after(given, slices)
+    columns = jnp.where(
+        y_here == 0,
+        jnp.concatenate([keep, given], axis=1),
+        jnp.concatenate([given, keep], axis=1),
+    )
+    weight = lax.all_gather(columns, "sz", axis=1, tiled=True)
+    pieces, columns = after(pieces, columns)
     tails = [p[rows - 16 :] for p in pieces]
     closing = jnp.where(
         y_here == 1, jnp.stack([tails[0], tails[2]]), jnp.stack([tails[1], tails[3]])
     )
     halo = onward(closing, 1)
-
-    turned = turn(x_here.reshape(1).astype(jnp.int32), out_weight)
-    turned = turned.reshape(2, GROUP, out_weight.shape[1])
-    across = send(turned, lambda x, z, y, t: (x, z, y, 1 - t))
-    own = turned.astype(F32)
-    rotated = (across.astype(F32) + jnp.where(t_here == 0, own, -own)).astype(BF16)
-    kept = lax.dynamic_index_in_dim(rotated, y_here, 0, keepdims=False)
-    given = swap(lax.dynamic_index_in_dim(rotated, 1 - y_here, 0, keepdims=False), 1)
-    columns = jnp.where(
-        y_here == 0,
-        jnp.concatenate([kept, given], axis=1),
-        jnp.concatenate([given, kept], axis=1),
-    )
-    weight = lax.all_gather(columns, "sz", axis=1, tiled=True)
-
-    zs = [swap(z, k + 1) for k, z in enumerate(cut(order, z_in))]
-
-    xc, bc, low, cum, pair, first, fade = conv_states(
+    slices, pieces = after(slices, pieces)
+    zs = [swap(z, k + 1) for k, z in enumerate(slices)]
+
+    xc, bc, low, cum, kept, pair, first, fade = conv_states(
         place, pieces, halo, conv_x, conv_bc, steps, a_log[:, None], dt_bias[:, None]
     )
     near = onward(pair, 1)
     y = within(place, xc, bc, low, cum, jnp.repeat(d_skip, HEADDIM)[None])
+    near, y = after(near, y)
     span = join(pair, near)
     distance = 2
     far = onward(span, distance)
@@ -456,7 +481,7 @@
         distance *= 2
         far = onward(span, distance)
     act = gate_norm(
-        place, y, bc, cum, near, far, first, fade, z_in, zs, gain[None], sign_bits[None]
+        place, y, bc, kept, near, far, first, fade, z_in, zs, gain[None], sign_bits[None]
     )
 
     act = act.reshape(4 * rows, GROUP)

time: 225 us -> 220 us (0.978)
  the two profiles are of different devices: /device:TPU:0 before, /device:TPU:28 now
where the time goes in v2:
time: 220 us; the launch traced here: 218 us
  waiting for transfers between devices  122 us (55%)
  Pallas kernels  42 us (19%)
  starting transfers between devices  18.7 us (8%)
  between operations  13.6 us (6%)
  matrix products  10.6 us (5%)
  local copies, waits for them, and re-layouts  6.3 us (3%)
  other arithmetic  4.07 us (2%)
    ppermute x18, waiting for transfers between devices, send(): return lax.ppermute(array, AXES, pairs)  122 us
    ppermute x18, starting transfers between devices, send(): return lax.ppermute(array, AXES, pairs)  18.7 us
    pallas_call x1, Pallas kernels, conv_states(): pl.pallas_call(conv_kernel, grid_spec=pltpu.PrefetchScalarGridSpec(num_sc...  12.7 us
    pallas_call x1, Pallas kernels, gate_norm(): pl.pallas_call(gate_kernel, grid_spec=pltpu.PrefetchScalarGridSpec(num_sc...  8.22 us
    pallas_call x1, Pallas kernels, within(): pl.pallas_call(within_kernel, grid_spec=pltpu.PrefetchScalarGridSpec(num_...  7.54 us
    dot_general x1, matrix products, per_device(): away = jnp.dot(act, theirs, preferred_element_type=F32).astype(BF16)  6.1 us
    dot_general x1, matrix products, per_device(): stay = jnp.dot(act, ours, preferred_element_type=F32) + back.astype(F32)  4.55 us
  transfers between devices with their start and end apart: 19, of which 13 were waited for; matrix products, arithmetic and copies ran while one was open for 2% of the time, Pallas kernels for 17%

profile of v2, /device:TPU:28, one launch (start us, length us, event | category | flops | bytes accessed | tf_op | source)
XLA Modules:
  0.0 217.5 jit_solution(12350568648409442382)
XLA Ops:
  6.5 4.0 %turn.1 = bf16[8,256,256]{2,1,0:T(8,128)(2,1)} custom-call(s32[1]{0:T(128)} %bitcast.5.sign, bf16[4096,256]{1,0:T(8,128)(2,1)} %w.1), custom_call_target="tpu_custom_call" | custom-call | tf_op jit(solution)/shard_map/turn/pallas_call | solution.py:175
  12.0 4.1 %pack.1 = (bf16[256,1280]{1,0:T(8,128)(2,1)}, bf16[256,1280]{1,0:T(8,128)(2,1)}, bf16[256,1280]{1,0:T(8,128)(2,1)}, bf16[256,1280]{1,0:T(8,128)(2,1)}, f32[16,25...) custom-call(s32[4]{0:T(128)} %pad_add_fusion.1.order, bf16[256,4096]{1,0:T(8,128)(2,1)} %x3, ...), custom_call_target="tpu_custom_call" | custom-call | tf_op jit(solution)/shard_map/pack/pallas_call | solution.py:92
  17.1 3.2 %cut.1 = (bf16[256,1024]{1,0:T(8,128)(2,1)}, bf16[256,1024]{1,0:T(8,128)(2,1)}, bf16[256,1024]{1,0:T(8,128)(2,1)}) custom-call(s32[4]{0:T(128)} %pad_add_fusion.1.order, bf16[256,4096]{1,0:T(8,128)(2,1)} %z0, bf16[256,4096]{1,0:T(8,128)(2,1)} %z0, bf16[256,4096]{1,0:T(8,128)(2,1)} %z0), custom_call_target="tpu_custom_call" | custom-call | tf_op jit(solution)/shard_map/cut/pallas_call | solution.py:122
  20.4 10.6 %collective-permute-done.1 = bf16[1024,256]{1,0:T(8,128)(2,1)S(1)} collective-permute-done((bf16[1024,256]{1,0:T(8,128)(2,1)S(1)}, bf16[1024,256]{1,0:T(8,128)(2,1)S(1)}, u32[]{:S(2)}, u32[]{:S(2)}) %collective-permute-start.1) | collective-permute-done | bytes 524320 | tf_op jit(solution)/shard_map/ppermute | solution.py:38
  31.0 1.2 maximum_select_fusion
  32.8 1.5 collective-permute-start.3
  34.3 1.5 collective-permute-start.4
  36.3 1.5 collective-permute-start.7
  37.8 12.0 %collective-permute-done.2.p1 = bf16[256,1280]{1,0:T(8,128)(2,1)S(1)} collective-permute-done((bf16[256,1280]{1,0:T(8,128)(2,1)}, bf16[256,1280]{1,0:T(8,128)(2,1)S(1)}, u32[]{:S(2)}, u32[]{:S(2)}) %collective-permute-start.2) | collective-permute-done | bytes 655392 | tf_op jit(solution)/shard_map/ppermute | solution.py:38
  49.8 1.4 collective-permute-start.8
  51.2 13.0 %collective-permute-done.4.p3 = bf16[256,1280]{1,0:T(8,128)(2,1)S(1)} collective-permute-done((bf16[256,1280]{1,0:T(8,128)(2,1)S(1)}, bf16[256,1280]{1,0:T(8,128)(2,1)S(1)}, u32[]{:S(2)}, u32[]{:S(2)}) %collective-permute-start.4) | collective-permute-done | bytes 655392 | tf_op jit(solution)/shard_map/ppermute | solution.py:38
  65.0 1.3 collective-permute-start.5
  68.4 6.8 %collective-permute-done.5.halo = bf16[2,16,1280]{2,1,0:T(8,128)(2,1)S(1)} collective-permute-done((bf16[2,16,1280]{2,1,0:T(8,128)(2,1)S(1)}, bf16[2,16,1280]{2,1,0:T(8,128)(2,1)S(1)}, u32[]{:S(2)}, u32[]{:S(2)}) %collective-permute-start.5) | collective-permute-done | bytes 81952 | tf_op jit(solution)/shard_map/ppermute | solution.py:38
  75.9 12.7 %conv_states.1 = (bf16[4,256,1024]{2,1,0:T(8,128)(2,1)}, bf16[4,256,256]{2,1,0:T(8,128)(2,1)}, f32[4,16,256]{2,1,0:T(8,128)}, f32[4,256,16]{2,1,0:T(8,128)}, bf1...) custom-call(s32[2]{0:T(128)} %pad_add_fusion.place, ...), custom_call_target="tpu_custom_call" | custom-call | tf_op jit(solution)/shard_map/conv_states/pallas_call | solution.py:274
  88.6 1.3 collective-permute-start.9
  90.6 7.5 %within.1.y = f32[4,256,1024]{2,1,0:T(8,128)} custom-call(s32[2]{0:T(128)} %pad_add_fusion.place, bf16[4,256,1024]{2,1,0:T(8,128)(2,1)} %get-tuple-element.107.xc, bf16[4,256,256]{2,1,0:T(8,128)(2,1)} %get-tuple-element.108.bc, f32[4,16,256]{2,1,0:T(8,128)} %get-tuple-element.109.low, f32[4,256,16]{2,1,0:T(8,128)} %get-tuple-element.110.cum, ...), custom_call_target="tpu_custom_call" | custom-call | tf_op jit(solution)/shard_map/within/pallas_call | solution.py:357
  98.2 26.9 %collective-permute-done.9.early.near = bf16[2,144,1024]{2,1,0:T(8,128)(2,1)S(1)} collective-permute-done((bf16[2,144,1024]{2,1,0:T(8,128)(2,1)}, bf16[2,144,1024]{2,1,0:T(8,128)(2,1)S(1)}, u32[]{:S(2)}, u32[]{:S(2)}) %collective-permute-start.9) | collective-permute-done | bytes 589856 | tf_op jit(solution)/shard_map/ppermute | solution.py:38
  126.0 2.3 %join.1 = bf16[2,144,1024]{2,1,0:T(8,128)(2,1)} custom-call(bf16[2,144,1024]{2,1,0:T(8,128)(2,1)} %get-tuple-element.106.late, bf16[2,144,1024]{2,1,0:T(8,128)(2,1)} %copy-done.1), custom_call_target="tpu_custom_call" | custom-call | tf_op jit(solution)/shard_map/join/pallas_call | solution.py:309
  128.2 1.5 collective-permute-start.10
  130.3 1.5 collective-permute-start.12
  131.8 1.5 collective-permute-start.13
  133.3 10.8 %collective-permute-done.11.z1 = bf16[256,1024]{1,0:T(8,128)(2,1)S(1)} collective-permute-done((bf16[256,1024]{1,0:T(8,128)(2,1)}, bf16[256,1024]{1,0:T(8,128)(2,1)S(1)}, u32[]{:S(2)}, u32[]{:S(2)}) %collective-permute-start.11) | collective-permute-done | bytes 524320 | tf_op jit(solution)/shard_map/ppermute | solution.py:38
  145.1 10.5 %collective-permute-done.13.z3 = bf16[256,1024]{1,0:T(8,128)(2,1)S(1)} collective-permute-done((bf16[256,1024]{1,0:T(8,128)(2,1)S(1)}, bf16[256,1024]{1,0:T(8,128)(2,1)S(1)}, u32[]{:S(2)}, u32[]{:S(2)}) %collective-permute-start.13) | collective-permute-done | bytes 524320 | tf_op jit(solution)/shard_map/ppermute | solution.py:38
  155.6 3.1 %collective-permute-done.10.far = bf16[2,144,1024]{2,1,0:T(8,128)(2,1)S(1)} collective-permute-done((bf16[2,144,1024]{2,1,0:T(8,128)(2,1)}, bf16[2,144,1024]{2,1,0:T(8,128)(2,1)S(1)}, u32[]{:S(2)}, u32[]{:S(2)}) %collective-permute-start.10) | collective-permute-done | bytes 589856 | tf_op jit(solution)/shard_map/ppermute | solution.py:38
  159.5 8.2 %gate_norm.1 = bf16[4,256,1024]{2,1,0:T(8,128)(2,1)} custom-call(s32[2]{0:T(128)} %pad_add_fusion.place, f32[4,256,1024]{2,1,0:T(8,128)} %within.1.y, bf16[4,256,256]{2,1,0:T(8,128)(2,1)} %get-tuple-element.108.bc, bf16[4,48,256]{2,1,0:T(8,128)(2,1)} %get-tuple-element.112.kept, bf16[2,144,1024]{2,1,0:T(8,128)(2,1)} %copy-done.1, ...), custom_call_target="tpu_custom_call" | custom-call | tf_op jit(solution)/shard_map/gate_norm/pallas_call | solution.py:403
  167.8 6.1 %fusion.8 = bf16[1024,1024]{1,0:T(8,128)(2,1)} fusion(bf16[1024,1024]{1,0:T(8,128)(2,1)} %bitcast.28, bf16[1024,2048]{1,0:T(8,128)(2,1)} %all-gather.2.cloned.1.call-done, s32[]{:T(128)S(6)} %select_n.46), kind=kOutput, calls=%fused_computation.8 | convolution fusion | flops 2148532224 | bytes 6291460 | tf_op jit(solution)/shard_map/dot_general | solution.py:491
  173.9 4.5 %collective-permute-done.14 = bf16[1024,1024]{1,0:T(8,128)(2,1)} collective-permute-done((bf16[1024,1024]{1,0:T(8,128)(2,1)}, bf16[1024,1024]{1,0:T(8,128)(2,1)}, u32[]{:S(2)}, u32[]{:S(2)}) %collective-permute-start.14) | collective-permute-done | bytes 2097184 | tf_op jit(solution)/shard_map/ppermute | solution.py:38
  178.4 4.6 %fusion.17 = (bf16[1024,1024]{1,0:T(8,128)(2,1)S(1)}, f32[1024,1024]{1,0:T(8,128)S(1)}) fusion(bf16[1024,1024]{1,0:T(8,128)(2,1)} %collective-permute-done.14, bf16[1024,1024]{1,0:T(8,128)(2,1)S(1)} %bitcast.29, bf16[1024,2048]{1,0:T(8,128)(2,1)} %all-gather.2.cloned.1.call-done, s32[]{:T(128)S(6)} %select_n.45), kind=kOutput, calls=%fused_computation.26 | convolution fusion | flops 2150629376 | bytes 12582916 | tf_op jit(solution)/shard_map/dot_general | solution.py:493
  183.4 1.7 collective-permute-start.16
  185.2 1.5 collective-permute-start.17
  186.6 10.5 %collective-permute-done.15 = bf16[256,1024]{1,0:T(8,128)(2,1)S(1)} collective-permute-done((bf16[256,1024]{1,0:T(8,128)(2,1)S(1)}, bf16[256,1024]{1,0:T(8,128)(2,1)S(1)}, u32[]{:S(2)}, u32[]{:S(2)}) %collective-permute-start.15) | collective-permute-done | bytes 524320 | tf_op jit(solution)/shard_map/ppermute | solution.py:38
  198.2 11.3 %collective-permute-done.17 = bf16[256,1024]{1,0:T(8,128)(2,1)S(1)} collective-permute-done((bf16[256,1024]{1,0:T(8,128)(2,1)S(1)}, bf16[256,1024]{1,0:T(8,128)(2,1)S(1)}, u32[]{:S(2)}, u32[]{:S(2)}) %collective-permute-start.17) | collective-permute-done | bytes 524320 | tf_op jit(solution)/shard_map/ppermute | solution.py:38
  (81 shorter events, 14.0 us)
Async XLA Ops:
  6.5 161.2 %all-gather.2.cloned.1.call-start = ((), (), s32[]{:S(2)}) async-start(), calls=%async_computation | async-start | bytes 5242880 | tf_op jit(solution)/shard_map/all_gather | solution.py:460
  10.6 5.5 %collective-permute-start = (bf16[2,1024,256]{2,1,0:T(8,128)(2,1)}, bf16[2,1024,256]{2,1,0:T(8,128)(2,1)S(1)}, u32[]{:S(2)}, u32[]{:S(2)}) collective-permute-start(bf16[2,1024,256]{2,1,0:T(8,128)(2,1)} %bitcast.26), channel_id=1, source_target_pairs={{0,1},{1,0},{2,3},{3,2},{4,5},{5,4},{6,7},{7,6},{8,9},{9,8},{10,11... | collective-permute-start | bytes 3145736 | tf_op jit(solution)/shard_map/ppermute | solution.py:38
  16.6 14.4 %collective-permute-start.1 = (bf16[1024,256]{1,0:T(8,128)(2,1)S(1)}, bf16[1024,256]{1,0:T(8,128)(2,1)S(1)}, u32[]{:S(2)}, u32[]{:S(2)}) collective-permute-start(bf16[1024,256]{1,0:T(8,128)(2,1)S(1)} %get-tuple-element.123), channel_id=1, source_target_pairs={{0,2},{1,3},{2,0},{3,1},{4,6},{5,7},{6,4},{7,5},{8,10},{9,11},{10,... | collective-permute-start | bytes 1572872 | tf_op jit(solution)/shard_map/ppermute | solution.py:38
  20.4 13.9 %copy-start.18 = (bf16[256,1280]{1,0:T(8,128)(2,1)S(1)}, bf16[256,1280]{1,0:T(8,128)(2,1)}, u32[]{:S(2)}) copy-start(bf16[256,1280]{1,0:T(8,128)(2,1)} %get-tuple-element.85) | copy-start | bytes 1966084
  20.4 15.4 %copy-start.24 = (f32[16,256]{1,0:T(8,128)S(1)}, f32[16,256]{1,0:T(8,128)}, u32[]{:S(2)}) copy-start(f32[16,256]{1,0:T(8,128)} %get-tuple-element.87) | copy-start | bytes 49156
  20.4 15.9 %copy-start.23 = (f32[16,256]{1,0:T(8,128)S(1)}, f32[16,256]{1,0:T(8,128)}, u32[]{:S(2)}) copy-start(f32[16,256]{1,0:T(8,128)} %get-tuple-element.88) | copy-start | bytes 49156
  20.4 29.4 %copy-start.22 = (f32[16,256]{1,0:T(8,128)S(1)}, f32[16,256]{1,0:T(8,128)}, u32[]{:S(2)}) copy-start(f32[16,256]{1,0:T(8,128)} %get-tuple-element.89) | copy-start | bytes 49156
  20.4 46.6 %copy-start.15 = (f32[64]{0:T(128)S(1)}, f32[64]{0:T(128)}, u32[]{:S(2)}) copy-start(f32[64]{0:T(128)} %param.18) | copy-start | bytes 772
  20.4 47.3 %copy-start.16 = (f32[64]{0:T(128)S(1)}, f32[64]{0:T(128)}, u32[]{:S(2)}) copy-start(f32[64]{0:T(128)} %param.19) | copy-start | bytes 772
  32.2 57.7 %copy-start.17 = (f32[64]{0:T(128)S(1)}, f32[64]{0:T(128)}, u32[]{:S(2)}) copy-start(f32[64]{0:T(128)} %param.20) | copy-start | bytes 772
  32.2 17.5 %collective-permute-start.2 = (bf16[256,1280]{1,0:T(8,128)(2,1)}, bf16[256,1280]{1,0:T(8,128)(2,1)S(1)}, u32[]{:S(2)}, u32[]{:S(2)}) collective-permute-start(bf16[256,1280]{1,0:T(8,128)(2,1)} %get-tuple-element.83), channel_id=1, source_target_pairs={{0,2},{1,3},{2,0},{3,1},{4,6},{5,7},{6,4},{7,5},{8,10},{9,11},{10,... | collective-permute-start | bytes 1966088 | tf_op jit(solution)/shard_map/ppermute | solution.py:38
  32.8 18.4 %collective-permute-start.3 = (bf16[256,1280]{1,0:T(8,128)(2,1)S(1)}, bf16[256,1280]{1,0:T(8,128)(2,1)S(1)}, u32[]{:S(2)}, u32[]{:S(2)}) collective-permute-start(bf16[256,1280]{1,0:T(8,128)(2,1)S(1)} %copy-done.19), channel_id=1, source_target_pairs={{0,16},{1,17},{2,18},{3,19},{4,20},{5,21},{6,22},{7,23},{8,24},{9,... | collective-permute-start | bytes 1966088 | tf_op jit(solution)/shard_map/ppermute | solution.py:38
  34.3 29.9 %collective-permute-start.4 = (bf16[256,1280]{1,0:T(8,128)(2,1)S(1)}, bf16[256,1280]{1,0:T(8,128)(2,1)S(1)}, u32[]{:S(2)}, u32[]{:S(2)}) collective-permute-start(bf16[256,1280]{1,0:T(8,128)(2,1)S(1)} %copy-done.18), channel_id=1, source_target_pairs={{0,18},{1,19},{2,16},{3,17},{4,22},{5,23},{6,20},{7,21},{8,26},{9,... | collective-permute-start | bytes 1966088 | tf_op jit(solution)/shard_map/ppermute | solution.py:38
  35.8 32.6 %collective-permute-start.6 = (f32[16,256]{1,0:T(8,128)S(1)}, f32[16,256]{1,0:T(8,128)S(1)}, u32[]{:S(2)}, u32[]{:S(2)}) collective-permute-start(f32[16,256]{1,0:T(8,128)S(1)} %copy-done.24), channel_id=1, source_target_pairs={{0,2},{1,3},{2,0},{3,1},{4,6},{5,7},{6,4},{7,5},{8,10},{9,11},{10,... | collective-permute-start | bytes 49160 | tf_op jit(solution)/shard_map/ppermute | solution.py:38
  36.3 32.1 %collective-permute-start.7 = (f32[16,256]{1,0:T(8,128)S(1)}, f32[16,256]{1,0:T(8,128)S(1)}, u32[]{:S(2)}, u32[]{:S(2)}) collective-permute-start(f32[16,256]{1,0:T(8,128)S(1)} %copy-done.23), channel_id=1, source_target_pairs={{0,16},{1,17},{2,18},{3,19},{4,20},{5,21},{6,22},{7,23},{8,24},{9,... | collective-permute-start | bytes 49160 | tf_op jit(solution)/shard_map/ppermute | solution.py:38
  49.8 25.5 %copy-start.3 = (bf16[256,1280]{1,0:T(8,128)(2,1)}, bf16[256,1280]{1,0:T(8,128)(2,1)S(1)}, u32[]{:S(2)}) copy-start(bf16[256,1280]{1,0:T(8,128)(2,1)S(1)} %collective-permute-done.2.p1) | copy-start | bytes 1966084
  49.8 18.6 %collective-permute-start.8 = (f32[16,256]{1,0:T(8,128)S(1)}, f32[16,256]{1,0:T(8,128)S(1)}, u32[]{:S(2)}, u32[]{:S(2)}) collective-permute-start(f32[16,256]{1,0:T(8,128)S(1)} %copy-done.22), channel_id=1, source_target_pairs={{0,18},{1,19},{2,16},{3,17},{4,22},{5,23},{6,20},{7,21},{8,26},{9,... | collective-permute-start | bytes 49160 | tf_op jit(solution)/shard_map/ppermute | solution.py:38
  51.2 24.0 %copy-start.4 = (bf16[256,1280]{1,0:T(8,128)(2,1)}, bf16[256,1280]{1,0:T(8,128)(2,1)S(1)}, u32[]{:S(2)}) copy-start(bf16[256,1280]{1,0:T(8,128)(2,1)S(1)} %collective-permute-done.3.p2) | copy-start | bytes 1966084
  65.0 10.2 %collective-permute-start.5 = (bf16[2,16,1280]{2,1,0:T(8,128)(2,1)S(1)}, bf16[2,16,1280]{2,1,0:T(8,128)(2,1)S(1)}, u32[]{:S(2)}, u32[]{:S(2)}) collective-permute-start(bf16[2,16,1280]{2,1,0:T(8,128)(2,1)S(1)} %maximum_select_fusion.1), channel_id=1, source_target_pairs={{0,4},{1,5},{2,6},{3,7},{4,8},{5,9},{6,10},{7,11},{8,12},{9,13},{1... | collective-permute-start | bytes 245768 | tf_op jit(solution)/shard_map/ppermute | solution.py:38
  88.6 36.6 %collective-permute-start.9 = (bf16[2,144,1024]{2,1,0:T(8,128)(2,1)}, bf16[2,144,1024]{2,1,0:T(8,128)(2,1)S(1)}, u32[]{:S(2)}, u32[]{:S(2)}) collective-permute-start(bf16[2,144,1024]{2,1,0:T(8,128)(2,1)} %get-tuple-element.106.late), channel_id=1, source_target_pairs={{0,4},{1,5},{2,6},{3,7},{4,8},{5,9},{6,10},{7,11},{8,12},{9,13},{1... | collective-permute-start | bytes 1769480 | tf_op jit(solution)/shard_map/ppermute | solution.py:38
  90.6 39.7 %copy-start.21 = (bf16[256,1024]{1,0:T(8,128)(2,1)S(1)}, bf16[256,1024]{1,0:T(8,128)(2,1)}, u32[]{:S(2)}) copy-start(bf16[256,1024]{1,0:T(8,128)(2,1)} %get-tuple-element.117) | copy-start | bytes 1572868
  90.6 41.1 %copy-start.20 = (bf16[256,1024]{1,0:T(8,128)(2,1)S(1)}, bf16[256,1024]{1,0:T(8,128)(2,1)}, u32[]{:S(2)}) copy-start(bf16[256,1024]{1,0:T(8,128)(2,1)} %get-tuple-element.118) | copy-start | bytes 1572868
  128.2 30.5 %collective-permute-start.10 = (bf16[2,144,1024]{2,1,0:T(8,128)(2,1)}, bf16[2,144,1024]{2,1,0:T(8,128)(2,1)S(1)}, u32[]{:S(2)}, u32[]{:S(2)}) collective-permute-start(bf16[2,144,1024]{2,1,0:T(8,128)(2,1)} %join.1), channel_id=1, source_target_pairs={{0,8},{1,9},{2,10},{3,11},{4,12},{5,13},{6,14},{7,15},{16,24},{17,... | collective-permute-start | bytes 1769480 | tf_op jit(solution)/shard_map/ppermute | solution.py:38
  129.7 14.4 %collective-permute-start.11 = (bf16[256,1024]{1,0:T(8,128)(2,1)}, bf16[256,1024]{1,0:T(8,128)(2,1)S(1)}, u32[]{:S(2)}, u32[]{:S(2)}) collective-permute-start(bf16[256,1024]{1,0:T(8,128)(2,1)} %get-tuple-element.116), channel_id=1, source_target_pairs={{0,2},{1,3},{2,0},{3,1},{4,6},{5,7},{6,4},{7,5},{8,10},{9,11},{10,... | collective-permute-start | bytes 1572872 | tf_op jit(solution)/shard_map/ppermute | solution.py:38
  130.3 14.8 %collective-permute-start.12 = (bf16[256,1024]{1,0:T(8,128)(2,1)S(1)}, bf16[256,1024]{1,0:T(8,128)(2,1)S(1)}, u32[]{:S(2)}, u32[]{:S(2)}) collective-permute-start(bf16[256,1024]{1,0:T(8,128)(2,1)S(1)} %copy-done.21), channel_id=1, source_target_pairs={{0,16},{1,17},{2,18},{3,19},{4,20},{5,21},{6,22},{7,23},{8,24},{9,... | collective-permute-start | bytes 1572872 | tf_op jit(solution)/shard_map/ppermute | solution.py:38
  131.8 23.8 %collective-permute-start.13 = (bf16[256,1024]{1,0:T(8,128)(2,1)S(1)}, bf16[256,1024]{1,0:T(8,128)(2,1)S(1)}, u32[]{:S(2)}, u32[]{:S(2)}) collective-permute-start(bf16[256,1024]{1,0:T(8,128)(2,1)S(1)} %copy-done.20), channel_id=1, source_target_pairs={{0,18},{1,19},{2,16},{3,17},{4,22},{5,23},{6,20},{7,21},{8,26},{9,... | collective-permute-start | bytes 1572872 | tf_op jit(solution)/shard_map/ppermute | solution.py:38
  144.1 14.6 %copy-start.7 = (bf16[256,1024]{1,0:T(8,128)(2,1)}, bf16[256,1024]{1,0:T(8,128)(2,1)S(1)}, u32[]{:S(2)}) copy-start(bf16[256,1024]{1,0:T(8,128)(2,1)S(1)} %collective-permute-done.11.z1) | copy-start | bytes 1572868
  145.1 13.6 %copy-start.8 = (bf16[256,1024]{1,0:T(8,128)(2,1)}, bf16[256,1024]{1,0:T(8,128)(2,1)S(1)}, u32[]{:S(2)}) copy-start(bf16[256,1024]{1,0:T(8,128)(2,1)S(1)} %collective-permute-done.12.z2) | copy-start | bytes 1572868
  173.9 4.5 %collective-permute-start.14 = (bf16[1024,1024]{1,0:T(8,128)(2,1)}, bf16[1024,1024]{1,0:T(8,128)(2,1)}, u32[]{:S(2)}, u32[]{:S(2)}) collective-permute-start(bf16[1024,1024]{1,0:T(8,128)(2,1)} %fusion.8), channel_id=1, source_target_pairs={{0,1},{1,0},{2,3},{3,2},{4,5},{5,4},{6,7},{7,6},{8,9},{9,8},{10,11... | collective-permute-start | bytes 6291464 | tf_op jit(solution)/shard_map/ppermute | solution.py:38
  183.1 14.0 %collective-permute-start.15 = (bf16[256,1024]{1,0:T(8,128)(2,1)S(1)}, bf16[256,1024]{1,0:T(8,128)(2,1)S(1)}, u32[]{:S(2)}, u32[]{:S(2)}) collective-permute-start(bf16[256,1024]{1,0:T(8,128)(2,1)S(1)} %get-tuple-element.119), channel_id=1, source_target_pairs={{0,2},{1,3},{2,0},{3,1},{4,6},{5,7},{6,4},{7,5},{8,10},{9,11},{10,... | collective-permute-start | bytes 1572872 | tf_op jit(solution)/shard_map/ppermute | solution.py:38
  183.4 14.8 %collective-permute-start.16 = (bf16[256,1024]{1,0:T(8,128)(2,1)S(1)}, bf16[256,1024]{1,0:T(8,128)(2,1)S(1)}, u32[]{:S(2)}, u32[]{:S(2)}) collective-permute-start(bf16[256,1024]{1,0:T(8,128)(2,1)S(1)} %get-tuple-element.121), channel_id=1, source_target_pairs={{0,16},{1,17},{2,18},{3,19},{4,20},{5,21},{6,22},{7,23},{8,24},{9,... | collective-permute-start | bytes 1572872 | tf_op jit(solution)/shard_map/ppermute | solution.py:38
  185.2 24.4 %collective-permute-start.17 = (bf16[256,1024]{1,0:T(8,128)(2,1)S(1)}, bf16[256,1024]{1,0:T(8,128)(2,1)S(1)}, u32[]{:S(2)}, u32[]{:S(2)}) collective-permute-start(bf16[256,1024]{1,0:T(8,128)(2,1)S(1)} %get-tuple-element.120), channel_id=1, source_target_pairs={{0,18},{1,19},{2,16},{3,17},{4,22},{5,23},{6,20},{7,21},{8,26},{9,... | collective-permute-start | bytes 1572872 | tf_op jit(solution)/shard_map/ppermute | solution.py:38
  (12 other events, 68.2 us)
Sparse Core Ops, SparseCore 0:
  32.4 91.3 all-gather.1

commit v3 on v2

--- a/solution.py
+++ b/solution.py
@@ -472,7 +472,7 @@
     )
     near = onward(pair, 1)
     y = within(place, xc, bc, low, cum, jnp.repeat(d_skip, HEADDIM)[None])
-    near, y = after(near, y)
+    near, (y, zs) = after(near, (y, zs))
     span = join(pair, near)
     distance = 2
     far = onward(span, distance)
@@ -484,17 +484,16 @@
         place, y, bc, kept, near, far, first, fade, z_in, zs, gain[None], sign_bits[None]
     )
 
-    act = act.reshape(4 * rows, GROUP)
     half = weight.shape[1] // 2
     theirs = lax.dynamic_slice_in_dim(weight, (1 - t_here) * half, half, 1)
     ours = lax.dynamic_slice_in_dim(weight, t_here * half, half, 1)
-    away = jnp.dot(act, theirs, preferred_element_type=F32).astype(BF16)
-    back = send(away, lambda x, z, y, t: (x, z, y, 1 - t))
-    stay = jnp.dot(act, ours, preferred_element_type=F32) + back.astype(F32)
-    stay = stay.reshape(4, rows, half)
-    total = stay[0]
-    for k in range(1, 4):
-        total = total + swap(stay[k].astype(BF16), k).astype(F32)
+    parts = []
+    for k in (3, 2, 1, 0):
+        away = jnp.dot(act[k], theirs, preferred_element_type=F32).astype(BF16)
+        back = send(away, lambda x, z, y, t: (x, z, y, 1 - t))
+        stay = jnp.dot(act[k], ours, preferred_element_type=F32) + back.astype(F32)
+        parts.append(swap(stay.astype(BF16), k).astype(F32) if k else stay)
+    total = parts[3] + parts[2] + parts[1] + parts[0]
     return total.astype(BF16)
 
 

time: 220 us -> 213 us (0.968)
  waiting for transfers between devices: 122 us -> 117 us
    ppermute x18 -> x21, waiting for transfers between devices: 122 us -> 117 us  [send(): return lax.ppermute(array, AXES, pairs)]
    ppermute x18 -> x21, starting transfers between devices: 18.7 us -> 20.1 us  [send(): return lax.ppermute(array, AXES, pairs)]
    dot_general x2 -> x8, matrix products: 10.6 us -> 10.3 us  [the longest x4 6.38 us: per_device(): away = jnp.dot(act[k], theirs, preferred_element_type=F32).astype(BF16)]
  transfers between devices with their start and end apart: 19 -> 22, of which waited for: 13 -> 12; matrix products, arithmetic and copies ran while one was open for 2% -> 5% of each run, Pallas kernels for 17% -> 18%
where the time goes in v3:
time: 213 us; the launch traced here: 212 us
  waiting for transfers between devices  117 us (55%)
  Pallas kernels  42 us (20%)
  starting transfers between devices  20.1 us (9%)
  between operations  13.7 us (6%)
  matrix products  10.3 us (5%)
  local copies, waits for them, and re-layouts  6.16 us (3%)
  other arithmetic  2.93 us (1%)
    ppermute x21, waiting for transfers between devices, send(): return lax.ppermute(array, AXES, pairs)  117 us
    ppermute x21, starting transfers between devices, send(): return lax.ppermute(array, AXES, pairs)  20.1 us
    pallas_call x1, Pallas kernels, conv_states(): pl.pallas_call(conv_kernel, grid_spec=pltpu.PrefetchScalarGridSpec(num_sc...  12.7 us
    pallas_call x1, Pallas kernels, gate_norm(): pl.pallas_call(gate_kernel, grid_spec=pltpu.PrefetchScalarGridSpec(num_sc...  8.23 us
    pallas_call x1, Pallas kernels, within(): pl.pallas_call(within_kernel, grid_spec=pltpu.PrefetchScalarGridSpec(num_...  7.4 us
    dot_general x4, matrix products, per_device(): away = jnp.dot(act[k], theirs, preferred_element_type=F32).astype(BF16)  6.38 us
  transfers between devices with their start and end apart: 22, of which 12 were waited for; matrix products, arithmetic and copies ran while one was open for 5% of the time, Pallas kernels for 18%

profile of v3, /device:TPU:28, one launch (start us, length us, event | category | flops | bytes accessed | tf_op | source)
XLA Modules:
  0.0 212.1 jit_solution(6116481941889949215)
XLA Ops:
  6.5 4.0 %turn.1 = bf16[8,256,256]{2,1,0:T(8,128)(2,1)} custom-call(s32[1]{0:T(128)} %bitcast.5.sign, bf16[4096,256]{1,0:T(8,128)(2,1)} %w.1), custom_call_target="tpu_custom_call" | custom-call | tf_op jit(solution)/shard_map/turn/pallas_call | solution.py:175
  12.0 4.1 %pack.1 = (bf16[256,1280]{1,0:T(8,128)(2,1)}, bf16[256,1280]{1,0:T(8,128)(2,1)}, bf16[256,1280]{1,0:T(8,128)(2,1)}, bf16[256,1280]{1,0:T(8,128)(2,1)}, f32[16,25...) custom-call(s32[4]{0:T(128)} %pad_add_fusion.1.order, bf16[256,4096]{1,0:T(8,128)(2,1)} %x3, ...), custom_call_target="tpu_custom_call" | custom-call | tf_op jit(solution)/shard_map/pack/pallas_call | solution.py:92
  17.2 3.2 %cut.1 = (bf16[256,1024]{1,0:T(8,128)(2,1)}, bf16[256,1024]{1,0:T(8,128)(2,1)}, bf16[256,1024]{1,0:T(8,128)(2,1)}) custom-call(s32[4]{0:T(128)} %pad_add_fusion.1.order, bf16[256,4096]{1,0:T(8,128)(2,1)} %z0, bf16[256,4096]{1,0:T(8,128)(2,1)} %z0, bf16[256,4096]{1,0:T(8,128)(2,1)} %z0), custom_call_target="tpu_custom_call" | custom-call | tf_op jit(solution)/shard_map/cut/pallas_call | solution.py:122
  20.5 10.6 %collective-permute-done.1 = bf16[1024,256]{1,0:T(8,128)(2,1)S(1)} collective-permute-done((bf16[1024,256]{1,0:T(8,128)(2,1)S(1)}, bf16[1024,256]{1,0:T(8,128)(2,1)S(1)}, u32[]{:S(2)}, u32[]{:S(2)}) %collective-permute-start.1) | collective-permute-done | bytes 524320 | tf_op jit(solution)/shard_map/ppermute | solution.py:38
  32.9 1.5 collective-permute-start.3
  34.4 1.5 collective-permute-start.4
  36.4 1.5 collective-permute-start.7
  37.9 12.0 %collective-permute-done.2.p1 = bf16[256,1280]{1,0:T(8,128)(2,1)S(1)} collective-permute-done((bf16[256,1280]{1,0:T(8,128)(2,1)}, bf16[256,1280]{1,0:T(8,128)(2,1)S(1)}, u32[]{:S(2)}, u32[]{:S(2)}) %collective-permute-start.2) | collective-permute-done | bytes 655392 | tf_op jit(solution)/shard_map/ppermute | solution.py:38
  49.8 1.4 collective-permute-start.8
  51.3 13.0 %collective-permute-done.4.p3 = bf16[256,1280]{1,0:T(8,128)(2,1)S(1)} collective-permute-done((bf16[256,1280]{1,0:T(8,128)(2,1)S(1)}, bf16[256,1280]{1,0:T(8,128)(2,1)S(1)}, u32[]{:S(2)}, u32[]{:S(2)}) %collective-permute-start.4) | collective-permute-done | bytes 655392 | tf_op jit(solution)/shard_map/ppermute | solution.py:38
  65.1 1.3 collective-permute-start.5
  68.5 6.8 %collective-permute-done.5.halo = bf16[2,16,1280]{2,1,0:T(8,128)(2,1)S(1)} collective-permute-done((bf16[2,16,1280]{2,1,0:T(8,128)(2,1)S(1)}, bf16[2,16,1280]{2,1,0:T(8,128)(2,1)S(1)}, u32[]{:S(2)}, u32[]{:S(2)}) %collective-permute-start.5) | collective-permute-done | bytes 81952 | tf_op jit(solution)/shard_map/ppermute | solution.py:38
  76.0 12.7 %conv_states.1 = (bf16[4,256,1024]{2,1,0:T(8,128)(2,1)}, bf16[4,256,256]{2,1,0:T(8,128)(2,1)}, f32[4,16,256]{2,1,0:T(8,128)}, f32[4,256,16]{2,1,0:T(8,128)}, bf1...) custom-call(s32[2]{0:T(128)} %pad_add_fusion.place, ...), custom_call_target="tpu_custom_call" | custom-call | tf_op jit(solution)/shard_map/conv_states/pallas_call | solution.py:274
  90.5 1.6 collective-permute-start.11
  92.0 1.5 collective-permute-start.12
  94.3 7.4 %within.1.y = f32[4,256,1024]{2,1,0:T(8,128)} custom-call(s32[2]{0:T(128)} %pad_add_fusion.place, bf16[4,256,1024]{2,1,0:T(8,128)(2,1)} %get-tuple-element.110.xc, bf16[4,256,256]{2,1,0:T(8,128)(2,1)} %get-tuple-element.111.bc, f32[4,16,256]{2,1,0:T(8,128)} %get-tuple-element.112.low, f32[4,256,16]{2,1,0:T(8,128)} %get-tuple-element.113.cum, ...), custom_call_target="tpu_custom_call" | custom-call | tf_op jit(solution)/shard_map/within/pallas_call | solution.py:357
  101.7 2.4 %collective-permute-done.10.z1 = bf16[256,1024]{1,0:T(8,128)(2,1)S(1)} collective-permute-done((bf16[256,1024]{1,0:T(8,128)(2,1)}, bf16[256,1024]{1,0:T(8,128)(2,1)S(1)}, u32[]{:S(2)}, u32[]{:S(2)}) %collective-permute-start.10) | collective-permute-done | bytes 524320 | tf_op jit(solution)/shard_map/ppermute | solution.py:38
  104.1 1.4 collective-permute-done.11.z2
  105.5 9.7 %collective-permute-done.12.z3 = bf16[256,1024]{1,0:T(8,128)(2,1)S(1)} collective-permute-done((bf16[256,1024]{1,0:T(8,128)(2,1)S(1)}, bf16[256,1024]{1,0:T(8,128)(2,1)S(1)}, u32[]{:S(2)}, u32[]{:S(2)}) %collective-permute-start.12) | collective-permute-done | bytes 524320 | tf_op jit(solution)/shard_map/ppermute | solution.py:38
  115.2 10.0 %collective-permute-done.9.early.near = bf16[2,144,1024]{2,1,0:T(8,128)(2,1)S(1)} collective-permute-done((bf16[2,144,1024]{2,1,0:T(8,128)(2,1)}, bf16[2,144,1024]{2,1,0:T(8,128)(2,1)S(1)}, u32[]{:S(2)}, u32[]{:S(2)}) %collective-permute-start.9) | collective-permute-done | bytes 589856 | tf_op jit(solution)/shard_map/ppermute | solution.py:38
  126.0 2.3 %join.1 = bf16[2,144,1024]{2,1,0:T(8,128)(2,1)} custom-call(bf16[2,144,1024]{2,1,0:T(8,128)(2,1)} %get-tuple-element.109.late, bf16[2,144,1024]{2,1,0:T(8,128)(2,1)} %copy-done.1), custom_call_target="tpu_custom_call" | custom-call | tf_op jit(solution)/shard_map/join/pallas_call | solution.py:309
  128.3 1.5 collective-permute-start.13
  129.8 29.0 %collective-permute-done.13.far = bf16[2,144,1024]{2,1,0:T(8,128)(2,1)S(1)} collective-permute-done((bf16[2,144,1024]{2,1,0:T(8,128)(2,1)}, bf16[2,144,1024]{2,1,0:T(8,128)(2,1)S(1)}, u32[]{:S(2)}, u32[]{:S(2)}) %collective-permute-start.13) | collective-permute-done | bytes 589856 | tf_op jit(solution)/shard_map/ppermute | solution.py:38
  159.6 8.2 %gate_norm.1 = bf16[4,256,1024]{2,1,0:T(8,128)(2,1)} custom-call(s32[2]{0:T(128)} %pad_add_fusion.place, f32[4,256,1024]{2,1,0:T(8,128)} %within.1.y, bf16[4,256,256]{2,1,0:T(8,128)(2,1)} %get-tuple-element.111.bc, bf16[4,48,256]{2,1,0:T(8,128)(2,1)} %get-tuple-element.118.kept, bf16[2,144,1024]{2,1,0:T(8,128)(2,1)} %copy-done.1, ...), custom_call_target="tpu_custom_call" | custom-call | tf_op jit(solution)/shard_map/gate_norm/pallas_call | solution.py:403
  167.9 2.6 %fusion.23 = bf16[256,1024]{1,0:T(8,128)(2,1)S(1)} fusion(bf16[1024,2048]{1,0:T(8,128)(2,1)} %all-gather.2.cloned.1.call-done, s32[]{:T(128)S(6)} %select_n.46, bf16[4,256,1024]{2,1,0:T(8,128)(2,1)} %gate_norm.1), kind=kOutput, calls=%fused_computation.24 | convolution fusion | flops 537133056 | bytes 3145732 | tf_op jit(solution)/shard_map/dot_general | solution.py:492
  170.6 2.3 %fusion.26 = bf16[256,1024]{1,0:T(8,128)(2,1)S(1)} fusion(bf16[1024,2048]{1,0:T(8,128)(2,1)} %all-gather.2.cloned.1.call-done, s32[]{:T(128)S(6)} %select_n.46, bf16[4,256,1024]{2,1,0:T(8,128)(2,1)S(1)} %copy-done.2), kind=kOutput, calls=%fused_computation.25 | convolution fusion | flops 537133056 | bytes 3145732 | tf_op jit(solution)/shard_map/dot_general | solution.py:492
  177.4 1.8 collective-permute-start.18
  179.9 1.6 collective-permute-start.20
  181.5 8.7 %collective-permute-done.16 = bf16[256,1024]{1,0:T(8,128)(2,1)S(1)} collective-permute-done((bf16[256,1024]{1,0:T(8,128)(2,1)S(1)}, bf16[256,1024]{1,0:T(8,128)(2,1)S(1)}, u32[]{:S(2)}, u32[]{:S(2)}) %collective-permute-start.16) | collective-permute-done | bytes 524320 | tf_op jit(solution)/shard_map/ppermute | solution.py:38
  190.2 2.0 collective-permute-done.18
  192.3 11.2 %collective-permute-done.20 = bf16[256,1024]{1,0:T(8,128)(2,1)S(1)} collective-permute-done((bf16[256,1024]{1,0:T(8,128)(2,1)S(1)}, bf16[256,1024]{1,0:T(8,128)(2,1)S(1)}, u32[]{:S(2)}, u32[]{:S(2)}) %collective-permute-start.20) | collective-permute-done | bytes 524320 | tf_op jit(solution)/shard_map/ppermute | solution.py:38
  203.5 1.8 fusion.17
  (91 shorter events, 17.9 us)
Async XLA Ops:
  6.5 161.3 %all-gather.2.cloned.1.call-start = ((), (), s32[]{:S(2)}) async-start(), calls=%async_computation | async-start | bytes 5242880 | tf_op jit(solution)/shard_map/all_gather | solution.py:460
  10.6 5.6 %collective-permute-start = (bf16[2,1024,256]{2,1,0:T(8,128)(2,1)}, bf16[2,1024,256]{2,1,0:T(8,128)(2,1)S(1)}, u32[]{:S(2)}, u32[]{:S(2)}) collective-permute-start(bf16[2,1024,256]{2,1,0:T(8,128)(2,1)} %bitcast.39), channel_id=1, source_target_pairs={{0,1},{1,0},{2,3},{3,2},{4,5},{5,4},{6,7},{7,6},{8,9},{9,8},{10,11... | collective-permute-start | bytes 3145736 | tf_op jit(solution)/shard_map/ppermute | solution.py:38
  16.6 14.4 %collective-permute-start.1 = (bf16[1024,256]{1,0:T(8,128)(2,1)S(1)}, bf16[1024,256]{1,0:T(8,128)(2,1)S(1)}, u32[]{:S(2)}, u32[]{:S(2)}) collective-permute-start(bf16[1024,256]{1,0:T(8,128)(2,1)S(1)} %get-tuple-element.126), channel_id=1, source_target_pairs={{0,2},{1,3},{2,0},{3,1},{4,6},{5,7},{6,4},{7,5},{8,10},{9,11},{10,... | collective-permute-start | bytes 1572872 | tf_op jit(solution)/shard_map/ppermute | solution.py:38
  20.5 29.4 %copy-start.22 = (f32[16,256]{1,0:T(8,128)S(1)}, f32[16,256]{1,0:T(8,128)}, u32[]{:S(2)}) copy-start(f32[16,256]{1,0:T(8,128)} %get-tuple-element.92) | copy-start | bytes 49156
  20.5 46.6 %copy-start.15 = (f32[64]{0:T(128)S(1)}, f32[64]{0:T(128)}, u32[]{:S(2)}) copy-start(f32[64]{0:T(128)} %param.18) | copy-start | bytes 772
  20.5 47.3 %copy-start.16 = (f32[64]{0:T(128)S(1)}, f32[64]{0:T(128)}, u32[]{:S(2)}) copy-start(f32[64]{0:T(128)} %param.19) | copy-start | bytes 772
  32.3 61.2 %copy-start.17 = (f32[64]{0:T(128)S(1)}, f32[64]{0:T(128)}, u32[]{:S(2)}) copy-start(f32[64]{0:T(128)} %param.20) | copy-start | bytes 772
  32.3 17.5 %collective-permute-start.2 = (bf16[256,1280]{1,0:T(8,128)(2,1)}, bf16[256,1280]{1,0:T(8,128)(2,1)S(1)}, u32[]{:S(2)}, u32[]{:S(2)}) collective-permute-start(bf16[256,1280]{1,0:T(8,128)(2,1)} %get-tuple-element.86), channel_id=1, source_target_pairs={{0,2},{1,3},{2,0},{3,1},{4,6},{5,7},{6,4},{7,5},{8,10},{9,11},{10,... | collective-permute-start | bytes 1966088 | tf_op jit(solution)/shard_map/ppermute | solution.py:38
  32.9 18.4 %collective-permute-start.3 = (bf16[256,1280]{1,0:T(8,128)(2,1)S(1)}, bf16[256,1280]{1,0:T(8,128)(2,1)S(1)}, u32[]{:S(2)}, u32[]{:S(2)}) collective-permute-start(bf16[256,1280]{1,0:T(8,128)(2,1)S(1)} %copy-done.20), channel_id=1, source_target_pairs={{0,16},{1,17},{2,18},{3,19},{4,20},{5,21},{6,22},{7,23},{8,24},{9,... | collective-permute-start | bytes 1966088 | tf_op jit(solution)/shard_map/ppermute | solution.py:38
  34.4 29.9 %collective-permute-start.4 = (bf16[256,1280]{1,0:T(8,128)(2,1)S(1)}, bf16[256,1280]{1,0:T(8,128)(2,1)S(1)}, u32[]{:S(2)}, u32[]{:S(2)}) collective-permute-start(bf16[256,1280]{1,0:T(8,128)(2,1)S(1)} %copy-done.19), channel_id=1, source_target_pairs={{0,18},{1,19},{2,16},{3,17},{4,22},{5,23},{6,20},{7,21},{8,26},{9,... | collective-permute-start | bytes 1966088 | tf_op jit(solution)/shard_map/ppermute | solution.py:38
  35.9 32.6 %collective-permute-start.6 = (f32[16,256]{1,0:T(8,128)S(1)}, f32[16,256]{1,0:T(8,128)S(1)}, u32[]{:S(2)}, u32[]{:S(2)}) collective-permute-start(f32[16,256]{1,0:T(8,128)S(1)} %copy-done.24), channel_id=1, source_target_pairs={{0,2},{1,3},{2,0},{3,1},{4,6},{5,7},{6,4},{7,5},{8,10},{9,11},{10,... | collective-permute-start | bytes 49160 | tf_op jit(solution)/shard_map/ppermute | solution.py:38
  36.4 32.1 %collective-permute-start.7 = (f32[16,256]{1,0:T(8,128)S(1)}, f32[16,256]{1,0:T(8,128)S(1)}, u32[]{:S(2)}, u32[]{:S(2)}) collective-permute-start(f32[16,256]{1,0:T(8,128)S(1)} %copy-done.23), channel_id=1, source_target_pairs={{0,16},{1,17},{2,18},{3,19},{4,20},{5,21},{6,22},{7,23},{8,24},{9,... | collective-permute-start | bytes 49160 | tf_op jit(solution)/shard_map/ppermute | solution.py:38
  49.8 25.5 %copy-start.3 = (bf16[256,1280]{1,0:T(8,128)(2,1)}, bf16[256,1280]{1,0:T(8,128)(2,1)S(1)}, u32[]{:S(2)}) copy-start(bf16[256,1280]{1,0:T(8,128)(2,1)S(1)} %collective-permute-done.2.p1) | copy-start | bytes 1966084
  49.8 18.6 %collective-permute-start.8 = (f32[16,256]{1,0:T(8,128)S(1)}, f32[16,256]{1,0:T(8,128)S(1)}, u32[]{:S(2)}, u32[]{:S(2)}) collective-permute-start(f32[16,256]{1,0:T(8,128)S(1)} %copy-done.22), channel_id=1, source_target_pairs={{0,18},{1,19},{2,16},{3,17},{4,22},{5,23},{6,20},{7,21},{8,26},{9,... | collective-permute-start | bytes 49160 | tf_op jit(solution)/shard_map/ppermute | solution.py:38
  51.3 24.0 %copy-start.4 = (bf16[256,1280]{1,0:T(8,128)(2,1)}, bf16[256,1280]{1,0:T(8,128)(2,1)S(1)}, u32[]{:S(2)}) copy-start(bf16[256,1280]{1,0:T(8,128)(2,1)S(1)} %collective-permute-done.3.p2) | copy-start | bytes 1966084
  51.3 40.7 %copy-start.21 = (bf16[256,1024]{1,0:T(8,128)(2,1)S(1)}, bf16[256,1024]{1,0:T(8,128)(2,1)}, u32[]{:S(2)}) copy-start(bf16[256,1024]{1,0:T(8,128)(2,1)} %get-tuple-element.116) | copy-start | bytes 1572868
  65.1 10.2 %collective-permute-start.5 = (bf16[2,16,1280]{2,1,0:T(8,128)(2,1)S(1)}, bf16[2,16,1280]{2,1,0:T(8,128)(2,1)S(1)}, u32[]{:S(2)}, u32[]{:S(2)}) collective-permute-start(bf16[2,16,1280]{2,1,0:T(8,128)(2,1)S(1)} %maximum_select_fusion.1), channel_id=1, source_target_pairs={{0,4},{1,5},{2,6},{3,7},{4,8},{5,9},{6,10},{7,11},{8,12},{9,13},{1... | collective-permute-start | bytes 245768 | tf_op jit(solution)/shard_map/ppermute | solution.py:38
  88.7 36.6 %collective-permute-start.9 = (bf16[2,144,1024]{2,1,0:T(8,128)(2,1)}, bf16[2,144,1024]{2,1,0:T(8,128)(2,1)S(1)}, u32[]{:S(2)}, u32[]{:S(2)}) collective-permute-start(bf16[2,144,1024]{2,1,0:T(8,128)(2,1)} %get-tuple-element.109.late), channel_id=1, source_target_pairs={{0,4},{1,5},{2,6},{3,7},{4,8},{5,9},{6,10},{7,11},{8,12},{9,13},{1... | collective-permute-start | bytes 1769480 | tf_op jit(solution)/shard_map/ppermute | solution.py:38
  89.9 14.2 %collective-permute-start.10 = (bf16[256,1024]{1,0:T(8,128)(2,1)}, bf16[256,1024]{1,0:T(8,128)(2,1)S(1)}, u32[]{:S(2)}, u32[]{:S(2)}) collective-permute-start(bf16[256,1024]{1,0:T(8,128)(2,1)} %get-tuple-element.114), channel_id=1, source_target_pairs={{0,2},{1,3},{2,0},{3,1},{4,6},{5,7},{6,4},{7,5},{8,10},{9,11},{10,... | collective-permute-start | bytes 1572872 | tf_op jit(solution)/shard_map/ppermute | solution.py:38
  90.5 15.0 %collective-permute-start.11 = (bf16[256,1024]{1,0:T(8,128)(2,1)}, bf16[256,1024]{1,0:T(8,128)(2,1)S(1)}, u32[]{:S(2)}, u32[]{:S(2)}) collective-permute-start(bf16[256,1024]{1,0:T(8,128)(2,1)} %get-tuple-element.115), channel_id=1, source_target_pairs={{0,16},{1,17},{2,18},{3,19},{4,20},{5,21},{6,22},{7,23},{8,24},{9,... | collective-permute-start | bytes 1572872 | tf_op jit(solution)/shard_map/ppermute | solution.py:38
  92.0 23.1 %collective-permute-start.12 = (bf16[256,1024]{1,0:T(8,128)(2,1)S(1)}, bf16[256,1024]{1,0:T(8,128)(2,1)S(1)}, u32[]{:S(2)}, u32[]{:S(2)}) collective-permute-start(bf16[256,1024]{1,0:T(8,128)(2,1)S(1)} %copy-done.21), channel_id=1, source_target_pairs={{0,18},{1,19},{2,16},{3,17},{4,22},{5,23},{6,20},{7,21},{8,26},{9,... | collective-permute-start | bytes 1572872 | tf_op jit(solution)/shard_map/ppermute | solution.py:38
  104.1 54.7 %copy-start.7 = (bf16[256,1024]{1,0:T(8,128)(2,1)}, bf16[256,1024]{1,0:T(8,128)(2,1)S(1)}, u32[]{:S(2)}) copy-start(bf16[256,1024]{1,0:T(8,128)(2,1)S(1)} %collective-permute-done.10.z1) | copy-start | bytes 1572868
  105.5 53.3 %copy-start.8 = (bf16[256,1024]{1,0:T(8,128)(2,1)}, bf16[256,1024]{1,0:T(8,128)(2,1)S(1)}, u32[]{:S(2)}) copy-start(bf16[256,1024]{1,0:T(8,128)(2,1)S(1)} %collective-permute-done.11.z2) | copy-start | bytes 1572868
  115.2 43.6 %copy-start.9 = (bf16[256,1024]{1,0:T(8,128)(2,1)}, bf16[256,1024]{1,0:T(8,128)(2,1)S(1)}, u32[]{:S(2)}) copy-start(bf16[256,1024]{1,0:T(8,128)(2,1)S(1)} %collective-permute-done.12.z3) | copy-start | bytes 1572868
  128.3 30.5 %collective-permute-start.13 = (bf16[2,144,1024]{2,1,0:T(8,128)(2,1)}, bf16[2,144,1024]{2,1,0:T(8,128)(2,1)S(1)}, u32[]{:S(2)}, u32[]{:S(2)}) collective-permute-start(bf16[2,144,1024]{2,1,0:T(8,128)(2,1)} %join.1), channel_id=1, source_target_pairs={{0,8},{1,9},{2,10},{3,11},{4,12},{5,13},{6,14},{7,15},{16,24},{17,... | collective-permute-start | bytes 1769480 | tf_op jit(solution)/shard_map/ppermute | solution.py:38
  170.5 5.1 %collective-permute-start.15 = (bf16[256,1024]{1,0:T(8,128)(2,1)S(1)}, bf16[256,1024]{1,0:T(8,128)(2,1)S(1)}, u32[]{:S(2)}, u32[]{:S(2)}) collective-permute-start(bf16[256,1024]{1,0:T(8,128)(2,1)S(1)} %fusion.23), channel_id=1, source_target_pairs={{0,1},{1,0},{2,3},{3,2},{4,5},{5,4},{6,7},{7,6},{8,9},{9,8},{10,11... | collective-permute-start | bytes 1572872 | tf_op jit(solution)/shard_map/ppermute | solution.py:38
  172.9 3.8 %collective-permute-start.17 = (bf16[256,1024]{1,0:T(8,128)(2,1)S(1)}, bf16[256,1024]{1,0:T(8,128)(2,1)S(1)}, u32[]{:S(2)}, u32[]{:S(2)}) collective-permute-start(bf16[256,1024]{1,0:T(8,128)(2,1)S(1)} %fusion.26), channel_id=1, source_target_pairs={{0,1},{1,0},{2,3},{3,2},{4,5},{5,4},{6,7},{7,6},{8,9},{9,8},{10,11... | collective-permute-start | bytes 1572872 | tf_op jit(solution)/shard_map/ppermute | solution.py:38
  174.2 7.3 %collective-permute-start.14 = (bf16[256,1024]{1,0:T(8,128)(2,1)S(1)}, bf16[256,1024]{1,0:T(8,128)(2,1)S(1)}, u32[]{:S(2)}, u32[]{:S(2)}) collective-permute-start(bf16[256,1024]{1,0:T(8,128)(2,1)S(1)} %fusion.20), channel_id=1, source_target_pairs={{0,1},{1,0},{2,3},{3,2},{4,5},{5,4},{6,7},{7,6},{8,9},{9,8},{10,11... | collective-permute-start | bytes 1572872 | tf_op jit(solution)/shard_map/ppermute | solution.py:38
  175.0 4.2 %collective-permute-start.19 = (bf16[256,1024]{1,0:T(8,128)(2,1)S(1)}, bf16[256,1024]{1,0:T(8,128)(2,1)S(1)}, u32[]{:S(2)}, u32[]{:S(2)}) collective-permute-start(bf16[256,1024]{1,0:T(8,128)(2,1)S(1)} %fusion.29), channel_id=1, source_target_pairs={{0,1},{1,0},{2,3},{3,2},{4,5},{5,4},{6,7},{7,6},{8,9},{9,8},{10,11... | collective-permute-start | bytes 1572872 | tf_op jit(solution)/shard_map/ppermute | solution.py:38
  176.3 13.9 %collective-permute-start.16 = (bf16[256,1024]{1,0:T(8,128)(2,1)S(1)}, bf16[256,1024]{1,0:T(8,128)(2,1)S(1)}, u32[]{:S(2)}, u32[]{:S(2)}) collective-permute-start(bf16[256,1024]{1,0:T(8,128)(2,1)S(1)} %fusion.32), channel_id=1, source_target_pairs={{0,2},{1,3},{2,0},{3,1},{4,6},{5,7},{6,4},{7,5},{8,10},{9,11},{10,... | collective-permute-start | bytes 1572872 | tf_op jit(solution)/shard_map/ppermute | solution.py:38
  177.4 14.9 %collective-permute-start.18 = (bf16[256,1024]{1,0:T(8,128)(2,1)S(1)}, bf16[256,1024]{1,0:T(8,128)(2,1)S(1)}, u32[]{:S(2)}, u32[]{:S(2)}) collective-permute-start(bf16[256,1024]{1,0:T(8,128)(2,1)S(1)} %fusion.35), channel_id=1, source_target_pairs={{0,16},{1,17},{2,18},{3,19},{4,20},{5,21},{6,22},{7,23},{8,24},{9,... | collective-permute-start | bytes 1572872 | tf_op jit(solution)/shard_map/ppermute | solution.py:38
  179.9 23.5 %collective-permute-start.20 = (bf16[256,1024]{1,0:T(8,128)(2,1)S(1)}, bf16[256,1024]{1,0:T(8,128)(2,1)S(1)}, u32[]{:S(2)}, u32[]{:S(2)}) collective-permute-start(bf16[256,1024]{1,0:T(8,128)(2,1)S(1)} %fusion.38), channel_id=1, source_target_pairs={{0,18},{1,19},{2,16},{3,17},{4,22},{5,23},{6,20},{7,21},{8,26},{9,... | collective-permute-start | bytes 1572872 | tf_op jit(solution)/shard_map/ppermute | solution.py:38
  (15 other events, 108.3 us)
Sparse Core Ops, SparseCore 0:
  32.4 91.3 all-gather.1

commit v4 on v3

--- a/solution.py
+++ b/solution.py
@@ -73,16 +73,18 @@
     return half + half * jnp.tanh(half)
 
 
-def pack_kernel(order, x0, x1, x2, x3, b0, b1, b2, b3, dt, o0, o1, o2, o3, d0, d1, d2, d3, turned):
+def pack_kernel(order, x0, x1, x2, x3, b0, b1, b2, b3, dt, o0, o1, o2, o3, d0, d1, d2, d3, e0, e1, e2, e3, turned):
     turned[...] = dt[...].T
-    for k, (x, b, o, d) in enumerate(
-        ((x0, b0, o0, d0), (x1, b1, o1, d1), (x2, b2, o2, d2), (x3, b3, o3, d3))
+    rows = x0.shape[0]
+    for k, (x, b, o, d, e) in enumerate(
+        ((x0, b0, o0, d0, e0), (x1, b1, o1, d1, e1), (x2, b2, o2, d2, e2), (x3, b3, o3, d3, e3))
     ):
         o[:, :GROUP] = x[...]
         o[:, GROUP : GROUP + STATE] = b[0]
         o[:, GROUP + STATE :] = b[1]
         first = pl.multiple_of(order[k] * PER, PER)
         d[...] = turned[pl.ds(first, PER), :]
+        e[...] = o[rows - 16 :, :]
 
 
 def pack(order, x_in, bc_in, dt_raw):
@@ -102,11 +104,12 @@
                 for k in range(4)
             ]
             + [whole(rows, dt_raw.shape[1])],
-            out_specs=[whole(rows, wide)] * 4 + [whole(PER, rows)] * 4,
+            out_specs=[whole(rows, wide)] * 4 + [whole(PER, rows)] * 4 + [whole(16, wide)] * 4,
             scratch_shapes=[pltpu.VMEM((dt_raw.shape[1], rows), F32)],
         ),
         out_shape=[jax.ShapeDtypeStruct((rows, wide), BF16)] * 4
-        + [jax.ShapeDtypeStruct((PER, rows), F32)] * 4,
+        + [jax.ShapeDtypeStruct((PER, rows), F32)] * 4
+        + [jax.ShapeDtypeStruct((16, wide), BF16)] * 4,
         name="pack",
     )(order, x_in, x_in, x_in, x_in, bc_in, bc_in, bc_in, bc_in, dt_raw)
 
@@ -435,23 +438,32 @@
     order = jnp.stack([mine ^ k for k in range(4)]).astype(jnp.int32)
     place = jnp.stack([mine, y_here]).astype(jnp.int32)
 
+    packed = pack(order, x_in, bc_in, dt_raw)
+    out_weight, packed = after(out_weight, packed)
+    second = swap(packed[1], 1)
+    tails = [
+        send(
+            packed[8 + k],
+            lambda x, z, y, t, k=k: (x ^ (k >> 1), z + 1, y ^ (k & 1), t) if y == 1 else None,
+        )
+        for k in range(4)
+    ]
+
     turned = turn(x_here.reshape(1).astype(jnp.int32), out_weight)
     turned = turned.reshape(2, GROUP, out_weight.shape[1])
     across = send(turned, lambda x, z, y, t: (x, z, y, 1 - t))
-
-    x_in, turned = after(x_in, turned)
-    packed = pack(order, x_in, bc_in, dt_raw)
-    packed, across = after(packed, across)
     own = turned.astype(F32)
     rotated = (across.astype(F32) + jnp.where(t_here == 0, own, -own)).astype(BF16)
-    packed, rotated = after(packed, rotated)
+    rotated, (second, tails) = after(rotated, (second, tails))
     keep = lax.dynamic_index_in_dim(rotated, y_here, 0, keepdims=False)
     given = swap(lax.dynamic_index_in_dim(rotated, 1 - y_here, 0, keepdims=False), 1)
-    pieces = [packed[0]] + [swap(packed[k], k) for k in range(1, 4)]
-    steps = [packed[4]] + [swap(packed[4 + k], k) for k in range(1, 4)]
     z_in, packed = after(z_in, packed)
     slices = cut(order, z_in)
-    given, slices = after(given, slices)
+    third = swap(packed[2], 2)
+    steps = [packed[4]] + [swap(packed[4 + k], k) for k in range(1, 4)]
+    given, (slices, third, steps, fourth) = after(given, (slices, third, steps, packed[3]))
+    pieces = [packed[0], second, third, swap(fourth, 3)]
+    halo = jnp.stack([tails[0] + tails[1], tails[2] + tails[3]])
     columns = jnp.where(
         y_here == 0,
         jnp.concatenate([keep, given], axis=1),
@@ -459,11 +471,6 @@
     )
     weight = lax.all_gather(columns, "sz", axis=1, tiled=True)
     pieces, columns = after(pieces, columns)
-    tails = [p[rows - 16 :] for p in pieces]
-    closing = jnp.where(
-        y_here == 1, jnp.stack([tails[0], tails[2]]), jnp.stack([tails[1], tails[3]])
-    )
-    halo = onward(closing, 1)
     slices, pieces = after(slices, pieces)
     zs = [swap(z, k + 1) for k, z in enumerate(slices)]
 

time: 213 us -> 221 us (1.038)
  starting transfers between devices: 20.1 us -> 25.6 us
    ppermute x21 -> x24, starting transfers between devices: 20.1 us -> 25.6 us  [send(): return lax.ppermute(array, AXES, pairs)]
    ppermute x21 -> x24, waiting for transfers between devices: 117 us -> 118 us  [send(): return lax.ppermute(array, AXES, pairs)]
  transfers between devices with their start and end apart: 22 -> 25, of which waited for: 12 -> 13; matrix products, arithmetic and copies ran while one was open for 5% -> 5% of each run, Pallas kernels for 18% -> 15%
where the time goes in v4:
time: 221 us; the launch traced here: 220 us
  waiting for transfers between devices  118 us (53%)
  Pallas kernels  41.9 us (19%)
  starting transfers between devices  25.6 us (12%)
  between operations  13.8 us (6%)
  matrix products  10.3 us (5%)
  local copies, waits for them, and re-layouts  6.35 us (3%)
  other arithmetic  4.67 us (2%)
    ppermute x24, waiting for transfers between devices, send(): return lax.ppermute(array, AXES, pairs)  118 us
    ppermute x24, starting transfers between devices, send(): return lax.ppermute(array, AXES, pairs)  25.6 us
    pallas_call x1, Pallas kernels, conv_states(): pl.pallas_call(conv_kernel, grid_spec=pltpu.PrefetchScalarGridSpec(num_sc...  12.7 us
    pallas_call x1, Pallas kernels, gate_norm(): pl.pallas_call(gate_kernel, grid_spec=pltpu.PrefetchScalarGridSpec(num_sc...  8.25 us
    pallas_call x1, Pallas kernels, within(): pl.pallas_call(within_kernel, grid_spec=pltpu.PrefetchScalarGridSpec(num_...  7.4 us
    dot_general x4, matrix products, per_device(): away = jnp.dot(act[k], theirs, preferred_element_type=F32).astype(BF16)  6.38 us
  transfers between devices with their start and end apart: 25, of which 13 were waited for; matrix products, arithmetic and copies ran while one was open for 5% of the time, Pallas kernels for 15%

profile of v4, /device:TPU:28, one launch (start us, length us, event | category | flops | bytes accessed | tf_op | source)
XLA Modules:
  0.0 220.3 jit_solution(5466589813217121799)
XLA Ops:
  6.5 1.6 copy.13.dt
  8.7 4.0 %pack.1 = (bf16[256,1280]{1,0:T(8,128)(2,1)}, bf16[256,1280]{1,0:T(8,128)(2,1)}, bf16[256,1280]{1,0:T(8,128)(2,1)}, bf16[256,1280]{1,0:T(8,128)(2,1)}, f32[16,25...) custom-call(s32[4]{0:T(128)} %pad_add_fusion.1.order, ...), custom_call_target="tpu_custom_call" | custom-call | tf_op jit(solution)/shard_map/pack/pallas_call | solution.py:94
  12.8 4.1 %turn.1 = bf16[8,256,256]{2,1,0:T(8,128)(2,1)} custom-call(s32[1]{0:T(128)} %bitcast.2.sign, bf16[4096,256]{1,0:T(8,128)(2,1)} %w), custom_call_target="tpu_custom_call" | custom-call | tf_op jit(solution)/shard_map/turn/pallas_call | solution.py:178
  21.4 1.6 fusion.1
  23.3 1.5 collective-permute-start.7
  24.8 3.0 %collective-permute-done.4 = bf16[16,1280]{1,0:T(8,128)(2,1)S(1)} collective-permute-done((bf16[16,1280]{1,0:T(8,128)(2,1)S(1)}, bf16[16,1280]{1,0:T(8,128)(2,1)S(1)}, u32[]{:S(2)}, u32[]{:S(2)}) %collective-permute-start.4) | collective-permute-done | bytes 40992 | tf_op jit(solution)/shard_map/ppermute | solution.py:38
  27.8 6.2 %collective-permute-done.1.p1 = bf16[256,1280]{1,0:T(8,128)(2,1)S(1)} collective-permute-done((bf16[256,1280]{1,0:T(8,128)(2,1)S(1)}, bf16[256,1280]{1,0:T(8,128)(2,1)S(1)}, u32[]{:S(2)}, u32[]{:S(2)}) %collective-permute-start.1) | collective-permute-done | bytes 655392 | tf_op jit(solution)/shard_map/ppermute | solution.py:38
  34.1 2.3 %collective-permute-start.6 = (bf16[1024,256]{1,0:T(8,128)(2,1)S(1)}, bf16[1024,256]{1,0:T(8,128)(2,1)S(1)}, u32[]{:S(2)}, u32[]{:S(2)}) collective-permute-start(bf16[1024,256]{1,0:T(8,128)(2,1)S(1)} %get-tuple-element.158), channel_id=1, source_target_pairs={{0,2},{1,3},{2,0},{3,1},{4,6},{5,7},{6,4},{7,5},{8,10},{9,11},{10,... | collective-permute-start | bytes 1572872 | tf_op jit(solution)/shard_map/ppermute | solution.py:38
  37.5 1.9 collective-permute-start.8
  39.9 3.3 %cut.1 = (bf16[256,1024]{1,0:T(8,128)(2,1)}, bf16[256,1024]{1,0:T(8,128)(2,1)}, bf16[256,1024]{1,0:T(8,128)(2,1)}) custom-call(s32[4]{0:T(128)} %pad_add_fusion.1.order, bf16[256,4096]{1,0:T(8,128)(2,1)} %z0, bf16[256,4096]{1,0:T(8,128)(2,1)} %z0, bf16[256,4096]{1,0:T(8,128)(2,1)} %z0), custom_call_target="tpu_custom_call" | custom-call | tf_op jit(solution)/shard_map/cut/pallas_call | solution.py:125
  43.2 5.6 %collective-permute-done.8.d1 = f32[16,256]{1,0:T(8,128)S(1)} collective-permute-done((f32[16,256]{1,0:T(8,128)S(1)}, f32[16,256]{1,0:T(8,128)S(1)}, u32[]{:S(2)}, u32[]{:S(2)}) %collective-permute-start.8) | collective-permute-done | bytes 16416 | tf_op jit(solution)/shard_map/ppermute | solution.py:38
  52.1 2.7 %collective-permute-start.11 = (bf16[256,1280]{1,0:T(8,128)(2,1)S(1)}, bf16[256,1280]{1,0:T(8,128)(2,1)S(1)}, u32[]{:S(2)}, u32[]{:S(2)}) collective-permute-start(bf16[256,1280]{1,0:T(8,128)(2,1)S(1)} %copy-done.16), channel_id=1, source_target_pairs={{0,18},{1,19},{2,16},{3,17},{4,22},{5,23},{6,20},{7,21},{8,26},{9,... | collective-permute-start | bytes 1966088 | tf_op jit(solution)/shard_map/ppermute | solution.py:38
  55.5 13.3 %collective-permute-done.11.p3 = bf16[256,1280]{1,0:T(8,128)(2,1)S(1)} collective-permute-done((bf16[256,1280]{1,0:T(8,128)(2,1)S(1)}, bf16[256,1280]{1,0:T(8,128)(2,1)S(1)}, u32[]{:S(2)}, u32[]{:S(2)}) %collective-permute-start.11) | collective-permute-done | bytes 655392 | tf_op jit(solution)/shard_map/ppermute | solution.py:38
  69.6 12.7 %conv_states.1 = (bf16[4,256,1024]{2,1,0:T(8,128)(2,1)}, bf16[4,256,256]{2,1,0:T(8,128)(2,1)}, f32[4,16,256]{2,1,0:T(8,128)}, f32[4,256,16]{2,1,0:T(8,128)}, bf1...) custom-call(s32[2]{0:T(128)} %pad_add_fusion.place, ...), custom_call_target="tpu_custom_call" | custom-call | tf_op jit(solution)/shard_map/conv_states/pallas_call | solution.py:277
  83.6 1.5 collective-permute-start.13
  85.1 1.5 collective-permute-start.14
  87.9 7.4 %within.1.y = f32[4,256,1024]{2,1,0:T(8,128)} custom-call(s32[2]{0:T(128)} %pad_add_fusion.place, bf16[4,256,1024]{2,1,0:T(8,128)(2,1)} %get-tuple-element.142.xc, bf16[4,256,256]{2,1,0:T(8,128)(2,1)} %get-tuple-element.143.bc, f32[4,16,256]{2,1,0:T(8,128)} %get-tuple-element.144.low, f32[4,256,16]{2,1,0:T(8,128)} %get-tuple-element.145.cum, ...), custom_call_target="tpu_custom_call" | custom-call | tf_op jit(solution)/shard_map/within/pallas_call | solution.py:360
  95.3 2.6 %collective-permute-done.13.z1 = bf16[256,1024]{1,0:T(8,128)(2,1)S(1)} collective-permute-done((bf16[256,1024]{1,0:T(8,128)(2,1)}, bf16[256,1024]{1,0:T(8,128)(2,1)S(1)}, u32[]{:S(2)}, u32[]{:S(2)}) %collective-permute-start.13) | collective-permute-done | bytes 524320 | tf_op jit(solution)/shard_map/ppermute | solution.py:38
  97.9 1.9 collective-permute-done.14.z2
  99.9 8.3 %collective-permute-done.15.z3 = bf16[256,1024]{1,0:T(8,128)(2,1)S(1)} collective-permute-done((bf16[256,1024]{1,0:T(8,128)(2,1)S(1)}, bf16[256,1024]{1,0:T(8,128)(2,1)S(1)}, u32[]{:S(2)}, u32[]{:S(2)}) %collective-permute-start.15) | collective-permute-done | bytes 524320 | tf_op jit(solution)/shard_map/ppermute | solution.py:38
  108.2 17.8 %collective-permute-done.12.early.near = bf16[2,144,1024]{2,1,0:T(8,128)(2,1)S(1)} collective-permute-done((bf16[2,144,1024]{2,1,0:T(8,128)(2,1)}, bf16[2,144,1024]{2,1,0:T(8,128)(2,1)S(1)}, u32[]{:S(2)}, u32[]{:S(2)}) %collective-permute-start.12) | collective-permute-done | bytes 589856 | tf_op jit(solution)/shard_map/ppermute | solution.py:38
  126.8 2.3 %join.1 = bf16[2,144,1024]{2,1,0:T(8,128)(2,1)} custom-call(bf16[2,144,1024]{2,1,0:T(8,128)(2,1)} %get-tuple-element.141.late, bf16[2,144,1024]{2,1,0:T(8,128)(2,1)} %copy-done), custom_call_target="tpu_custom_call" | custom-call | tf_op jit(solution)/shard_map/join/pallas_call | solution.py:312
  130.6 36.5 %collective-permute-done.16.far = bf16[2,144,1024]{2,1,0:T(8,128)(2,1)S(1)} collective-permute-done((bf16[2,144,1024]{2,1,0:T(8,128)(2,1)}, bf16[2,144,1024]{2,1,0:T(8,128)(2,1)S(1)}, u32[]{:S(2)}, u32[]{:S(2)}) %collective-permute-start.16) | collective-permute-done | bytes 589856 | tf_op jit(solution)/shard_map/ppermute | solution.py:38
  167.9 8.2 %gate_norm.1 = bf16[4,256,1024]{2,1,0:T(8,128)(2,1)} custom-call(s32[2]{0:T(128)} %pad_add_fusion.place, f32[4,256,1024]{2,1,0:T(8,128)} %within.1.y, bf16[4,256,256]{2,1,0:T(8,128)(2,1)} %get-tuple-element.143.bc, bf16[4,48,256]{2,1,0:T(8,128)(2,1)} %get-tuple-element.150.kept, bf16[2,144,1024]{2,1,0:T(8,128)(2,1)} %copy-done, ...), custom_call_target="tpu_custom_call" | custom-call | tf_op jit(solution)/shard_map/gate_norm/pallas_call | solution.py:406
  176.2 2.6 %fusion.23 = bf16[256,1024]{1,0:T(8,128)(2,1)S(1)} fusion(bf16[1024,2048]{1,0:T(8,128)(2,1)} %all-gather.2.cloned.1.call-done, s32[]{:T(128)S(6)} %select_n.36, bf16[4,256,1024]{2,1,0:T(8,128)(2,1)} %gate_norm.1), kind=kOutput, calls=%fused_computation.24 | convolution fusion | flops 537133056 | bytes 3145732 | tf_op jit(solution)/shard_map/dot_general | solution.py:499
  178.9 2.3 %fusion.26 = bf16[256,1024]{1,0:T(8,128)(2,1)S(1)} fusion(bf16[1024,2048]{1,0:T(8,128)(2,1)} %all-gather.2.cloned.1.call-done, s32[]{:T(128)S(6)} %select_n.36, bf16[4,256,1024]{2,1,0:T(8,128)(2,1)S(1)} %copy-done.1), kind=kOutput, calls=%fused_computation.25 | convolution fusion | flops 537133056 | bytes 3145732 | tf_op jit(solution)/shard_map/dot_general | solution.py:499
  185.8 1.7 collective-permute-start.21
  188.2 1.5 collective-permute-start.23
  189.8 8.7 %collective-permute-done.19 = bf16[256,1024]{1,0:T(8,128)(2,1)S(1)} collective-permute-done((bf16[256,1024]{1,0:T(8,128)(2,1)S(1)}, bf16[256,1024]{1,0:T(8,128)(2,1)S(1)}, u32[]{:S(2)}, u32[]{:S(2)}) %collective-permute-start.19) | collective-permute-done | bytes 524320 | tf_op jit(solution)/shard_map/ppermute | solution.py:38
  198.5 2.1 collective-permute-done.21
  200.6 11.1 %collective-permute-done.23 = bf16[256,1024]{1,0:T(8,128)(2,1)S(1)} collective-permute-done((bf16[256,1024]{1,0:T(8,128)(2,1)S(1)}, bf16[256,1024]{1,0:T(8,128)(2,1)S(1)}, u32[]{:S(2)}, u32[]{:S(2)}) %collective-permute-start.23) | collective-permute-done | bytes 524320 | tf_op jit(solution)/shard_map/ppermute | solution.py:38
  211.8 1.8 fusion.17
  (100 shorter events, 22.7 us)
Async XLA Ops:
  6.5 169.6 %all-gather.2.cloned.1.call-start = ((), (), s32[]{:S(2)}) async-start(), calls=%async_computation | async-start | bytes 5242880 | tf_op jit(solution)/shard_map/all_gather | solution.py:472
  16.9 3.8 %collective-permute-start = (bf16[2,1024,256]{2,1,0:T(8,128)(2,1)}, bf16[2,1024,256]{2,1,0:T(8,128)(2,1)S(1)}, u32[]{:S(2)}, u32[]{:S(2)}) collective-permute-start(bf16[2,1024,256]{2,1,0:T(8,128)(2,1)} %bitcast.37), channel_id=1, source_target_pairs={{0,1},{1,0},{2,3},{3,2},{4,5},{5,4},{6,7},{7,6},{8,9},{9,8},{10,11... | collective-permute-start | bytes 3145736 | tf_op jit(solution)/shard_map/ppermute | solution.py:38
  16.9 17.1 %collective-permute-start.1 = (bf16[256,1280]{1,0:T(8,128)(2,1)S(1)}, bf16[256,1280]{1,0:T(8,128)(2,1)S(1)}, u32[]{:S(2)}, u32[]{:S(2)}) collective-permute-start(bf16[256,1280]{1,0:T(8,128)(2,1)S(1)} %copy-done.17), channel_id=1, source_target_pairs={{0,2},{1,3},{2,0},{3,1},{4,6},{5,7},{6,4},{7,5},{8,10},{9,11},{10,... | collective-permute-start | bytes 1966088 | tf_op jit(solution)/shard_map/ppermute | solution.py:38
  17.4 5.9 %collective-permute-start.2 = (bf16[16,1280]{1,0:T(8,128)(2,1)S(1)}, bf16[16,1280]{1,0:T(8,128)(2,1)S(1)}, u32[]{:S(2)}, u32[]{:S(2)}) collective-permute-start(bf16[16,1280]{1,0:T(8,128)(2,1)S(1)} %copy-done.23), channel_id=1, source_target_pairs={{2,6},{3,7},{6,10},{7,11},{10,14},{11,15},{18,22},{19,23},{22,26},... | collective-permute-start | bytes 122888 | tf_op jit(solution)/shard_map/ppermute | solution.py:38
  18.7 6.1 %collective-permute-start.3 = (bf16[16,1280]{1,0:T(8,128)(2,1)S(1)}, bf16[16,1280]{1,0:T(8,128)(2,1)S(1)}, u32[]{:S(2)}, u32[]{:S(2)}) collective-permute-start(bf16[16,1280]{1,0:T(8,128)(2,1)S(1)} %copy-done.22), channel_id=1, source_target_pairs={{2,4},{3,5},{6,8},{7,9},{10,12},{11,13},{18,20},{19,21},{22,24},{2... | collective-permute-start | bytes 122888 | tf_op jit(solution)/shard_map/ppermute | solution.py:38
  19.4 8.4 %collective-permute-start.4 = (bf16[16,1280]{1,0:T(8,128)(2,1)S(1)}, bf16[16,1280]{1,0:T(8,128)(2,1)S(1)}, u32[]{:S(2)}, u32[]{:S(2)}) collective-permute-start(bf16[16,1280]{1,0:T(8,128)(2,1)S(1)} %copy-done.21), channel_id=1, source_target_pairs={{2,22},{3,23},{6,26},{7,27},{10,30},{11,31},{18,6},{19,7},{22,10},... | collective-permute-start | bytes 122888 | tf_op jit(solution)/shard_map/ppermute | solution.py:38
  20.7 7.1 %collective-permute-start.5 = (bf16[16,1280]{1,0:T(8,128)(2,1)S(1)}, bf16[16,1280]{1,0:T(8,128)(2,1)S(1)}, u32[]{:S(2)}, u32[]{:S(2)}) collective-permute-start(bf16[16,1280]{1,0:T(8,128)(2,1)S(1)} %copy-done.20), channel_id=1, source_target_pairs={{2,20},{3,21},{6,24},{7,25},{10,28},{11,29},{18,4},{19,5},{22,8},{... | collective-permute-start | bytes 122888 | tf_op jit(solution)/shard_map/ppermute | solution.py:38
  23.3 25.6 %collective-permute-start.7 = (bf16[256,1280]{1,0:T(8,128)(2,1)}, bf16[256,1280]{1,0:T(8,128)(2,1)S(1)}, u32[]{:S(2)}, u32[]{:S(2)}) collective-permute-start(bf16[256,1280]{1,0:T(8,128)(2,1)} %get-tuple-element.111), channel_id=1, source_target_pairs={{0,16},{1,17},{2,18},{3,19},{4,20},{5,21},{6,22},{7,23},{8,24},{9,... | collective-permute-start | bytes 1966088 | tf_op jit(solution)/shard_map/ppermute | solution.py:38
  34.1 14.8 %collective-permute-start.6 = (bf16[1024,256]{1,0:T(8,128)(2,1)S(1)}, bf16[1024,256]{1,0:T(8,128)(2,1)S(1)}, u32[]{:S(2)}, u32[]{:S(2)}) collective-permute-start(bf16[1024,256]{1,0:T(8,128)(2,1)S(1)} %get-tuple-element.158), channel_id=1, source_target_pairs={{0,2},{1,3},{2,0},{3,1},{4,6},{5,7},{6,4},{7,5},{8,10},{9,11},{10,... | collective-permute-start | bytes 1572872 | tf_op jit(solution)/shard_map/ppermute | solution.py:38
  36.4 6.8 %collective-permute-start.10 = (f32[16,256]{1,0:T(8,128)S(1)}, f32[16,256]{1,0:T(8,128)S(1)}, u32[]{:S(2)}, u32[]{:S(2)}) collective-permute-start(f32[16,256]{1,0:T(8,128)S(1)} %copy-done.26), channel_id=1, source_target_pairs={{0,18},{1,19},{2,16},{3,17},{4,22},{5,23},{6,20},{7,21},{8,26},{9,... | collective-permute-start | bytes 49160 | tf_op jit(solution)/shard_map/ppermute | solution.py:38
  37.5 11.4 %collective-permute-start.8 = (f32[16,256]{1,0:T(8,128)S(1)}, f32[16,256]{1,0:T(8,128)S(1)}, u32[]{:S(2)}, u32[]{:S(2)}) collective-permute-start(f32[16,256]{1,0:T(8,128)S(1)} %copy-done.25), channel_id=1, source_target_pairs={{0,2},{1,3},{2,0},{3,1},{4,6},{5,7},{6,4},{7,5},{8,10},{9,11},{10,... | collective-permute-start | bytes 49160 | tf_op jit(solution)/shard_map/ppermute | solution.py:38
  39.4 9.5 %collective-permute-start.9 = (f32[16,256]{1,0:T(8,128)S(1)}, f32[16,256]{1,0:T(8,128)S(1)}, u32[]{:S(2)}, u32[]{:S(2)}) collective-permute-start(f32[16,256]{1,0:T(8,128)S(1)} %copy-done.24), channel_id=1, source_target_pairs={{0,16},{1,17},{2,18},{3,19},{4,20},{5,21},{6,22},{7,23},{8,24},{9,... | collective-permute-start | bytes 49160 | tf_op jit(solution)/shard_map/ppermute | solution.py:38
  43.2 25.5 %copy-start.9 = (f32[16,256]{1,0:T(8,128)}, f32[16,256]{1,0:T(8,128)S(1)}, u32[]{:S(2)}) copy-start(f32[16,256]{1,0:T(8,128)S(1)} %collective-permute-done.10.d3) | copy-start | bytes 49156
  50.2 34.9 %copy-start.19 = (bf16[256,1024]{1,0:T(8,128)(2,1)S(1)}, bf16[256,1024]{1,0:T(8,128)(2,1)}, u32[]{:S(2)}) copy-start(bf16[256,1024]{1,0:T(8,128)(2,1)} %get-tuple-element.147) | copy-start | bytes 1572868
  50.2 36.4 %copy-start.18 = (bf16[256,1024]{1,0:T(8,128)(2,1)S(1)}, bf16[256,1024]{1,0:T(8,128)(2,1)}, u32[]{:S(2)}) copy-start(bf16[256,1024]{1,0:T(8,128)(2,1)} %get-tuple-element.148) | copy-start | bytes 1572868
  50.2 37.0 %copy-start.14 = (f32[64]{0:T(128)S(1)}, f32[64]{0:T(128)}, u32[]{:S(2)}) copy-start(f32[64]{0:T(128)} %param.20) | copy-start | bytes 772
  52.1 16.6 %collective-permute-start.11 = (bf16[256,1280]{1,0:T(8,128)(2,1)S(1)}, bf16[256,1280]{1,0:T(8,128)(2,1)S(1)}, u32[]{:S(2)}, u32[]{:S(2)}) collective-permute-start(bf16[256,1280]{1,0:T(8,128)(2,1)S(1)} %copy-done.16), channel_id=1, source_target_pairs={{0,18},{1,19},{2,16},{3,17},{4,22},{5,23},{6,20},{7,21},{8,26},{9,... | collective-permute-start | bytes 1966088 | tf_op jit(solution)/shard_map/ppermute | solution.py:38
  82.3 43.8 %collective-permute-start.12 = (bf16[2,144,1024]{2,1,0:T(8,128)(2,1)}, bf16[2,144,1024]{2,1,0:T(8,128)(2,1)S(1)}, u32[]{:S(2)}, u32[]{:S(2)}) collective-permute-start(bf16[2,144,1024]{2,1,0:T(8,128)(2,1)} %get-tuple-element.141.late), channel_id=1, source_target_pairs={{0,4},{1,5},{2,6},{3,7},{4,8},{5,9},{6,10},{7,11},{8,12},{9,13},{1... | collective-permute-start | bytes 1769480 | tf_op jit(solution)/shard_map/ppermute | solution.py:38
  83.6 14.4 %collective-permute-start.13 = (bf16[256,1024]{1,0:T(8,128)(2,1)}, bf16[256,1024]{1,0:T(8,128)(2,1)S(1)}, u32[]{:S(2)}, u32[]{:S(2)}) collective-permute-start(bf16[256,1024]{1,0:T(8,128)(2,1)} %get-tuple-element.146), channel_id=1, source_target_pairs={{0,2},{1,3},{2,0},{3,1},{4,6},{5,7},{6,4},{7,5},{8,10},{9,11},{10,... | collective-permute-start | bytes 1572872 | tf_op jit(solution)/shard_map/ppermute | solution.py:38
  85.1 14.8 %collective-permute-start.14 = (bf16[256,1024]{1,0:T(8,128)(2,1)S(1)}, bf16[256,1024]{1,0:T(8,128)(2,1)S(1)}, u32[]{:S(2)}, u32[]{:S(2)}) collective-permute-start(bf16[256,1024]{1,0:T(8,128)(2,1)S(1)} %copy-done.19), channel_id=1, source_target_pairs={{0,16},{1,17},{2,18},{3,19},{4,20},{5,21},{6,22},{7,23},{8,24},{9,... | collective-permute-start | bytes 1572872 | tf_op jit(solution)/shard_map/ppermute | solution.py:38
  86.6 21.6 %collective-permute-start.15 = (bf16[256,1024]{1,0:T(8,128)(2,1)S(1)}, bf16[256,1024]{1,0:T(8,128)(2,1)S(1)}, u32[]{:S(2)}, u32[]{:S(2)}) collective-permute-start(bf16[256,1024]{1,0:T(8,128)(2,1)S(1)} %copy-done.18), channel_id=1, source_target_pairs={{0,18},{1,19},{2,16},{3,17},{4,22},{5,23},{6,20},{7,21},{8,26},{9,... | collective-permute-start | bytes 1572872 | tf_op jit(solution)/shard_map/ppermute | solution.py:38
  97.9 69.1 %copy-start.6 = (bf16[256,1024]{1,0:T(8,128)(2,1)}, bf16[256,1024]{1,0:T(8,128)(2,1)S(1)}, u32[]{:S(2)}) copy-start(bf16[256,1024]{1,0:T(8,128)(2,1)S(1)} %collective-permute-done.13.z1) | copy-start | bytes 1572868
  99.9 67.2 %copy-start.7 = (bf16[256,1024]{1,0:T(8,128)(2,1)}, bf16[256,1024]{1,0:T(8,128)(2,1)S(1)}, u32[]{:S(2)}) copy-start(bf16[256,1024]{1,0:T(8,128)(2,1)S(1)} %collective-permute-done.14.z2) | copy-start | bytes 1572868
  108.2 58.8 %copy-start.8 = (bf16[256,1024]{1,0:T(8,128)(2,1)}, bf16[256,1024]{1,0:T(8,128)(2,1)S(1)}, u32[]{:S(2)}) copy-start(bf16[256,1024]{1,0:T(8,128)(2,1)S(1)} %collective-permute-done.15.z3) | copy-start | bytes 1572868
  129.1 38.0 %collective-permute-start.16 = (bf16[2,144,1024]{2,1,0:T(8,128)(2,1)}, bf16[2,144,1024]{2,1,0:T(8,128)(2,1)S(1)}, u32[]{:S(2)}, u32[]{:S(2)}) collective-permute-start(bf16[2,144,1024]{2,1,0:T(8,128)(2,1)} %join.1), channel_id=1, source_target_pairs={{0,8},{1,9},{2,10},{3,11},{4,12},{5,13},{6,14},{7,15},{16,24},{17,... | collective-permute-start | bytes 1769480 | tf_op jit(solution)/shard_map/ppermute | solution.py:38
  178.8 5.1 %collective-permute-start.18 = (bf16[256,1024]{1,0:T(8,128)(2,1)S(1)}, bf16[256,1024]{1,0:T(8,128)(2,1)S(1)}, u32[]{:S(2)}, u32[]{:S(2)}) collective-permute-start(bf16[256,1024]{1,0:T(8,128)(2,1)S(1)} %fusion.23), channel_id=1, source_target_pairs={{0,1},{1,0},{2,3},{3,2},{4,5},{5,4},{6,7},{7,6},{8,9},{9,8},{10,11... | collective-permute-start | bytes 1572872 | tf_op jit(solution)/shard_map/ppermute | solution.py:38
  181.2 3.8 %collective-permute-start.20 = (bf16[256,1024]{1,0:T(8,128)(2,1)S(1)}, bf16[256,1024]{1,0:T(8,128)(2,1)S(1)}, u32[]{:S(2)}, u32[]{:S(2)}) collective-permute-start(bf16[256,1024]{1,0:T(8,128)(2,1)S(1)} %fusion.26), channel_id=1, source_target_pairs={{0,1},{1,0},{2,3},{3,2},{4,5},{5,4},{6,7},{7,6},{8,9},{9,8},{10,11... | collective-permute-start | bytes 1572872 | tf_op jit(solution)/shard_map/ppermute | solution.py:38
  182.5 7.3 %collective-permute-start.17 = (bf16[256,1024]{1,0:T(8,128)(2,1)S(1)}, bf16[256,1024]{1,0:T(8,128)(2,1)S(1)}, u32[]{:S(2)}, u32[]{:S(2)}) collective-permute-start(bf16[256,1024]{1,0:T(8,128)(2,1)S(1)} %fusion.20), channel_id=1, source_target_pairs={{0,1},{1,0},{2,3},{3,2},{4,5},{5,4},{6,7},{7,6},{8,9},{9,8},{10,11... | collective-permute-start | bytes 1572872 | tf_op jit(solution)/shard_map/ppermute | solution.py:38
  183.3 4.2 %collective-permute-start.22 = (bf16[256,1024]{1,0:T(8,128)(2,1)S(1)}, bf16[256,1024]{1,0:T(8,128)(2,1)S(1)}, u32[]{:S(2)}, u32[]{:S(2)}) collective-permute-start(bf16[256,1024]{1,0:T(8,128)(2,1)S(1)} %fusion.29), channel_id=1, source_target_pairs={{0,1},{1,0},{2,3},{3,2},{4,5},{5,4},{6,7},{7,6},{8,9},{9,8},{10,11... | collective-permute-start | bytes 1572872 | tf_op jit(solution)/shard_map/ppermute | solution.py:38
  184.6 13.9 %collective-permute-start.19 = (bf16[256,1024]{1,0:T(8,128)(2,1)S(1)}, bf16[256,1024]{1,0:T(8,128)(2,1)S(1)}, u32[]{:S(2)}, u32[]{:S(2)}) collective-permute-start(bf16[256,1024]{1,0:T(8,128)(2,1)S(1)} %fusion.32), channel_id=1, source_target_pairs={{0,2},{1,3},{2,0},{3,1},{4,6},{5,7},{6,4},{7,5},{8,10},{9,11},{10,... | collective-permute-start | bytes 1572872 | tf_op jit(solution)/shard_map/ppermute | solution.py:38
  185.8 14.9 %collective-permute-start.21 = (bf16[256,1024]{1,0:T(8,128)(2,1)S(1)}, bf16[256,1024]{1,0:T(8,128)(2,1)S(1)}, u32[]{:S(2)}, u32[]{:S(2)}) collective-permute-start(bf16[256,1024]{1,0:T(8,128)(2,1)S(1)} %fusion.35), channel_id=1, source_target_pairs={{0,16},{1,17},{2,18},{3,19},{4,20},{5,21},{6,22},{7,23},{8,24},{9,... | collective-permute-start | bytes 1572872 | tf_op jit(solution)/shard_map/ppermute | solution.py:38
  188.2 23.5 %collective-permute-start.23 = (bf16[256,1024]{1,0:T(8,128)(2,1)S(1)}, bf16[256,1024]{1,0:T(8,128)(2,1)S(1)}, u32[]{:S(2)}, u32[]{:S(2)}) collective-permute-start(bf16[256,1024]{1,0:T(8,128)(2,1)S(1)} %fusion.38), channel_id=1, source_target_pairs={{0,18},{1,19},{2,16},{3,17},{4,22},{5,23},{6,20},{7,21},{8,26},{9,... | collective-permute-start | bytes 1572872 | tf_op jit(solution)/shard_map/ppermute | solution.py:38
  (20 other events, 175.9 us)
Sparse Core Ops, SparseCore 0:
  50.3 109.4 all-gather.1

commit v5 on v3

--- a/solution.py
+++ b/solution.py
@@ -73,16 +73,18 @@
     return half + half * jnp.tanh(half)
 
 
-def pack_kernel(order, x0, x1, x2, x3, b0, b1, b2, b3, dt, o0, o1, o2, o3, d0, d1, d2, d3, turned):
+def pack_kernel(order, x0, x1, x2, x3, b0, b1, b2, b3, dt, o0, o1, o2, o3, d0, d1, d2, d3, e0, e1, e2, e3, turned):
     turned[...] = dt[...].T
-    for k, (x, b, o, d) in enumerate(
-        ((x0, b0, o0, d0), (x1, b1, o1, d1), (x2, b2, o2, d2), (x3, b3, o3, d3))
+    rows = x0.shape[0]
+    for k, (x, b, o, d, e) in enumerate(
+        ((x0, b0, o0, d0, e0), (x1, b1, o1, d1, e1), (x2, b2, o2, d2, e2), (x3, b3, o3, d3, e3))
     ):
         o[:, :GROUP] = x[...]
         o[:, GROUP : GROUP + STATE] = b[0]
         o[:, GROUP + STATE :] = b[1]
         first = pl.multiple_of(order[k] * PER, PER)
         d[...] = turned[pl.ds(first, PER), :]
+        e[...] = o[rows - 16 :, :]
 
 
 def pack(order, x_in, bc_in, dt_raw):
@@ -102,11 +104,12 @@
                 for k in range(4)
             ]
             + [whole(rows, dt_raw.shape[1])],
-            out_specs=[whole(rows, wide)] * 4 + [whole(PER, rows)] * 4,
+            out_specs=[whole(rows, wide)] * 4 + [whole(PER, rows)] * 4 + [whole(16, wide)] * 4,
             scratch_shapes=[pltpu.VMEM((dt_raw.shape[1], rows), F32)],
         ),
         out_shape=[jax.ShapeDtypeStruct((rows, wide), BF16)] * 4
-        + [jax.ShapeDtypeStruct((PER, rows), F32)] * 4,
+        + [jax.ShapeDtypeStruct((PER, rows), F32)] * 4
+        + [jax.ShapeDtypeStruct((16, wide), BF16)] * 4,
         name="pack",
     )(order, x_in, x_in, x_in, x_in, bc_in, bc_in, bc_in, bc_in, dt_raw)
 
@@ -451,7 +454,15 @@
     steps = [packed[4]] + [swap(packed[4 + k], k) for k in range(1, 4)]
     z_in, packed = after(z_in, packed)
     slices = cut(order, z_in)
-    given, slices = after(given, slices)
+    tails = [
+        send(
+            packed[8 + k],
+            lambda x, z, y, t, k=k: (x ^ (k >> 1), z + 1, y ^ (k & 1), t) if y == 1 else None,
+        )
+        for k in range(4)
+    ]
+    given, (slices, tails) = after(given, (slices, tails))
+    halo = jnp.stack([tails[0] + tails[1], tails[2] + tails[3]])
     columns = jnp.where(
         y_here == 0,
         jnp.concatenate([keep, given], axis=1),
@@ -459,11 +470,6 @@
     )
     weight = lax.all_gather(columns, "sz", axis=1, tiled=True)
     pieces, columns = after(pieces, columns)
-    tails = [p[rows - 16 :] for p in pieces]
-    closing = jnp.where(
-        y_here == 1, jnp.stack([tails[0], tails[2]]), jnp.stack([tails[1], tails[3]])
-    )
-    halo = onward(closing, 1)
     slices, pieces = after(slices, pieces)
     zs = [swap(z, k + 1) for k, z in enumerate(slices)]
 

time: 213 us -> 211 us (level)
  waiting for transfers between devices: 117 us -> 109 us
  starting transfers between devices: 20.1 us -> 24.7 us
    ppermute x21 -> x24, waiting for transfers between devices: 117 us -> 109 us  [send(): return lax.ppermute(array, AXES, pairs)]
    ppermute x21 -> x24, starting transfers between devices: 20.1 us -> 24.7 us  [send(): return lax.ppermute(array, AXES, pairs)]
  transfers between devices with their start and end apart: 22 -> 25, of which waited for: 12 -> 14; matrix products, arithmetic and copies ran while one was open for 5% -> 5% of each run, Pallas kernels for 18% -> 18%
where the time goes in v5:
time: 211 us; the launch traced here: 209 us
  waiting for transfers between devices  109 us (52%)
  Pallas kernels  42 us (20%)
  starting transfers between devices  24.7 us (12%)
  between operations  13.7 us (6%)
  matrix products  10.3 us (5%)
  local copies, waits for them, and re-layouts  5.86 us (3%)
  other arithmetic  3.4 us (2%)
    ppermute x24, waiting for transfers between devices, send(): return lax.ppermute(array, AXES, pairs)  109 us
    ppermute x24, starting transfers between devices, send(): return lax.ppermute(array, AXES, pairs)  24.7 us
    pallas_call x1, Pallas kernels, conv_states(): pl.pallas_call(conv_kernel, grid_spec=pltpu.PrefetchScalarGridSpec(num_sc...  12.7 us
    pallas_call x1, Pallas kernels, gate_norm(): pl.pallas_call(gate_kernel, grid_spec=pltpu.PrefetchScalarGridSpec(num_sc...  8.25 us
    pallas_call x1, Pallas kernels, within(): pl.pallas_call(within_kernel, grid_spec=pltpu.PrefetchScalarGridSpec(num_...  7.41 us
    dot_general x4, matrix products, per_device(): away = jnp.dot(act[k], theirs, preferred_element_type=F32).astype(BF16)  6.38 us
  transfers between devices with their start and end apart: 25, of which 14 were waited for; matrix products, arithmetic and copies ran while one was open for 5% of the time, Pallas kernels for 18%

profile of v5, /device:TPU:28, one launch (start us, length us, event | category | flops | bytes accessed | tf_op | source)
XLA Modules:
  0.0 209.0 jit_solution(16123342911013657923)
XLA Ops:
  6.5 4.1 %turn.1 = bf16[8,256,256]{2,1,0:T(8,128)(2,1)} custom-call(s32[1]{0:T(128)} %bitcast.5.sign, bf16[4096,256]{1,0:T(8,128)(2,1)} %w.1), custom_call_target="tpu_custom_call" | custom-call | tf_op jit(solution)/shard_map/turn/pallas_call | solution.py:178
  11.9 4.1 %pack.1 = (bf16[256,1280]{1,0:T(8,128)(2,1)}, bf16[256,1280]{1,0:T(8,128)(2,1)}, bf16[256,1280]{1,0:T(8,128)(2,1)}, bf16[256,1280]{1,0:T(8,128)(2,1)}, f32[16,25...) custom-call(s32[4]{0:T(128)} %pad_add_fusion.1.order, ...), custom_call_target="tpu_custom_call" | custom-call | tf_op jit(solution)/shard_map/pack/pallas_call | solution.py:94
  21.2 3.2 %cut.1 = (bf16[256,1024]{1,0:T(8,128)(2,1)}, bf16[256,1024]{1,0:T(8,128)(2,1)}, bf16[256,1024]{1,0:T(8,128)(2,1)}) custom-call(s32[4]{0:T(128)} %pad_add_fusion.1.order, bf16[256,4096]{1,0:T(8,128)(2,1)} %z0, bf16[256,4096]{1,0:T(8,128)(2,1)} %z0, bf16[256,4096]{1,0:T(8,128)(2,1)} %z0), custom_call_target="tpu_custom_call" | custom-call | tf_op jit(solution)/shard_map/cut/pallas_call | solution.py:125
  24.4 3.2 %collective-permute-done.4 = bf16[16,1280]{1,0:T(8,128)(2,1)S(1)} collective-permute-done((bf16[16,1280]{1,0:T(8,128)(2,1)S(1)}, bf16[16,1280]{1,0:T(8,128)(2,1)S(1)}, u32[]{:S(2)}, u32[]{:S(2)}) %collective-permute-start.4) | collective-permute-done | bytes 40992 | tf_op jit(solution)/shard_map/ppermute | solution.py:38
  27.6 3.4 %collective-permute-done.1 = bf16[1024,256]{1,0:T(8,128)(2,1)S(1)} collective-permute-done((bf16[1024,256]{1,0:T(8,128)(2,1)S(1)}, bf16[1024,256]{1,0:T(8,128)(2,1)S(1)}, u32[]{:S(2)}, u32[]{:S(2)}) %collective-permute-start.1) | collective-permute-done | bytes 524320 | tf_op jit(solution)/shard_map/ppermute | solution.py:38
  32.3 2.3 %collective-permute-start.6 = (bf16[256,1280]{1,0:T(8,128)(2,1)}, bf16[256,1280]{1,0:T(8,128)(2,1)S(1)}, u32[]{:S(2)}, u32[]{:S(2)}) collective-permute-start(bf16[256,1280]{1,0:T(8,128)(2,1)} %get-tuple-element.114), channel_id=1, source_target_pairs={{0,2},{1,3},{2,0},{3,1},{4,6},{5,7},{6,4},{7,5},{8,10},{9,11},{10,... | collective-permute-start | bytes 1966088 | tf_op jit(solution)/shard_map/ppermute | solution.py:38
  36.6 1.5 collective-permute-start.7
  38.1 1.5 collective-permute-start.10
  39.6 2.0 collective-permute-start.11
  41.6 7.8 %collective-permute-done.6.p1 = bf16[256,1280]{1,0:T(8,128)(2,1)S(1)} collective-permute-done((bf16[256,1280]{1,0:T(8,128)(2,1)}, bf16[256,1280]{1,0:T(8,128)(2,1)S(1)}, u32[]{:S(2)}, u32[]{:S(2)}) %collective-permute-start.6) | collective-permute-done | bytes 655392 | tf_op jit(solution)/shard_map/ppermute | solution.py:38
  49.4 1.7 collective-permute-start.9
  51.8 2.4 %collective-permute-done.7.p2 = bf16[256,1280]{1,0:T(8,128)(2,1)S(1)} collective-permute-done((bf16[256,1280]{1,0:T(8,128)(2,1)S(1)}, bf16[256,1280]{1,0:T(8,128)(2,1)S(1)}, u32[]{:S(2)}, u32[]{:S(2)}) %collective-permute-start.7) | collective-permute-done | bytes 655392 | tf_op jit(solution)/shard_map/ppermute | solution.py:38
  54.2 12.5 %collective-permute-done.8.p3 = bf16[256,1280]{1,0:T(8,128)(2,1)S(1)} collective-permute-done((bf16[256,1280]{1,0:T(8,128)(2,1)S(1)}, bf16[256,1280]{1,0:T(8,128)(2,1)S(1)}, u32[]{:S(2)}, u32[]{:S(2)}) %collective-permute-start.8) | collective-permute-done | bytes 655392 | tf_op jit(solution)/shard_map/ppermute | solution.py:38
  68.4 12.7 %conv_states.1 = (bf16[4,256,1024]{2,1,0:T(8,128)(2,1)}, bf16[4,256,256]{2,1,0:T(8,128)(2,1)}, f32[4,16,256]{2,1,0:T(8,128)}, f32[4,256,16]{2,1,0:T(8,128)}, bf1...) custom-call(s32[2]{0:T(128)} %pad_add_fusion.place, ...), custom_call_target="tpu_custom_call" | custom-call | tf_op jit(solution)/shard_map/conv_states/pallas_call | solution.py:277
  82.3 1.7 collective-permute-start.13
  84.0 1.5 collective-permute-start.14
  86.7 7.4 %within.1.y = f32[4,256,1024]{2,1,0:T(8,128)} custom-call(s32[2]{0:T(128)} %pad_add_fusion.place, bf16[4,256,1024]{2,1,0:T(8,128)(2,1)} %get-tuple-element.150.xc, bf16[4,256,256]{2,1,0:T(8,128)(2,1)} %get-tuple-element.151.bc, f32[4,16,256]{2,1,0:T(8,128)} %get-tuple-element.152.low, f32[4,256,16]{2,1,0:T(8,128)} %get-tuple-element.153.cum, ...), custom_call_target="tpu_custom_call" | custom-call | tf_op jit(solution)/shard_map/within/pallas_call | solution.py:360
  94.1 2.4 %collective-permute-done.13.z1 = bf16[256,1024]{1,0:T(8,128)(2,1)S(1)} collective-permute-done((bf16[256,1024]{1,0:T(8,128)(2,1)}, bf16[256,1024]{1,0:T(8,128)(2,1)S(1)}, u32[]{:S(2)}, u32[]{:S(2)}) %collective-permute-start.13) | collective-permute-done | bytes 524320 | tf_op jit(solution)/shard_map/ppermute | solution.py:38
  96.5 2.5 %collective-permute-done.14.z2 = bf16[256,1024]{1,0:T(8,128)(2,1)S(1)} collective-permute-done((bf16[256,1024]{1,0:T(8,128)(2,1)}, bf16[256,1024]{1,0:T(8,128)(2,1)S(1)}, u32[]{:S(2)}, u32[]{:S(2)}) %collective-permute-start.14) | collective-permute-done | bytes 524320 | tf_op jit(solution)/shard_map/ppermute | solution.py:38
  99.0 8.7 %collective-permute-done.15.z3 = bf16[256,1024]{1,0:T(8,128)(2,1)S(1)} collective-permute-done((bf16[256,1024]{1,0:T(8,128)(2,1)}, bf16[256,1024]{1,0:T(8,128)(2,1)S(1)}, u32[]{:S(2)}, u32[]{:S(2)}) %collective-permute-start.15) | collective-permute-done | bytes 524320 | tf_op jit(solution)/shard_map/ppermute | solution.py:38
  107.7 15.3 %collective-permute-done.12.early.near = bf16[2,144,1024]{2,1,0:T(8,128)(2,1)S(1)} collective-permute-done((bf16[2,144,1024]{2,1,0:T(8,128)(2,1)}, bf16[2,144,1024]{2,1,0:T(8,128)(2,1)S(1)}, u32[]{:S(2)}, u32[]{:S(2)}) %collective-permute-start.12) | collective-permute-done | bytes 589856 | tf_op jit(solution)/shard_map/ppermute | solution.py:38
  123.8 2.3 %join.1 = bf16[2,144,1024]{2,1,0:T(8,128)(2,1)} custom-call(bf16[2,144,1024]{2,1,0:T(8,128)(2,1)} %get-tuple-element.149.late, bf16[2,144,1024]{2,1,0:T(8,128)(2,1)} %copy-done.1), custom_call_target="tpu_custom_call" | custom-call | tf_op jit(solution)/shard_map/join/pallas_call | solution.py:312
  126.0 1.5 collective-permute-start.16
  127.5 28.2 %collective-permute-done.16.far = bf16[2,144,1024]{2,1,0:T(8,128)(2,1)S(1)} collective-permute-done((bf16[2,144,1024]{2,1,0:T(8,128)(2,1)}, bf16[2,144,1024]{2,1,0:T(8,128)(2,1)S(1)}, u32[]{:S(2)}, u32[]{:S(2)}) %collective-permute-start.16) | collective-permute-done | bytes 589856 | tf_op jit(solution)/shard_map/ppermute | solution.py:38
  156.5 8.2 %gate_norm.1 = bf16[4,256,1024]{2,1,0:T(8,128)(2,1)} custom-call(s32[2]{0:T(128)} %pad_add_fusion.place, f32[4,256,1024]{2,1,0:T(8,128)} %within.1.y, bf16[4,256,256]{2,1,0:T(8,128)(2,1)} %get-tuple-element.151.bc, bf16[4,48,256]{2,1,0:T(8,128)(2,1)} %get-tuple-element.158.kept, bf16[2,144,1024]{2,1,0:T(8,128)(2,1)} %copy-done.1, ...), custom_call_target="tpu_custom_call" | custom-call | tf_op jit(solution)/shard_map/gate_norm/pallas_call | solution.py:406
  164.8 2.6 %fusion.23 = bf16[256,1024]{1,0:T(8,128)(2,1)S(1)} fusion(bf16[1024,2048]{1,0:T(8,128)(2,1)} %all-gather.2.cloned.1.call-done, s32[]{:T(128)S(6)} %select_n.36, bf16[4,256,1024]{2,1,0:T(8,128)(2,1)} %gate_norm.1), kind=kOutput, calls=%fused_computation.24 | convolution fusion | flops 537133056 | bytes 3145732 | tf_op jit(solution)/shard_map/dot_general | solution.py:498
  167.5 2.3 %fusion.26 = bf16[256,1024]{1,0:T(8,128)(2,1)S(1)} fusion(bf16[1024,2048]{1,0:T(8,128)(2,1)} %all-gather.2.cloned.1.call-done, s32[]{:T(128)S(6)} %select_n.36, bf16[4,256,1024]{2,1,0:T(8,128)(2,1)S(1)} %copy-done.2), kind=kOutput, calls=%fused_computation.25 | convolution fusion | flops 537133056 | bytes 3145732 | tf_op jit(solution)/shard_map/dot_general | solution.py:498
  173.3 1.5 collective-permute-start.19
  178.4 8.7 %collective-permute-done.19 = bf16[256,1024]{1,0:T(8,128)(2,1)S(1)} collective-permute-done((bf16[256,1024]{1,0:T(8,128)(2,1)S(1)}, bf16[256,1024]{1,0:T(8,128)(2,1)S(1)}, u32[]{:S(2)}, u32[]{:S(2)}) %collective-permute-start.19) | collective-permute-done | bytes 524320 | tf_op jit(solution)/shard_map/ppermute | solution.py:38
  187.2 3.2 %collective-permute-done.21 = bf16[256,1024]{1,0:T(8,128)(2,1)S(1)} collective-permute-done((bf16[256,1024]{1,0:T(8,128)(2,1)S(1)}, bf16[256,1024]{1,0:T(8,128)(2,1)S(1)}, u32[]{:S(2)}, u32[]{:S(2)}) %collective-permute-start.21) | collective-permute-done | bytes 524320 | tf_op jit(solution)/shard_map/ppermute | solution.py:38
  190.4 10.0 %collective-permute-done.23 = bf16[256,1024]{1,0:T(8,128)(2,1)S(1)} collective-permute-done((bf16[256,1024]{1,0:T(8,128)(2,1)S(1)}, bf16[256,1024]{1,0:T(8,128)(2,1)S(1)}, u32[]{:S(2)}, u32[]{:S(2)}) %collective-permute-start.23) | collective-permute-done | bytes 524320 | tf_op jit(solution)/shard_map/ppermute | solution.py:38
  200.4 1.8 fusion.17
  (100 shorter events, 23.0 us)
Async XLA Ops:
  6.5 158.3 %all-gather.2.cloned.1.call-start = ((), (), s32[]{:S(2)}) async-start(), calls=%async_computation | async-start | bytes 5242880 | tf_op jit(solution)/shard_map/all_gather | solution.py:471
  10.6 5.5 %collective-permute-start = (bf16[2,1024,256]{2,1,0:T(8,128)(2,1)}, bf16[2,1024,256]{2,1,0:T(8,128)(2,1)S(1)}, u32[]{:S(2)}, u32[]{:S(2)}) collective-permute-start(bf16[2,1024,256]{2,1,0:T(8,128)(2,1)} %bitcast.35), channel_id=1, source_target_pairs={{0,1},{1,0},{2,3},{3,2},{4,5},{5,4},{6,7},{7,6},{8,9},{9,8},{10,11... | collective-permute-start | bytes 3145736 | tf_op jit(solution)/shard_map/ppermute | solution.py:38
  16.6 14.4 %collective-permute-start.1 = (bf16[1024,256]{1,0:T(8,128)(2,1)S(1)}, bf16[1024,256]{1,0:T(8,128)(2,1)S(1)}, u32[]{:S(2)}, u32[]{:S(2)}) collective-permute-start(bf16[1024,256]{1,0:T(8,128)(2,1)S(1)} %get-tuple-element.166), channel_id=1, source_target_pairs={{0,2},{1,3},{2,0},{3,1},{4,6},{5,7},{6,4},{7,5},{8,10},{9,11},{10,... | collective-permute-start | bytes 1572872 | tf_op jit(solution)/shard_map/ppermute | solution.py:38
  17.2 7.2 %collective-permute-start.2 = (bf16[16,1280]{1,0:T(8,128)(2,1)S(1)}, bf16[16,1280]{1,0:T(8,128)(2,1)S(1)}, u32[]{:S(2)}, u32[]{:S(2)}) collective-permute-start(bf16[16,1280]{1,0:T(8,128)(2,1)S(1)} %copy-done.23), channel_id=1, source_target_pairs={{2,6},{3,7},{6,10},{7,11},{10,14},{11,15},{18,22},{19,23},{22,26},... | collective-permute-start | bytes 122888 | tf_op jit(solution)/shard_map/ppermute | solution.py:38
  18.5 5.9 %collective-permute-start.3 = (bf16[16,1280]{1,0:T(8,128)(2,1)S(1)}, bf16[16,1280]{1,0:T(8,128)(2,1)S(1)}, u32[]{:S(2)}, u32[]{:S(2)}) collective-permute-start(bf16[16,1280]{1,0:T(8,128)(2,1)S(1)} %copy-done.22), channel_id=1, source_target_pairs={{2,4},{3,5},{6,8},{7,9},{10,12},{11,13},{18,20},{19,21},{22,24},{2... | collective-permute-start | bytes 122888 | tf_op jit(solution)/shard_map/ppermute | solution.py:38
  19.2 8.4 %collective-permute-start.4 = (bf16[16,1280]{1,0:T(8,128)(2,1)S(1)}, bf16[16,1280]{1,0:T(8,128)(2,1)S(1)}, u32[]{:S(2)}, u32[]{:S(2)}) collective-permute-start(bf16[16,1280]{1,0:T(8,128)(2,1)S(1)} %copy-done.21), channel_id=1, source_target_pairs={{2,22},{3,23},{6,26},{7,27},{10,30},{11,31},{18,6},{19,7},{22,10},... | collective-permute-start | bytes 122888 | tf_op jit(solution)/shard_map/ppermute | solution.py:38
  20.5 7.1 %collective-permute-start.5 = (bf16[16,1280]{1,0:T(8,128)(2,1)S(1)}, bf16[16,1280]{1,0:T(8,128)(2,1)S(1)}, u32[]{:S(2)}, u32[]{:S(2)}) collective-permute-start(bf16[16,1280]{1,0:T(8,128)(2,1)S(1)} %copy-done.20), channel_id=1, source_target_pairs={{2,20},{3,21},{6,24},{7,25},{10,28},{11,29},{18,4},{19,5},{22,8},{... | collective-permute-start | bytes 122888 | tf_op jit(solution)/shard_map/ppermute | solution.py:38
  24.4 15.2 %copy-start.25 = (f32[16,256]{1,0:T(8,128)S(1)}, f32[16,256]{1,0:T(8,128)}, u32[]{:S(2)}) copy-start(f32[16,256]{1,0:T(8,128)} %get-tuple-element.120) | copy-start | bytes 49156
  24.4 25.0 %copy-start.24 = (f32[16,256]{1,0:T(8,128)S(1)}, f32[16,256]{1,0:T(8,128)}, u32[]{:S(2)}) copy-start(f32[16,256]{1,0:T(8,128)} %get-tuple-element.118) | copy-start | bytes 49156
  32.3 53.6 %copy-start.16 = (f32[64]{0:T(128)S(1)}, f32[64]{0:T(128)}, u32[]{:S(2)}) copy-start(f32[64]{0:T(128)} %param.20) | copy-start | bytes 772
  32.3 17.1 %collective-permute-start.6 = (bf16[256,1280]{1,0:T(8,128)(2,1)}, bf16[256,1280]{1,0:T(8,128)(2,1)S(1)}, u32[]{:S(2)}, u32[]{:S(2)}) collective-permute-start(bf16[256,1280]{1,0:T(8,128)(2,1)} %get-tuple-element.114), channel_id=1, source_target_pairs={{0,2},{1,3},{2,0},{3,1},{4,6},{5,7},{6,4},{7,5},{8,10},{9,11},{10,... | collective-permute-start | bytes 1966088 | tf_op jit(solution)/shard_map/ppermute | solution.py:38
  36.6 17.6 %collective-permute-start.7 = (bf16[256,1280]{1,0:T(8,128)(2,1)S(1)}, bf16[256,1280]{1,0:T(8,128)(2,1)S(1)}, u32[]{:S(2)}, u32[]{:S(2)}) collective-permute-start(bf16[256,1280]{1,0:T(8,128)(2,1)S(1)} %copy-done.19), channel_id=1, source_target_pairs={{0,16},{1,17},{2,18},{3,19},{4,20},{5,21},{6,22},{7,23},{8,24},{9,... | collective-permute-start | bytes 1966088 | tf_op jit(solution)/shard_map/ppermute | solution.py:38
  38.1 28.6 %collective-permute-start.8 = (bf16[256,1280]{1,0:T(8,128)(2,1)S(1)}, bf16[256,1280]{1,0:T(8,128)(2,1)S(1)}, u32[]{:S(2)}, u32[]{:S(2)}) collective-permute-start(bf16[256,1280]{1,0:T(8,128)(2,1)S(1)} %copy-done.18), channel_id=1, source_target_pairs={{0,18},{1,19},{2,16},{3,17},{4,22},{5,23},{6,20},{7,21},{8,26},{9,... | collective-permute-start | bytes 1966088 | tf_op jit(solution)/shard_map/ppermute | solution.py:38
  38.1 29.1 %collective-permute-start.10 = (f32[16,256]{1,0:T(8,128)S(1)}, f32[16,256]{1,0:T(8,128)S(1)}, u32[]{:S(2)}, u32[]{:S(2)}) collective-permute-start(f32[16,256]{1,0:T(8,128)S(1)} %copy-done.26), channel_id=1, source_target_pairs={{0,16},{1,17},{2,18},{3,19},{4,20},{5,21},{6,22},{7,23},{8,24},{9,... | collective-permute-start | bytes 49160 | tf_op jit(solution)/shard_map/ppermute | solution.py:38
  39.6 27.6 %collective-permute-start.11 = (f32[16,256]{1,0:T(8,128)S(1)}, f32[16,256]{1,0:T(8,128)S(1)}, u32[]{:S(2)}, u32[]{:S(2)}) collective-permute-start(f32[16,256]{1,0:T(8,128)S(1)} %copy-done.25), channel_id=1, source_target_pairs={{0,18},{1,19},{2,16},{3,17},{4,22},{5,23},{6,20},{7,21},{8,26},{9,... | collective-permute-start | bytes 49160 | tf_op jit(solution)/shard_map/ppermute | solution.py:38
  49.4 17.8 %copy-start.3 = (bf16[256,1280]{1,0:T(8,128)(2,1)}, bf16[256,1280]{1,0:T(8,128)(2,1)S(1)}, u32[]{:S(2)}) copy-start(bf16[256,1280]{1,0:T(8,128)(2,1)S(1)} %collective-permute-done.6.p1) | copy-start | bytes 1966084
  49.4 17.8 %collective-permute-start.9 = (f32[16,256]{1,0:T(8,128)S(1)}, f32[16,256]{1,0:T(8,128)S(1)}, u32[]{:S(2)}, u32[]{:S(2)}) collective-permute-start(f32[16,256]{1,0:T(8,128)S(1)} %copy-done.24), channel_id=1, source_target_pairs={{0,2},{1,3},{2,0},{3,1},{4,6},{5,7},{6,4},{7,5},{8,10},{9,11},{10,... | collective-permute-start | bytes 49160 | tf_op jit(solution)/shard_map/ppermute | solution.py:38
  81.0 41.9 %collective-permute-start.12 = (bf16[2,144,1024]{2,1,0:T(8,128)(2,1)}, bf16[2,144,1024]{2,1,0:T(8,128)(2,1)S(1)}, u32[]{:S(2)}, u32[]{:S(2)}) collective-permute-start(bf16[2,144,1024]{2,1,0:T(8,128)(2,1)} %get-tuple-element.149.late), channel_id=1, source_target_pairs={{0,4},{1,5},{2,6},{3,7},{4,8},{5,9},{6,10},{7,11},{8,12},{9,13},{1... | collective-permute-start | bytes 1769480 | tf_op jit(solution)/shard_map/ppermute | solution.py:38
  82.3 14.2 %collective-permute-start.13 = (bf16[256,1024]{1,0:T(8,128)(2,1)}, bf16[256,1024]{1,0:T(8,128)(2,1)S(1)}, u32[]{:S(2)}, u32[]{:S(2)}) collective-permute-start(bf16[256,1024]{1,0:T(8,128)(2,1)} %get-tuple-element.154), channel_id=1, source_target_pairs={{0,2},{1,3},{2,0},{3,1},{4,6},{5,7},{6,4},{7,5},{8,10},{9,11},{10,... | collective-permute-start | bytes 1572872 | tf_op jit(solution)/shard_map/ppermute | solution.py:38
  84.0 15.0 %collective-permute-start.14 = (bf16[256,1024]{1,0:T(8,128)(2,1)}, bf16[256,1024]{1,0:T(8,128)(2,1)S(1)}, u32[]{:S(2)}, u32[]{:S(2)}) collective-permute-start(bf16[256,1024]{1,0:T(8,128)(2,1)} %get-tuple-element.155), channel_id=1, source_target_pairs={{0,16},{1,17},{2,18},{3,19},{4,20},{5,21},{6,22},{7,23},{8,24},{9,... | collective-permute-start | bytes 1572872 | tf_op jit(solution)/shard_map/ppermute | solution.py:38
  85.5 22.2 %collective-permute-start.15 = (bf16[256,1024]{1,0:T(8,128)(2,1)}, bf16[256,1024]{1,0:T(8,128)(2,1)S(1)}, u32[]{:S(2)}, u32[]{:S(2)}) collective-permute-start(bf16[256,1024]{1,0:T(8,128)(2,1)} %get-tuple-element.156), channel_id=1, source_target_pairs={{0,18},{1,19},{2,16},{3,17},{4,22},{5,23},{6,20},{7,21},{8,26},{9,... | collective-permute-start | bytes 1572872 | tf_op jit(solution)/shard_map/ppermute | solution.py:38
  96.5 59.2 %copy-start.7 = (bf16[256,1024]{1,0:T(8,128)(2,1)}, bf16[256,1024]{1,0:T(8,128)(2,1)S(1)}, u32[]{:S(2)}) copy-start(bf16[256,1024]{1,0:T(8,128)(2,1)S(1)} %collective-permute-done.13.z1) | copy-start | bytes 1572868
  99.0 56.7 %copy-start.8 = (bf16[256,1024]{1,0:T(8,128)(2,1)}, bf16[256,1024]{1,0:T(8,128)(2,1)S(1)}, u32[]{:S(2)}) copy-start(bf16[256,1024]{1,0:T(8,128)(2,1)S(1)} %collective-permute-done.14.z2) | copy-start | bytes 1572868
  107.7 48.0 %copy-start.9 = (bf16[256,1024]{1,0:T(8,128)(2,1)}, bf16[256,1024]{1,0:T(8,128)(2,1)S(1)}, u32[]{:S(2)}) copy-start(bf16[256,1024]{1,0:T(8,128)(2,1)S(1)} %collective-permute-done.15.z3) | copy-start | bytes 1572868
  126.0 29.7 %collective-permute-start.16 = (bf16[2,144,1024]{2,1,0:T(8,128)(2,1)}, bf16[2,144,1024]{2,1,0:T(8,128)(2,1)S(1)}, u32[]{:S(2)}, u32[]{:S(2)}) collective-permute-start(bf16[2,144,1024]{2,1,0:T(8,128)(2,1)} %join.1), channel_id=1, source_target_pairs={{0,8},{1,9},{2,10},{3,11},{4,12},{5,13},{6,14},{7,15},{16,24},{17,... | collective-permute-start | bytes 1769480 | tf_op jit(solution)/shard_map/ppermute | solution.py:38
  167.4 5.1 %collective-permute-start.18 = (bf16[256,1024]{1,0:T(8,128)(2,1)S(1)}, bf16[256,1024]{1,0:T(8,128)(2,1)S(1)}, u32[]{:S(2)}, u32[]{:S(2)}) collective-permute-start(bf16[256,1024]{1,0:T(8,128)(2,1)S(1)} %fusion.23), channel_id=1, source_target_pairs={{0,1},{1,0},{2,3},{3,2},{4,5},{5,4},{6,7},{7,6},{8,9},{9,8},{10,11... | collective-permute-start | bytes 1572872 | tf_op jit(solution)/shard_map/ppermute | solution.py:38
  169.8 4.9 %collective-permute-start.20 = (bf16[256,1024]{1,0:T(8,128)(2,1)S(1)}, bf16[256,1024]{1,0:T(8,128)(2,1)S(1)}, u32[]{:S(2)}, u32[]{:S(2)}) collective-permute-start(bf16[256,1024]{1,0:T(8,128)(2,1)S(1)} %fusion.26), channel_id=1, source_target_pairs={{0,1},{1,0},{2,3},{3,2},{4,5},{5,4},{6,7},{7,6},{8,9},{9,8},{10,11... | collective-permute-start | bytes 1572872 | tf_op jit(solution)/shard_map/ppermute | solution.py:38
  171.1 7.3 %collective-permute-start.17 = (bf16[256,1024]{1,0:T(8,128)(2,1)S(1)}, bf16[256,1024]{1,0:T(8,128)(2,1)S(1)}, u32[]{:S(2)}, u32[]{:S(2)}) collective-permute-start(bf16[256,1024]{1,0:T(8,128)(2,1)S(1)} %fusion.20), channel_id=1, source_target_pairs={{0,1},{1,0},{2,3},{3,2},{4,5},{5,4},{6,7},{7,6},{8,9},{9,8},{10,11... | collective-permute-start | bytes 1572872 | tf_op jit(solution)/shard_map/ppermute | solution.py:38
  172.0 4.8 %collective-permute-start.22 = (bf16[256,1024]{1,0:T(8,128)(2,1)S(1)}, bf16[256,1024]{1,0:T(8,128)(2,1)S(1)}, u32[]{:S(2)}, u32[]{:S(2)}) collective-permute-start(bf16[256,1024]{1,0:T(8,128)(2,1)S(1)} %fusion.29), channel_id=1, source_target_pairs={{0,1},{1,0},{2,3},{3,2},{4,5},{5,4},{6,7},{7,6},{8,9},{9,8},{10,11... | collective-permute-start | bytes 1572872 | tf_op jit(solution)/shard_map/ppermute | solution.py:38
  173.3 13.9 %collective-permute-start.19 = (bf16[256,1024]{1,0:T(8,128)(2,1)S(1)}, bf16[256,1024]{1,0:T(8,128)(2,1)S(1)}, u32[]{:S(2)}, u32[]{:S(2)}) collective-permute-start(bf16[256,1024]{1,0:T(8,128)(2,1)S(1)} %fusion.32), channel_id=1, source_target_pairs={{0,2},{1,3},{2,0},{3,1},{4,6},{5,7},{6,4},{7,5},{8,10},{9,11},{10,... | collective-permute-start | bytes 1572872 | tf_op jit(solution)/shard_map/ppermute | solution.py:38
  175.5 14.9 %collective-permute-start.21 = (bf16[256,1024]{1,0:T(8,128)(2,1)S(1)}, bf16[256,1024]{1,0:T(8,128)(2,1)S(1)}, u32[]{:S(2)}, u32[]{:S(2)}) collective-permute-start(bf16[256,1024]{1,0:T(8,128)(2,1)S(1)} %fusion.35), channel_id=1, source_target_pairs={{0,16},{1,17},{2,18},{3,19},{4,20},{5,21},{6,22},{7,23},{8,24},{9,... | collective-permute-start | bytes 1572872 | tf_op jit(solution)/shard_map/ppermute | solution.py:38
  177.5 22.9 %collective-permute-start.23 = (bf16[256,1024]{1,0:T(8,128)(2,1)S(1)}, bf16[256,1024]{1,0:T(8,128)(2,1)S(1)}, u32[]{:S(2)}, u32[]{:S(2)}) collective-permute-start(bf16[256,1024]{1,0:T(8,128)(2,1)S(1)} %fusion.38), channel_id=1, source_target_pairs={{0,18},{1,19},{2,16},{3,17},{4,22},{5,23},{6,20},{7,21},{8,26},{9,... | collective-permute-start | bytes 1572872 | tf_op jit(solution)/shard_map/ppermute | solution.py:38
  (20 other events, 105.6 us)
Sparse Core Ops, SparseCore 0:
  32.4 92.3 all-gather.1

commit v6 on v5

--- a/solution.py
+++ b/solution.py
@@ -1,3 +1,4 @@
+import functools
 import math
 
 import jax
@@ -376,38 +377,30 @@
     )(place, xc, bc, low, cum, skip)
 
 
-def gate_kernel(
-    place, y, bc, kept, near, far, first, fade, z0, z1, z2, z3, gain, bits, out, gate
-):
-    k = pl.program_id(0)
-    for index, z in enumerate((z0, z1, z2, z3)):
-
-        @pl.when(k == index)
-        def _(z=z):
-            gate[...] = silu(z[...].astype(F32))
-
+def gate_kernel(k, place, y, bc, kept, near, far, first, fade, z, gain, bits, out):
     opening = place[1] == (k % 2)
     incoming = near[0, :STATE, :].astype(F32) + joined(near[0, STATE:, :]) * far[
         0, :STATE, :
     ].astype(F32)
     incoming = jnp.where(opening, incoming, fade[0, 7:8] * incoming + first[0])
     carried = jnp.dot(bc[0, :, STATE:], incoming.astype(BF16), preferred_element_type=F32)
-    gated = (y[0] + widen(kept[0], expander()) * carried) * gate[...]
+    gated = (y[0] + widen(kept[0], expander()) * carried) * silu(z[...].astype(F32))
     scale = lax.rsqrt(jnp.mean(gated * gated, axis=1, keepdims=True) + 1e-05)
     signed = gain[...] * (1 - 2 * bits[...]).astype(F32)
-    out[0] = (gated * scale * signed).astype(BF16)
-
-
-def gate_norm(place, y, bc, kept, near, far, first, fade, z_in, zs, gain, bits):
+    out[...] = (gated * scale * signed).astype(BF16)
+
+
+def gate_norm(k, place, y, bc, kept, near, far, first, fade, z, gain, bits):
     rows = y.shape[1]
-    block = lambda *shape: pl.BlockSpec((1,) + shape, lambda k, place: (k, 0, 0))
-    part = lambda *shape: pl.BlockSpec((1,) + shape, lambda k, place: (k // 2, 0, 0))
-    mine = lambda rows: pl.BlockSpec((rows, GROUP), lambda k, place: (0, place[0]))
-    return pl.pallas_call(
-        gate_kernel,
+    block = lambda *shape: pl.BlockSpec((1,) + shape, lambda i, place: (k, 0, 0))
+    part = lambda *shape: pl.BlockSpec((1,) + shape, lambda i, place: (k // 2, 0, 0))
+    mine = lambda rows: pl.BlockSpec((rows, GROUP), lambda i, place: (0, place[0]))
+    whole = pl.BlockSpec((rows, GROUP), lambda i, place: (0, 0))
+    return pl.pallas_call(
+        functools.partial(gate_kernel, k),
         grid_spec=pltpu.PrefetchScalarGridSpec(
             num_scalar_prefetch=1,
-            grid=(4,),
+            grid=(1,),
             in_specs=[
                 block(rows, GROUP),
                 block(rows, 2 * STATE),
@@ -416,16 +409,15 @@
                 part(STATE + 16, GROUP),
                 part(STATE, GROUP),
                 part(8, GROUP),
-                mine(rows),
-            ]
-            + [pl.BlockSpec((rows, GROUP), lambda k, place: (0, 0))] * 3
-            + [mine(1), mine(1)],
-            out_specs=block(rows, GROUP),
-            scratch_shapes=[pltpu.VMEM((rows, GROUP), F32)],
+                whole if k else mine(rows),
+                mine(1),
+                mine(1),
+            ],
+            out_specs=whole,
         ),
-        out_shape=jax.ShapeDtypeStruct((4, rows, GROUP), BF16),
+        out_shape=jax.ShapeDtypeStruct((rows, GROUP), BF16),
         name="gate_norm",
-    )(place, y, bc, kept, near, far, first, fade, z_in, *zs, gain, bits)
+    )(place, y, bc, kept, near, far, first, fade, z, gain, bits)
 
 
 def per_device(
@@ -486,18 +478,20 @@
         near, span = join(near, far), join(span, far)
         distance *= 2
         far = onward(span, distance)
-    act = gate_norm(
-        place, y, bc, kept, near, far, first, fade, z_in, zs, gain[None], sign_bits[None]
-    )
+    gates = [z_in] + zs
 
     half = weight.shape[1] // 2
     theirs = lax.dynamic_slice_in_dim(weight, (1 - t_here) * half, half, 1)
     ours = lax.dynamic_slice_in_dim(weight, t_here * half, half, 1)
     parts = []
     for k in (3, 2, 1, 0):
-        away = jnp.dot(act[k], theirs, preferred_element_type=F32).astype(BF16)
+        act = gate_norm(
+            k, place, y, bc, kept, near, far, first, fade, gates[k], gain[None], sign_bits[None]
+        )
+        away = jnp.dot(act, theirs, preferred_element_type=F32).astype(BF16)
         back = send(away, lambda x, z, y, t: (x, z, y, 1 - t))
-        stay = jnp.dot(act[k], ours, preferred_element_type=F32) + back.astype(F32)
+        stay = jnp.dot(act, ours, preferred_element_type=F32) + back.astype(F32)
+        far, stay = after(far, stay)
         parts.append(swap(stay.astype(BF16), k).astype(F32) if k else stay)
     total = parts[3] + parts[2] + parts[1] + parts[0]
     return total.astype(BF16)

time: 211 us -> 231 us (1.095)
  matrix products: 10.3 us -> 19.3 us
  Pallas kernels: 42 us -> 49.6 us
    dot_general x8, matrix products: 10.3 us -> 19.3 us  [the longest x4 10.1 us: per_device(): away = jnp.dot(act, theirs, preferred_element_type=F32).astype(BF16)]
    pallas_call x1 -> x4, Pallas kernels: 8.25 us -> 15.9 us  [gate_norm(): pl.pallas_call(functools.partial(gate_kernel, k), grid_spec=pltpu.Prefetc...]
    ppermute x24, waiting for transfers between devices: 109 us -> 111 us  [send(): return lax.ppermute(array, AXES, pairs)]
  transfers between devices with their start and end apart: 25 -> 25, of which waited for: 14 -> 16; matrix products, arithmetic and copies ran while one was open for 5% -> 3% of each run, Pallas kernels for 18% -> 15%
where the time goes in v6:
time: 231 us; the launch traced here: 230 us
  waiting for transfers between devices  111 us (48%)
  Pallas kernels  49.6 us (21%)
  starting transfers between devices  24.9 us (11%)
  matrix products  19.3 us (8%)
  between operations  13.7 us (6%)
  local copies, waits for them, and re-layouts  5.85 us (3%)
  other arithmetic  4.62 us (2%)
    ppermute x24, waiting for transfers between devices, send(): return lax.ppermute(array, AXES, pairs)  111 us
    ppermute x24, starting transfers between devices, send(): return lax.ppermute(array, AXES, pairs)  24.9 us
    pallas_call x4, Pallas kernels, gate_norm(): pl.pallas_call(functools.partial(gate_kernel, k), grid_spec=pltpu.Prefetc...  15.9 us
    pallas_call x1, Pallas kernels, conv_states(): pl.pallas_call(conv_kernel, grid_spec=pltpu.PrefetchScalarGridSpec(num_sc...  12.7 us
    dot_general x4, matrix products, per_device(): away = jnp.dot(act, theirs, preferred_element_type=F32).astype(BF16)  10.1 us
    dot_general x4, matrix products, per_device(): stay = jnp.dot(act, ours, preferred_element_type=F32) + back.astype(F32)  9.29 us
    pallas_call x1, Pallas kernels, within(): pl.pallas_call(within_kernel, grid_spec=pltpu.PrefetchScalarGridSpec(num_...  7.41 us
  transfers between devices with their start and end apart: 25, of which 16 were waited for; matrix products, arithmetic and copies ran while one was open for 3% of the time, Pallas kernels for 15%

profile of v6, /device:TPU:28, one launch (start us, length us, event | category | flops | bytes accessed | tf_op | source)
XLA Modules:
  0.0 229.5 jit_solution(8623454089296106762)
XLA Ops:
  6.5 4.0 %turn.1 = bf16[8,256,256]{2,1,0:T(8,128)(2,1)} custom-call(s32[1]{0:T(128)} %bitcast.5.sign, bf16[4096,256]{1,0:T(8,128)(2,1)} %w.1), custom_call_target="tpu_custom_call" | custom-call | tf_op jit(solution)/shard_map/turn/pallas_call | solution.py:179
  12.0 4.2 %pack.1 = (bf16[256,1280]{1,0:T(8,128)(2,1)}, bf16[256,1280]{1,0:T(8,128)(2,1)}, bf16[256,1280]{1,0:T(8,128)(2,1)}, bf16[256,1280]{1,0:T(8,128)(2,1)}, f32[16,25...) custom-call(s32[4]{0:T(128)} %pad_add_fusion.1.order, ...), custom_call_target="tpu_custom_call" | custom-call | tf_op jit(solution)/shard_map/pack/pallas_call | solution.py:95
  21.2 3.2 %cut.1 = (bf16[256,1024]{1,0:T(8,128)(2,1)}, bf16[256,1024]{1,0:T(8,128)(2,1)}, bf16[256,1024]{1,0:T(8,128)(2,1)}) custom-call(s32[4]{0:T(128)} %pad_add_fusion.1.order, bf16[256,4096]{1,0:T(8,128)(2,1)} %z, bf16[256,4096]{1,0:T(8,128)(2,1)} %z, bf16[256,4096]{1,0:T(8,128)(2,1)} %z), custom_call_target="tpu_custom_call" | custom-call | tf_op jit(solution)/shard_map/cut/pallas_call | solution.py:126
  24.5 3.2 %collective-permute-done.4 = bf16[16,1280]{1,0:T(8,128)(2,1)S(1)} collective-permute-done((bf16[16,1280]{1,0:T(8,128)(2,1)S(1)}, bf16[16,1280]{1,0:T(8,128)(2,1)S(1)}, u32[]{:S(2)}, u32[]{:S(2)}) %collective-permute-start.4) | collective-permute-done | bytes 40992 | tf_op jit(solution)/shard_map/ppermute | solution.py:39
  27.6 3.5 %collective-permute-done.1 = bf16[1024,256]{1,0:T(8,128)(2,1)S(1)} collective-permute-done((bf16[1024,256]{1,0:T(8,128)(2,1)S(1)}, bf16[1024,256]{1,0:T(8,128)(2,1)S(1)}, u32[]{:S(2)}, u32[]{:S(2)}) %collective-permute-start.1) | collective-permute-done | bytes 524320 | tf_op jit(solution)/shard_map/ppermute | solution.py:39
  32.3 2.3 %collective-permute-start.6 = (bf16[256,1280]{1,0:T(8,128)(2,1)}, bf16[256,1280]{1,0:T(8,128)(2,1)S(1)}, u32[]{:S(2)}, u32[]{:S(2)}) collective-permute-start(bf16[256,1280]{1,0:T(8,128)(2,1)} %get-tuple-element.121), channel_id=1, source_target_pairs={{0,2},{1,3},{2,0},{3,1},{4,6},{5,7},{6,4},{7,5},{8,10},{9,11},{10,... | collective-permute-start | bytes 1966088 | tf_op jit(solution)/shard_map/ppermute | solution.py:39
  41.6 7.9 %collective-permute-done.6.p1 = bf16[256,1280]{1,0:T(8,128)(2,1)S(1)} collective-permute-done((bf16[256,1280]{1,0:T(8,128)(2,1)}, bf16[256,1280]{1,0:T(8,128)(2,1)S(1)}, u32[]{:S(2)}, u32[]{:S(2)}) %collective-permute-start.6) | collective-permute-done | bytes 655392 | tf_op jit(solution)/shard_map/ppermute | solution.py:39
  49.6 2.7 %collective-permute-start.11 = (f32[16,256]{1,0:T(8,128)S(1)}, f32[16,256]{1,0:T(8,128)S(1)}, u32[]{:S(2)}, u32[]{:S(2)}) collective-permute-start(f32[16,256]{1,0:T(8,128)S(1)} %copy-done.24), channel_id=1, source_target_pairs={{0,18},{1,19},{2,16},{3,17},{4,22},{5,23},{6,20},{7,21},{8,26},{9,... | collective-permute-start | bytes 49160 | tf_op jit(solution)/shard_map/ppermute | solution.py:39
  54.2 12.5 %collective-permute-done.8.p3 = bf16[256,1280]{1,0:T(8,128)(2,1)S(1)} collective-permute-done((bf16[256,1280]{1,0:T(8,128)(2,1)S(1)}, bf16[256,1280]{1,0:T(8,128)(2,1)S(1)}, u32[]{:S(2)}, u32[]{:S(2)}) %collective-permute-start.8) | collective-permute-done | bytes 655392 | tf_op jit(solution)/shard_map/ppermute | solution.py:39
  68.4 12.7 %conv_states.1 = (bf16[4,256,1024]{2,1,0:T(8,128)(2,1)}, bf16[4,256,256]{2,1,0:T(8,128)(2,1)}, f32[4,16,256]{2,1,0:T(8,128)}, f32[4,256,16]{2,1,0:T(8,128)}, bf1...) custom-call(s32[2]{0:T(128)} %pad_add_fusion.place, ...), custom_call_target="tpu_custom_call" | custom-call | tf_op jit(solution)/shard_map/conv_states/pallas_call | solution.py:278
  86.7 7.4 %within.1.y = f32[4,256,1024]{2,1,0:T(8,128)} custom-call(s32[2]{0:T(128)} %pad_add_fusion.place, bf16[4,256,1024]{2,1,0:T(8,128)(2,1)} %get-tuple-element.157.xc, bf16[4,256,256]{2,1,0:T(8,128)(2,1)} %get-tuple-element.158.bc, f32[4,16,256]{2,1,0:T(8,128)} %get-tuple-element.159.low, f32[4,256,16]{2,1,0:T(8,128)} %get-tuple-element.160.cum, ...), custom_call_target="tpu_custom_call" | custom-call | tf_op jit(solution)/shard_map/within/pallas_call | solution.py:361
  94.1 2.4 %collective-permute-done.13.z = bf16[256,1024]{1,0:T(8,128)(2,1)S(1)} collective-permute-done((bf16[256,1024]{1,0:T(8,128)(2,1)}, bf16[256,1024]{1,0:T(8,128)(2,1)S(1)}, u32[]{:S(2)}, u32[]{:S(2)}) %collective-permute-start.13) | collective-permute-done | bytes 524320 | tf_op jit(solution)/shard_map/ppermute | solution.py:39
  96.6 2.5 %collective-permute-done.14.z = bf16[256,1024]{1,0:T(8,128)(2,1)S(1)} collective-permute-done((bf16[256,1024]{1,0:T(8,128)(2,1)}, bf16[256,1024]{1,0:T(8,128)(2,1)S(1)}, u32[]{:S(2)}, u32[]{:S(2)}) %collective-permute-start.14) | collective-permute-done | bytes 524320 | tf_op jit(solution)/shard_map/ppermute | solution.py:39
  99.0 8.4 %collective-permute-done.15.z = bf16[256,1024]{1,0:T(8,128)(2,1)S(1)} collective-permute-done((bf16[256,1024]{1,0:T(8,128)(2,1)}, bf16[256,1024]{1,0:T(8,128)(2,1)S(1)}, u32[]{:S(2)}, u32[]{:S(2)}) %collective-permute-start.15) | collective-permute-done | bytes 524320 | tf_op jit(solution)/shard_map/ppermute | solution.py:39
  107.4 15.5 %collective-permute-done.12.early.near = bf16[2,144,1024]{2,1,0:T(8,128)(2,1)S(1)} collective-permute-done((bf16[2,144,1024]{2,1,0:T(8,128)(2,1)}, bf16[2,144,1024]{2,1,0:T(8,128)(2,1)S(1)}, u32[]{:S(2)}, u32[]{:S(2)}) %collective-permute-start.12) | collective-permute-done | bytes 589856 | tf_op jit(solution)/shard_map/ppermute | solution.py:39
  123.7 2.3 join.1
  127.5 27.8 %collective-permute-done.16.far = bf16[2,144,1024]{2,1,0:T(8,128)(2,1)S(1)} collective-permute-done((bf16[2,144,1024]{2,1,0:T(8,128)(2,1)}, bf16[2,144,1024]{2,1,0:T(8,128)(2,1)S(1)}, u32[]{:S(2)}, u32[]{:S(2)}) %collective-permute-start.16) | collective-permute-done | bytes 589856 | tf_op jit(solution)/shard_map/ppermute | solution.py:39
  156.1 3.9 %gate_norm.4 = bf16[256,1024]{1,0:T(8,128)(2,1)} custom-call(s32[2]{0:T(128)} %pad_add_fusion.place, f32[4,256,1024]{2,1,0:T(8,128)} %within.1.y, bf16[4,256,256]{2,1,0:T(8,128)(2,1)} %get-tuple-element.158.bc, bf16[4,48,256]{2,1,0:T(8,128)(2,1)} %get-tuple-element.166.kept, bf16[2,144,1024]{2,1,0:T(8,128)(2,1)} %copy-done, bf16[2,144,1024]{2,1,0:T(8,128)(2,1)} %copy-done.1, ...), custom_call_target="tpu_custom_call" | custom-call | tf_op jit(solution)/shard_map/gate_norm/pallas_call | solution.py:399
  160.0 2.5 %fusion.14 = bf16[256,1024]{1,0:T(8,128)(2,1)S(1)} fusion(bf16[256,1024]{1,0:T(8,128)(2,1)} %gate_norm.4, bf16[1024,2048]{1,0:T(8,128)(2,1)} %all-gather.2.cloned.1.call-done, s32[]{:T(128)S(6)} %select_n.36), kind=kOutput, calls=%fused_computation.19 | convolution fusion | flops 537133056 | bytes 3145732 | tf_op jit(solution)/shard_map/dot_general | solution.py:491
  164.5 2.3 %convolution_add_fusion.3 = bf16[256,1024]{1,0:T(8,128)(2,1)S(1)} fusion(bf16[256,1024]{1,0:T(8,128)(2,1)S(1)} %copy-done.10, bf16[1024,2048]{1,0:T(8,128)(2,1)} %all-gather.2.cloned.1.call-done, s32[]{:T(128)S(6)} %select_n.35, bf16[256,1024]{1,0:T(8,128)(2,1)S(1)} %collective-permute-done.17), kind=kOutput, calls=%fused_computation.6 | convolution fusion | flops 537657344 | bytes 3670020 | tf_op jit(solution)/shard_map/dot_general | solution.py:493
  166.9 3.9 %gate_norm.5 = bf16[256,1024]{1,0:T(8,128)(2,1)} custom-call(s32[2]{0:T(128)} %pad_add_fusion.place, f32[4,256,1024]{2,1,0:T(8,128)} %within.1.y, bf16[4,256,256]{2,1,0:T(8,128)(2,1)} %get-tuple-element.158.bc, bf16[4,48,256]{2,1,0:T(8,128)(2,1)} %get-tuple-element.166.kept, bf16[2,144,1024]{2,1,0:T(8,128)(2,1)} %copy-done, bf16[2,144,1024]{2,1,0:T(8,128)(2,1)} %copy-done.1, ...), custom_call_target="tpu_custom_call" | custom-call | tf_op jit(solution)/shard_map/gate_norm/pallas_call | solution.py:399
  170.8 2.5 %fusion.17 = bf16[256,1024]{1,0:T(8,128)(2,1)S(1)} fusion(bf16[256,1024]{1,0:T(8,128)(2,1)} %gate_norm.5, bf16[1024,2048]{1,0:T(8,128)(2,1)} %all-gather.2.cloned.1.call-done, s32[]{:T(128)S(6)} %select_n.36), kind=kOutput, calls=%fused_computation.20 | convolution fusion | flops 537133056 | bytes 3145732 | tf_op jit(solution)/shard_map/dot_general | solution.py:491
  175.3 2.3 %convolution_add_fusion.2 = bf16[256,1024]{1,0:T(8,128)(2,1)S(1)} fusion(bf16[256,1024]{1,0:T(8,128)(2,1)S(1)} %copy-done.11, bf16[1024,2048]{1,0:T(8,128)(2,1)} %all-gather.2.cloned.1.call-done, s32[]{:T(128)S(6)} %select_n.35, bf16[256,1024]{1,0:T(8,128)(2,1)S(1)} %collective-permute-done.18), kind=kOutput, calls=%fused_computation.5 | convolution fusion | flops 537657344 | bytes 3670020 | tf_op jit(solution)/shard_map/dot_general | solution.py:493
  177.6 4.0 %gate_norm.6 = bf16[256,1024]{1,0:T(8,128)(2,1)} custom-call(s32[2]{0:T(128)} %pad_add_fusion.place, f32[4,256,1024]{2,1,0:T(8,128)} %within.1.y, bf16[4,256,256]{2,1,0:T(8,128)(2,1)} %get-tuple-element.158.bc, bf16[4,48,256]{2,1,0:T(8,128)(2,1)} %get-tuple-element.166.kept, bf16[2,144,1024]{2,1,0:T(8,128)(2,1)} %copy-done, bf16[2,144,1024]{2,1,0:T(8,128)(2,1)} %copy-done.1, ...), custom_call_target="tpu_custom_call" | custom-call | tf_op jit(solution)/shard_map/gate_norm/pallas_call | solution.py:399
  181.6 2.5 %fusion.20 = bf16[256,1024]{1,0:T(8,128)(2,1)S(1)} fusion(bf16[256,1024]{1,0:T(8,128)(2,1)} %gate_norm.6, bf16[1024,2048]{1,0:T(8,128)(2,1)} %all-gather.2.cloned.1.call-done, s32[]{:T(128)S(6)} %select_n.36), kind=kOutput, calls=%fused_computation.21 | convolution fusion | flops 537133056 | bytes 3145732 | tf_op jit(solution)/shard_map/dot_general | solution.py:491
  186.1 2.3 %convolution_add_fusion.1 = bf16[256,1024]{1,0:T(8,128)(2,1)S(1)} fusion(bf16[256,1024]{1,0:T(8,128)(2,1)S(1)} %copy-done.12, bf16[1024,2048]{1,0:T(8,128)(2,1)} %all-gather.2.cloned.1.call-done, s32[]{:T(128)S(6)} %select_n.35, bf16[256,1024]{1,0:T(8,128)(2,1)S(1)} %collective-permute-done.19), kind=kOutput, calls=%fused_computation.4 | convolution fusion | flops 537657344 | bytes 3670020 | tf_op jit(solution)/shard_map/dot_general | solution.py:493
  188.5 4.0 %gate_norm.7 = bf16[256,1024]{1,0:T(8,128)(2,1)} custom-call(s32[2]{0:T(128)} %pad_add_fusion.place, f32[4,256,1024]{2,1,0:T(8,128)} %within.1.y, bf16[4,256,256]{2,1,0:T(8,128)(2,1)} %get-tuple-element.158.bc, bf16[4,48,256]{2,1,0:T(8,128)(2,1)} %get-tuple-element.166.kept, bf16[2,144,1024]{2,1,0:T(8,128)(2,1)} %copy-done, bf16[2,144,1024]{2,1,0:T(8,128)(2,1)} %copy-done.1, ...), custom_call_target="tpu_custom_call" | custom-call | tf_op jit(solution)/shard_map/gate_norm/pallas_call | solution.py:399
  192.5 2.5 %fusion.23 = bf16[256,1024]{1,0:T(8,128)(2,1)S(1)} fusion(bf16[256,1024]{1,0:T(8,128)(2,1)} %gate_norm.7, bf16[1024,2048]{1,0:T(8,128)(2,1)} %all-gather.2.cloned.1.call-done, s32[]{:T(128)S(6)} %select_n.36), kind=kOutput, calls=%fused_computation.22 | convolution fusion | flops 537133056 | bytes 3145732 | tf_op jit(solution)/shard_map/dot_general | solution.py:491
  195.2 2.2 collective-permute-start.23
  198.7 2.3 %convolution_add_fusion = f32[256,1024]{1,0:T(8,128)S(1)} fusion(bf16[256,1024]{1,0:T(8,128)(2,1)S(1)} %copy-done.3, bf16[1024,2048]{1,0:T(8,128)(2,1)} %all-gather.2.cloned.1.call-done, s32[]{:T(128)S(6)} %select_n.35, bf16[256,1024]{1,0:T(8,128)(2,1)S(1)} %collective-permute-done.20), kind=kOutput, calls=%fused_computation.3 | convolution fusion | flops 537395200 | bytes 4194308 | tf_op jit(solution)/shard_map/dot_general | solution.py:493
  201.0 9.9 %collective-permute-done.23 = bf16[256,1024]{1,0:T(8,128)(2,1)S(1)} collective-permute-done((bf16[256,1024]{1,0:T(8,128)(2,1)S(1)}, bf16[256,1024]{1,0:T(8,128)(2,1)S(1)}, u32[]{:S(2)}, u32[]{:S(2)}) %collective-permute-start.23) | collective-permute-done | bytes 524320 | tf_op jit(solution)/shard_map/ppermute | solution.py:39
  210.9 10.6 %collective-permute-done.22 = bf16[256,1024]{1,0:T(8,128)(2,1)S(1)} collective-permute-done((bf16[256,1024]{1,0:T(8,128)(2,1)S(1)}, bf16[256,1024]{1,0:T(8,128)(2,1)S(1)}, u32[]{:S(2)}, u32[]{:S(2)}) %collective-permute-start.22) | collective-permute-done | bytes 524320 | tf_op jit(solution)/shard_map/ppermute | solution.py:39
  (100 shorter events, 35.4 us)
Async XLA Ops:
  6.5 153.5 %all-gather.2.cloned.1.call-start = ((), (), s32[]{:S(2)}) async-start(), calls=%async_computation | async-start | bytes 5242880 | tf_op jit(solution)/shard_map/all_gather | solution.py:463
  10.6 5.6 %collective-permute-start = (bf16[2,1024,256]{2,1,0:T(8,128)(2,1)}, bf16[2,1024,256]{2,1,0:T(8,128)(2,1)S(1)}, u32[]{:S(2)}, u32[]{:S(2)}) collective-permute-start(bf16[2,1024,256]{2,1,0:T(8,128)(2,1)} %bitcast.27), channel_id=1, source_target_pairs={{0,1},{1,0},{2,3},{3,2},{4,5},{5,4},{6,7},{7,6},{8,9},{9,8},{10,11... | collective-permute-start | bytes 3145736 | tf_op jit(solution)/shard_map/ppermute | solution.py:39
  16.7 14.4 %collective-permute-start.1 = (bf16[1024,256]{1,0:T(8,128)(2,1)S(1)}, bf16[1024,256]{1,0:T(8,128)(2,1)S(1)}, u32[]{:S(2)}, u32[]{:S(2)}) collective-permute-start(bf16[1024,256]{1,0:T(8,128)(2,1)S(1)} %get-tuple-element.180), channel_id=1, source_target_pairs={{0,2},{1,3},{2,0},{3,1},{4,6},{5,7},{6,4},{7,5},{8,10},{9,11},{10,... | collective-permute-start | bytes 1572872 | tf_op jit(solution)/shard_map/ppermute | solution.py:39
  17.3 7.2 %collective-permute-start.2 = (bf16[16,1280]{1,0:T(8,128)(2,1)}, bf16[16,1280]{1,0:T(8,128)(2,1)S(1)}, u32[]{:S(2)}, u32[]{:S(2)}) collective-permute-start(bf16[16,1280]{1,0:T(8,128)(2,1)} %get-tuple-element.136), channel_id=1, source_target_pairs={{2,6},{3,7},{6,10},{7,11},{10,14},{11,15},{18,22},{19,23},{22,26},... | collective-permute-start | bytes 122888 | tf_op jit(solution)/shard_map/ppermute | solution.py:39
  18.5 5.9 %collective-permute-start.3 = (bf16[16,1280]{1,0:T(8,128)(2,1)}, bf16[16,1280]{1,0:T(8,128)(2,1)S(1)}, u32[]{:S(2)}, u32[]{:S(2)}) collective-permute-start(bf16[16,1280]{1,0:T(8,128)(2,1)} %get-tuple-element.137), channel_id=1, source_target_pairs={{2,4},{3,5},{6,8},{7,9},{10,12},{11,13},{18,20},{19,21},{22,24},{2... | collective-permute-start | bytes 122888 | tf_op jit(solution)/shard_map/ppermute | solution.py:39
  19.2 8.4 %collective-permute-start.4 = (bf16[16,1280]{1,0:T(8,128)(2,1)S(1)}, bf16[16,1280]{1,0:T(8,128)(2,1)S(1)}, u32[]{:S(2)}, u32[]{:S(2)}) collective-permute-start(bf16[16,1280]{1,0:T(8,128)(2,1)S(1)} %copy-done.23), channel_id=1, source_target_pairs={{2,22},{3,23},{6,26},{7,27},{10,30},{11,31},{18,6},{19,7},{22,10},... | collective-permute-start | bytes 122888 | tf_op jit(solution)/shard_map/ppermute | solution.py:39
  20.5 7.1 %collective-permute-start.5 = (bf16[16,1280]{1,0:T(8,128)(2,1)S(1)}, bf16[16,1280]{1,0:T(8,128)(2,1)S(1)}, u32[]{:S(2)}, u32[]{:S(2)}) collective-permute-start(bf16[16,1280]{1,0:T(8,128)(2,1)S(1)} %copy-done.22), channel_id=1, source_target_pairs={{2,20},{3,21},{6,24},{7,25},{10,28},{11,29},{18,4},{19,5},{22,8},{... | collective-permute-start | bytes 122888 | tf_op jit(solution)/shard_map/ppermute | solution.py:39
  24.4 13.7 %copy-start.20 = (bf16[256,1280]{1,0:T(8,128)(2,1)S(1)}, bf16[256,1280]{1,0:T(8,128)(2,1)}, u32[]{:S(2)}) copy-start(bf16[256,1280]{1,0:T(8,128)(2,1)} %get-tuple-element.123) | copy-start | bytes 1966084
  24.4 25.2 %copy-start.24 = (f32[16,256]{1,0:T(8,128)S(1)}, f32[16,256]{1,0:T(8,128)}, u32[]{:S(2)}) copy-start(f32[16,256]{1,0:T(8,128)} %get-tuple-element.127) | copy-start | bytes 49156
  32.3 53.6 %copy-start.19 = (f32[64]{0:T(128)S(1)}, f32[64]{0:T(128)}, u32[]{:S(2)}) copy-start(f32[64]{0:T(128)} %param.20) | copy-start | bytes 772
  32.3 17.3 %collective-permute-start.6 = (bf16[256,1280]{1,0:T(8,128)(2,1)}, bf16[256,1280]{1,0:T(8,128)(2,1)S(1)}, u32[]{:S(2)}, u32[]{:S(2)}) collective-permute-start(bf16[256,1280]{1,0:T(8,128)(2,1)} %get-tuple-element.121), channel_id=1, source_target_pairs={{0,2},{1,3},{2,0},{3,1},{4,6},{5,7},{6,4},{7,5},{8,10},{9,11},{10,... | collective-permute-start | bytes 1966088 | tf_op jit(solution)/shard_map/ppermute | solution.py:39
  36.6 17.6 %collective-permute-start.7 = (bf16[256,1280]{1,0:T(8,128)(2,1)S(1)}, bf16[256,1280]{1,0:T(8,128)(2,1)S(1)}, u32[]{:S(2)}, u32[]{:S(2)}) collective-permute-start(bf16[256,1280]{1,0:T(8,128)(2,1)S(1)} %copy-done.21), channel_id=1, source_target_pairs={{0,16},{1,17},{2,18},{3,19},{4,20},{5,21},{6,22},{7,23},{8,24},{9,... | collective-permute-start | bytes 1966088 | tf_op jit(solution)/shard_map/ppermute | solution.py:39
  38.1 28.6 %collective-permute-start.8 = (bf16[256,1280]{1,0:T(8,128)(2,1)S(1)}, bf16[256,1280]{1,0:T(8,128)(2,1)S(1)}, u32[]{:S(2)}, u32[]{:S(2)}) collective-permute-start(bf16[256,1280]{1,0:T(8,128)(2,1)S(1)} %copy-done.20), channel_id=1, source_target_pairs={{0,18},{1,19},{2,16},{3,17},{4,22},{5,23},{6,20},{7,21},{8,26},{9,... | collective-permute-start | bytes 1966088 | tf_op jit(solution)/shard_map/ppermute | solution.py:39
  38.1 28.6 %collective-permute-start.9 = (f32[16,256]{1,0:T(8,128)}, f32[16,256]{1,0:T(8,128)S(1)}, u32[]{:S(2)}, u32[]{:S(2)}) collective-permute-start(f32[16,256]{1,0:T(8,128)} %get-tuple-element.125), channel_id=1, source_target_pairs={{0,2},{1,3},{2,0},{3,1},{4,6},{5,7},{6,4},{7,5},{8,10},{9,11},{10,... | collective-permute-start | bytes 49160 | tf_op jit(solution)/shard_map/ppermute | solution.py:39
  40.1 27.1 %collective-permute-start.10 = (f32[16,256]{1,0:T(8,128)}, f32[16,256]{1,0:T(8,128)S(1)}, u32[]{:S(2)}, u32[]{:S(2)}) collective-permute-start(f32[16,256]{1,0:T(8,128)} %get-tuple-element.126), channel_id=1, source_target_pairs={{0,16},{1,17},{2,18},{3,19},{4,20},{5,21},{6,22},{7,23},{8,24},{9,... | collective-permute-start | bytes 49160 | tf_op jit(solution)/shard_map/ppermute | solution.py:39
  49.6 17.6 %copy-start.4 = (bf16[256,1280]{1,0:T(8,128)(2,1)}, bf16[256,1280]{1,0:T(8,128)(2,1)S(1)}, u32[]{:S(2)}) copy-start(bf16[256,1280]{1,0:T(8,128)(2,1)S(1)} %collective-permute-done.6.p1) | copy-start | bytes 1966084
  49.6 17.6 %collective-permute-start.11 = (f32[16,256]{1,0:T(8,128)S(1)}, f32[16,256]{1,0:T(8,128)S(1)}, u32[]{:S(2)}, u32[]{:S(2)}) collective-permute-start(f32[16,256]{1,0:T(8,128)S(1)} %copy-done.24), channel_id=1, source_target_pairs={{0,18},{1,19},{2,16},{3,17},{4,22},{5,23},{6,20},{7,21},{8,26},{9,... | collective-permute-start | bytes 49160 | tf_op jit(solution)/shard_map/ppermute | solution.py:39
  81.1 41.8 %collective-permute-start.12 = (bf16[2,144,1024]{2,1,0:T(8,128)(2,1)}, bf16[2,144,1024]{2,1,0:T(8,128)(2,1)S(1)}, u32[]{:S(2)}, u32[]{:S(2)}) collective-permute-start(bf16[2,144,1024]{2,1,0:T(8,128)(2,1)} %get-tuple-element.156.late), channel_id=1, source_target_pairs={{0,4},{1,5},{2,6},{3,7},{4,8},{5,9},{6,10},{7,11},{8,12},{9,13},{1... | collective-permute-start | bytes 1769480 | tf_op jit(solution)/shard_map/ppermute | solution.py:39
  82.4 14.2 %collective-permute-start.13 = (bf16[256,1024]{1,0:T(8,128)(2,1)}, bf16[256,1024]{1,0:T(8,128)(2,1)S(1)}, u32[]{:S(2)}, u32[]{:S(2)}) collective-permute-start(bf16[256,1024]{1,0:T(8,128)(2,1)} %get-tuple-element.161), channel_id=1, source_target_pairs={{0,2},{1,3},{2,0},{3,1},{4,6},{5,7},{6,4},{7,5},{8,10},{9,11},{10,... | collective-permute-start | bytes 1572872 | tf_op jit(solution)/shard_map/ppermute | solution.py:39
  84.0 15.0 %collective-permute-start.14 = (bf16[256,1024]{1,0:T(8,128)(2,1)}, bf16[256,1024]{1,0:T(8,128)(2,1)S(1)}, u32[]{:S(2)}, u32[]{:S(2)}) collective-permute-start(bf16[256,1024]{1,0:T(8,128)(2,1)} %get-tuple-element.162), channel_id=1, source_target_pairs={{0,16},{1,17},{2,18},{3,19},{4,20},{5,21},{6,22},{7,23},{8,24},{9,... | collective-permute-start | bytes 1572872 | tf_op jit(solution)/shard_map/ppermute | solution.py:39
  85.5 21.9 %collective-permute-start.15 = (bf16[256,1024]{1,0:T(8,128)(2,1)}, bf16[256,1024]{1,0:T(8,128)(2,1)S(1)}, u32[]{:S(2)}, u32[]{:S(2)}) collective-permute-start(bf16[256,1024]{1,0:T(8,128)(2,1)} %get-tuple-element.163), channel_id=1, source_target_pairs={{0,18},{1,19},{2,16},{3,17},{4,22},{5,23},{6,20},{7,21},{8,26},{9,... | collective-permute-start | bytes 1572872 | tf_op jit(solution)/shard_map/ppermute | solution.py:39
  96.5 66.0 %copy-start.7 = (bf16[256,1024]{1,0:T(8,128)(2,1)}, bf16[256,1024]{1,0:T(8,128)(2,1)S(1)}, u32[]{:S(2)}) copy-start(bf16[256,1024]{1,0:T(8,128)(2,1)S(1)} %collective-permute-done.13.z) | copy-start | bytes 1572868
  99.0 63.6 %copy-start.8 = (bf16[256,1024]{1,0:T(8,128)(2,1)}, bf16[256,1024]{1,0:T(8,128)(2,1)S(1)}, u32[]{:S(2)}) copy-start(bf16[256,1024]{1,0:T(8,128)(2,1)S(1)} %collective-permute-done.14.z) | copy-start | bytes 1572868
  107.4 47.9 %copy-start.9 = (bf16[256,1024]{1,0:T(8,128)(2,1)}, bf16[256,1024]{1,0:T(8,128)(2,1)S(1)}, u32[]{:S(2)}) copy-start(bf16[256,1024]{1,0:T(8,128)(2,1)S(1)} %collective-permute-done.15.z) | copy-start | bytes 1572868
  126.0 29.3 %collective-permute-start.16 = (bf16[2,144,1024]{2,1,0:T(8,128)(2,1)}, bf16[2,144,1024]{2,1,0:T(8,128)(2,1)S(1)}, u32[]{:S(2)}, u32[]{:S(2)}) collective-permute-start(bf16[2,144,1024]{2,1,0:T(8,128)(2,1)} %join.1), channel_id=1, source_target_pairs={{0,8},{1,9},{2,10},{3,11},{4,12},{5,13},{6,14},{7,15},{16,24},{17,... | collective-permute-start | bytes 1769480 | tf_op jit(solution)/shard_map/ppermute | solution.py:39
  162.6 2.0 collective-permute-start.17
  173.3 2.0 collective-permute-start.18
  184.1 2.0 collective-permute-start.19
  195.0 3.7 %collective-permute-start.20 = (bf16[256,1024]{1,0:T(8,128)(2,1)S(1)}, bf16[256,1024]{1,0:T(8,128)(2,1)S(1)}, u32[]{:S(2)}, u32[]{:S(2)}) collective-permute-start(bf16[256,1024]{1,0:T(8,128)(2,1)S(1)} %fusion.23), channel_id=1, source_target_pairs={{0,1},{1,0},{2,3},{3,2},{4,5},{5,4},{6,7},{7,6},{8,9},{9,8},{10,11... | collective-permute-start | bytes 1572872 | tf_op jit(solution)/shard_map/ppermute | solution.py:39
  195.2 15.7 %collective-permute-start.23 = (bf16[256,1024]{1,0:T(8,128)(2,1)S(1)}, bf16[256,1024]{1,0:T(8,128)(2,1)S(1)}, u32[]{:S(2)}, u32[]{:S(2)}) collective-permute-start(bf16[256,1024]{1,0:T(8,128)(2,1)S(1)} %convolution_add_fusion.3), channel_id=1, source_target_pairs={{0,18},{1,19},{2,16},{3,17},{4,22},{5,23},{6,20},{7,21},{8,26},{9,... | collective-permute-start | bytes 1572872 | tf_op jit(solution)/shard_map/ppermute | solution.py:39
  197.4 24.1 %collective-permute-start.22 = (bf16[256,1024]{1,0:T(8,128)(2,1)S(1)}, bf16[256,1024]{1,0:T(8,128)(2,1)S(1)}, u32[]{:S(2)}, u32[]{:S(2)}) collective-permute-start(bf16[256,1024]{1,0:T(8,128)(2,1)S(1)} %convolution_add_fusion.2), channel_id=1, source_target_pairs={{0,16},{1,17},{2,18},{3,19},{4,20},{5,21},{6,22},{7,23},{8,24},{9,... | collective-permute-start | bytes 1572872 | tf_op jit(solution)/shard_map/ppermute | solution.py:39
  198.1 23.5 %collective-permute-start.21 = (bf16[256,1024]{1,0:T(8,128)(2,1)S(1)}, bf16[256,1024]{1,0:T(8,128)(2,1)S(1)}, u32[]{:S(2)}, u32[]{:S(2)}) collective-permute-start(bf16[256,1024]{1,0:T(8,128)(2,1)S(1)} %convolution_add_fusion.1), channel_id=1, source_target_pairs={{0,2},{1,3},{2,0},{3,1},{4,6},{5,7},{6,4},{7,5},{8,10},{9,11},{10,... | collective-permute-start | bytes 1572872 | tf_op jit(solution)/shard_map/ppermute | solution.py:39
  (18 other events, 86.2 us)
Sparse Core Ops, SparseCore 0:
  32.4 92.3 all-gather.1
